TPU v7x, 512 devices: a whole 4x8x8 slice. The times are simulated.
512 devices in a mesh: band: 8 (over x, z_lo), tm: 64 (over y, z_hi, core).
Axes of the slice: x: 4, y: 8, z: 8 (z_hi: 4, z_lo: 2; z = z_hi * 2 + z_lo), core: 2. Of those that a mesh axis runs over, the one named last changes fastest.
Arguments:
- driven_wave: bfloat16 [2048, 2048], P('tm', 'band'), may hold values from -6 to 6
- responses: bfloat16 [1024, 512, 2048], P('tm', None, 'band'), may hold values from -0.01171875 to 0.01171875
- tap_counts: int32 [2048], P('band'), may hold values from 256 to 1024
- panel_links: int32 [2048, 2], P('band'), may hold values 0 or 1
Outputs:
- far_end: bfloat16 [1024, 2048], P('tm', 'band')
All inputs are finite; a program needn't handle non-finite values. No bound on the sum of `panel_links` on one device may be relied on, other than what follows from the above.
Results may differ from a plain program's by a relative error of at most 0.00155.
Values may be sent and summed in bfloat16 or wider, within the bound.
No kernel may reach another device: no remote copies, remote signals or barrier semaphores. Data moves between devices by JAX's collectives and lax.ppermute only.
A program may use at most 64 MiB of HBM per device.

v0:
```python
import jax
import jax.numpy as jnp
from jax import lax
from jax.sharding import PartitionSpec as P

SAMP_DEV = 16


def extended(cells, sides, width):
    for axis, dim in sides:
        count = lax.axis_size(axis)
        ends = count - 1
        head = lax.slice_in_dim(cells, 0, width, axis=dim)
        tail = lax.slice_in_dim(cells, cells.shape[dim] - width, cells.shape[dim], axis=dim)
        cells = jnp.concatenate(
            [
                lax.ppermute(tail, axis, [(i, (i + 1) % count) for i in range(ends)]),
                cells,
                lax.ppermute(head, axis, [((i + 1) % count, i) for i in range(ends)]),
            ],
            axis=dim,
        )
    return cells


def masked_weights(responses, tap_counts, panel_links, first_tap):
    tap_dev, coupled_ports, group_ports = responses.shape
    half_width = (coupled_ports - group_ports) // 2
    tap_index = first_tap + jnp.arange(tap_dev, dtype=jnp.int32)
    tap_alive = tap_index[:, None] < tap_counts[None, :]
    port_index = jnp.arange(coupled_ports, dtype=jnp.int32)[:, None]
    lower_open = panel_links[None, :, 0] == 1
    upper_open = panel_links[None, :, 1] == 1
    couple_open = jnp.where(
        port_index < half_width,
        lower_open,
        jnp.where(port_index >= half_width + group_ports, upper_open, True),
    )
    keep_mask = tap_alive[:, None, :] & couple_open[None, :, :]
    return jnp.where(keep_mask, responses, jnp.zeros_like(responses))


def per_device(driven_wave, responses, tap_counts, panel_links):
    tap_dev = responses.shape[0]
    group_ports = driven_wave.shape[1]
    coupled_ports = 2 * group_ports
    half_width = group_ports // 2
    total_taps = tap_dev * lax.axis_size("tm")
    first_tap = lax.axis_index("tm") * tap_dev
    weights = masked_weights(responses, tap_counts, panel_links, first_tap)
    widened = extended(driven_wave, (("band", 1),), half_width)
    history = lax.all_gather(widened, "tm", axis=0, tiled=True)
    block_count = tap_dev // 8
    first_row = jnp.int32(0)

    def add_block(block_index, running):
        lead_tap = (8 * block_index).astype(jnp.int32)
        offset = first_row + total_taps - first_tap - lead_tap - 7
        window = lax.dynamic_slice_in_dim(history, offset, lax.axis_size("tm") * SAMP_DEV + 7, 0)
        stacked = jnp.concatenate(
            [
                window[7 - shift_index : 7 - shift_index + lax.axis_size("tm") * SAMP_DEV]
                for shift_index in range(8)
            ],
            axis=1,
        )
        tap_panel = lax.dynamic_slice_in_dim(weights, lead_tap, 8, 0).reshape(
            8 * coupled_ports, group_ports
        )
        return running + jnp.dot(stacked, tap_panel, preferred_element_type=jnp.float32)

    summed = lax.psum_scatter(
        lax.fori_loop(
            0,
            block_count,
            add_block,
            jnp.zeros((lax.axis_size("tm") * SAMP_DEV, group_ports), jnp.float32),
        ),
        "tm",
        scatter_dimension=0,
        tiled=True,
    )
    return summed.astype(jnp.bfloat16)


def solution(mesh):
    return jax.shard_map(
        per_device,
        mesh=mesh,
        in_specs=(P("tm", "band"), P("tm", None, "band"), P("band"), P("band", None)),
        out_specs=P("tm", "band"),
        check_vma=False,
    )
```

profile of v0, /device:TPU:4, one launch (start us, length us, event | category | flops | bytes accessed | tf_op | source)
XLA Modules:
  0.0 309.9 jit_solution(17289685736764098820)
XLA Ops:
  6.5 0.0 all-gather.2.cloned.1.call-start
  6.5 0.7 fusion
  7.3 4.3 %collective-permute-start = (bf16[32,128]{1,0:T(8,128)(2,1)S(1)}, bf16[32,128]{1,0:T(8,128)(2,1)S(1)}, u32[]{:S(2)}, u32[]{:S(2)}) collective-permute-start(bf16[32,128]{1,0:T(8,128)(2,1)S(1)} %get-tuple-element.208), channel_id=1, source_target_pairs={{0,64},{64,128},{128,192},{192,256},{256,320},{320,384},{384,448},... | collective-permute-start | bytes 24584 | tf_op jit(solution)/shard_map/ppermute | solution.py:17
  11.5 2.5 collective-permute-start.1
  14.0 0.0 collective-permute-done
  14.0 3.1 collective-permute-done.1
  17.1 1.3 pad_maximum_fusion
  18.4 0.0 all-gather.2.cloned.1.call-update
  18.4 0.0 reduce-scatter.2.cloned.1.call-start
  18.5 0.8 compare_reduce_fusion.1
  19.3 0.8 broadcast_compare_fusion
  20.1 0.2 select_select_fusion
  20.3 5.4 %and_select_fusion = bf16[16,512,256]{2,1,0:T(8,128)(2,1)} fusion(bf16[16,512,256]{2,1,0:T(8,128)(2,1)} %param.7, pred[512,256]{1,0:T(8,128)(4,1)S(1)} %select_select_fusion, pred[16,256]{1,0:T(8,128)(4,1)S(1)} %broadcast_compare_fusion), kind=kLoop, calls=%fused_computation.10 | loop fusion | flops 4194304 | bytes 8523776 | tf_op jit(solution)/shard_map/jit(_where)/select_n | solution.py:40
  25.7 82.1 %all-gather.2.cloned.1.call-done = bf16[2048,512]{1,0:T(8,128)(2,1)} async-done(((bf16[32,512]{1,0:T(8,128)(2,1)}), bf16[2048,512]{1,0:T(8,128)(2,1)}) %all-gather.2.cloned.1.call-update) | async-done | bytes 2097168 | tf_op jit(solution)/shard_map/all_gather | solution.py:52
  107.8 46.4 %while.18 = (s32[]{:T(128)}, f32[1024,256]{1,0:T(8,128)S(1)}, s32[]{:T(128)}, bf16[2048,512]{1,0:T(8,128)(2,1)}, bf16[16,512,256]{2,1,0:T(8,128)(2,1)}, /*index=...) while((s32[]{:T(128)}, f32[1024,256]{1,0:T(8,128)S(1)}, ...), condition=%wide.region_1.2_spmd.clone, body=%wide.region_0.1_spmd.clone.sunk | while | flops 2148007936 | bytes 41943464 | solution.py:73
  107.8 0.0 copy-start
  107.8 2.5 dynamic-slice_dynamic-update-slice_fusion.16
  110.3 2.5 dynamic-slice_dynamic-update-slice_fusion.17
  112.8 2.5 dynamic-slice_dynamic-update-slice_fusion.18
  115.4 2.5 dynamic-slice_dynamic-update-slice_fusion.19
  117.9 0.0 copy-done
  117.9 1.3 dynamic-slice_dynamic-update-slice_fusion.20
  119.2 1.3 dynamic-slice_dynamic-update-slice_fusion.21
  120.5 1.3 dynamic-slice_dynamic-update-slice_fusion.22
  121.8 1.3 dynamic-slice_dynamic-update-slice_fusion.23
  123.1 1.7 constant_dynamic-slice_fusion.2
  124.9 6.1 %convolution_add_fusion.2 = f32[1024,256]{1,0:T(8,128)S(1)} fusion(bf16[1024,4096]{1,0:T(8,128)(2,1)} %dynamic-slice_dynamic-update-slice_fusion.23, bf16[4096,256]{1,0:T(8,128)(2,1)S(1)} %bitcast.9, f32[1024,256]{1,0:T(8,128)S(1)} %get-tuple-element.262, pred[]{:T(512)S(6)} %compare.3), kind=kOutput, calls=%fused_computation.clone.1 | convolution fusion | flops 2148007936 | bytes 12582913 | tf_op jit(solution)/shard_map/while/body/eval_jaxpr/dot_general | solution.py:70
  131.0 0.0 copy-start
  131.0 2.5 dynamic-slice_dynamic-update-slice_fusion.16
  133.5 2.5 dynamic-slice_dynamic-update-slice_fusion.17
  136.0 2.5 dynamic-slice_dynamic-update-slice_fusion.18
  138.6 2.5 dynamic-slice_dynamic-update-slice_fusion.19
  141.1 0.0 copy-done
  141.1 1.3 dynamic-slice_dynamic-update-slice_fusion.20
  142.4 1.3 dynamic-slice_dynamic-update-slice_fusion.21
  143.7 1.3 dynamic-slice_dynamic-update-slice_fusion.22
  145.0 1.3 dynamic-slice_dynamic-update-slice_fusion.23
  146.3 1.7 constant_dynamic-slice_fusion.2
  148.1 6.1 %convolution_add_fusion.2 = f32[1024,256]{1,0:T(8,128)S(1)} fusion(bf16[1024,4096]{1,0:T(8,128)(2,1)} %dynamic-slice_dynamic-update-slice_fusion.23, bf16[4096,256]{1,0:T(8,128)(2,1)S(1)} %bitcast.9, f32[1024,256]{1,0:T(8,128)S(1)} %get-tuple-element.262, pred[]{:T(512)S(6)} %compare.3), kind=kOutput, calls=%fused_computation.clone.1 | convolution fusion | flops 2148007936 | bytes 12582913 | tf_op jit(solution)/shard_map/while/body/eval_jaxpr/dot_general | solution.py:70
  154.2 0.0 copy-start.1
  154.2 1.0 copy-done.1
  155.2 0.0 reduce-scatter.2.cloned.1.call-update
  155.2 146.5 %reduce-scatter.2.cloned.1.call-done = f32[16,256]{1,0:T(8,128)} async-done(((f32[1024,256]{1,0:T(8,128)}), f32[16,256]{1,0:T(8,128)}) %reduce-scatter.2.cloned.1.call-update) | async-done | bytes 16400 | tf_op jit(solution)/shard_map/reduce_scatter | solution.py:72
  301.7 1.3 convert_element_type.3
  (3 shorter events, 0.0 us)
Async XLA Ops:
  6.5 101.3 %all-gather.2.cloned.1.call-start = ((), (), s32[]{:S(2)}) async-start(), calls=%async_computation.1 | async-start | bytes 2129920 | tf_op jit(solution)/shard_map/all_gather | solution.py:52
  7.3 6.7 %collective-permute-start = (bf16[32,128]{1,0:T(8,128)(2,1)S(1)}, bf16[32,128]{1,0:T(8,128)(2,1)S(1)}, u32[]{:S(2)}, u32[]{:S(2)}) collective-permute-start(bf16[32,128]{1,0:T(8,128)(2,1)S(1)} %get-tuple-element.208), channel_id=1, source_target_pairs={{0,64},{64,128},{128,192},{192,256},{256,320},{320,384},{384,448},... | collective-permute-start | bytes 24584 | tf_op jit(solution)/shard_map/ppermute | solution.py:17
  11.5 5.5 %collective-permute-start.1 = (bf16[32,128]{1,0:T(8,128)(2,1)S(1)}, bf16[32,128]{1,0:T(8,128)(2,1)S(1)}, u32[]{:S(2)}, u32[]{:S(2)}) collective-permute-start(bf16[32,128]{1,0:T(8,128)(2,1)S(1)} %get-tuple-element.209), channel_id=1, source_target_pairs={{64,0},{128,64},{192,128},{256,192},{320,256},{384,320},{448,384},... | collective-permute-start | bytes 24584 | tf_op jit(solution)/shard_map/ppermute | solution.py:19
  18.4 283.3 %reduce-scatter.2.cloned.1.call-start = ((), (), s32[]{:S(2)}) async-start(), calls=%async_computation.2 | async-start | bytes 1064960 | tf_op jit(solution)/shard_map/reduce_scatter | solution.py:72
  107.8 10.1 %copy-start = (bf16[2048,512]{1,0:T(8,128)(2,1)S(1)}, bf16[2048,512]{1,0:T(8,128)(2,1)}, u32[]{:S(2)}) copy-start(bf16[2048,512]{1,0:T(8,128)(2,1)} %get-tuple-element.282) | copy-start | bytes 6291460 | tf_op jit(solution)/shard_map/while
  131.0 10.1 %copy-start = (bf16[2048,512]{1,0:T(8,128)(2,1)S(1)}, bf16[2048,512]{1,0:T(8,128)(2,1)}, u32[]{:S(2)}) copy-start(bf16[2048,512]{1,0:T(8,128)(2,1)} %get-tuple-element.282) | copy-start | bytes 6291460 | tf_op jit(solution)/shard_map/while
  154.2 1.0 copy-start.1
Sparse Core Ops, SparseCore 0:
  18.5 89.2 all-gather.1
  155.3 146.3 reduce-scatter.1
where the time goes:
time: 311 us; the launch traced here: 310 us
  waiting for transfers between devices  232 us (75%)
  local copies, waits for them, and re-layouts  35.8 us (12%)
  between operations  13.5 us (4%)
  matrix products  12.2 us (4%)
  other arithmetic  9.8 us (3%)
  starting transfers between devices  6.77 us (2%)
    reduce_scatter x1, waiting for transfers between devices, per_device(): lax.psum_scatter(lax.fori_loop(0, block_count, add_block, jnp.zeros((lax....  147 us
    all_gather x1, waiting for transfers between devices, per_device(): history = lax.all_gather(widened, 'tm', axis=0, tiled=True)  82.1 us
    while x18, local copies, waits for them, and re-layouts  28 us
    dot_general x2, matrix products, add_block(): jnp.dot(stacked, tap_panel, preferred_element_type=jnp.float32)  12.2 us
  transfers between devices with their start and end apart: 4, of which 3 were waited for; matrix products, arithmetic and copies ran while one was open for 2% of the time, Pallas kernels for 0%

commit v1 on v0

v1 whole, which is shorter than its diff:
```python
import jax
import jax.numpy as jnp
from jax import lax
from jax.sharding import Mesh
from jax.sharding import PartitionSpec as P

TM = ("y", "zh", "core")


def extended(cells, width):
    count = lax.axis_size("band")
    ends = count - 1
    head = cells[:, :width]
    tail = cells[:, cells.shape[1] - width :]
    return jnp.concatenate(
        [
            lax.ppermute(tail, "band", [(i, (i + 1) % count) for i in range(ends)]),
            cells,
            lax.ppermute(head, "band", [((i + 1) % count, i) for i in range(ends)]),
        ],
        axis=1,
    )


def masked_weights(responses, tap_counts, panel_links, first_tap):
    tap_dev, coupled_ports, group_ports = responses.shape
    half_width = (coupled_ports - group_ports) // 2
    tap_index = first_tap + jnp.arange(tap_dev, dtype=jnp.int32)
    tap_alive = tap_index[:, None] < tap_counts[None, :]
    port_index = jnp.arange(coupled_ports, dtype=jnp.int32)[:, None]
    lower_open = panel_links[None, :, 0] == 1
    upper_open = panel_links[None, :, 1] == 1
    couple_open = jnp.where(
        port_index < half_width,
        lower_open,
        jnp.where(port_index >= half_width + group_ports, upper_open, True),
    )
    keep_mask = tap_alive[:, None, :] & couple_open[None, :, :]
    return jnp.where(keep_mask, responses, jnp.zeros_like(responses))


def gather_history(x):
    x = lax.all_gather(x, "core", axis=0, tiled=True)
    x = lax.all_gather(x, "zh", axis=0, tiled=True)
    return lax.all_gather(x, "y", axis=0, tiled=True)


def tm_index():
    return (lax.axis_index("y") * lax.axis_size("zh") + lax.axis_index("zh")) * lax.axis_size(
        "core"
    ) + lax.axis_index("core")


def per_device(driven_wave, responses, tap_counts, panel_links):
    tap_dev = responses.shape[0]
    group_ports = driven_wave.shape[1]
    half_width = group_ports // 2
    n_tm = lax.axis_size("y") * lax.axis_size("zh") * lax.axis_size("core")
    total_taps = tap_dev * n_tm
    window_len = driven_wave.shape[0] * n_tm - total_taps
    me = tm_index()
    first_tap = me * tap_dev
    weights = masked_weights(responses, tap_counts, panel_links, first_tap)[::-1]
    history = gather_history(extended(driven_wave, half_width))
    base = total_taps - first_tap - (tap_dev - 1)
    window = lax.dynamic_slice_in_dim(history, base, window_len + tap_dev - 1, 0)
    partial = lax.conv_general_dilated(
        window[None],
        weights,
        window_strides=(1,),
        padding="VALID",
        dimension_numbers=("NWC", "WIO", "NWC"),
        preferred_element_type=jnp.float32,
    )[0]
    blocks = partial.reshape(n_tm, window_len // n_tm, group_ports)
    summed = lax.all_to_all(blocks, TM, 0, 0, tiled=True).sum(0)
    return summed.astype(jnp.bfloat16)


def solution(mesh):
    band, tm = mesh.devices.shape
    view = Mesh(mesh.devices.reshape(band, tm // 8, 4, 2), ("band",) + TM)
    return jax.shard_map(
        per_device,
        mesh=view,
        in_specs=(P(TM, "band"), P(TM, None, "band"), P("band"), P("band", None)),
        out_specs=P(TM, "band"),
        check_vma=False,
    )
```

time: 311 us -> 147 us (0.47)
  the two profiles are of different devices: /device:TPU:4 before, /device:TPU:16 now
where the time goes in v1:
time: 147 us; the launch traced here: 146 us
  blocking collectives  64 us (44%)
  waiting for transfers between devices  45.3 us (31%)
  between operations  13.5 us (9%)
  matrix products  10.8 us (7%)
  starting transfers between devices  5.56 us (4%)
  local copies, waits for them, and re-layouts  3.85 us (3%)
  other arithmetic  3.16 us (2%)
    all_to_all x1, blocking collectives, per_device(): summed = lax.all_to_all(blocks, TM, 0, 0, tiled=True).sum(0)  42.8 us
    all_gather x1, waiting for transfers between devices, gather_history(): return lax.all_gather(x, 'y', axis=0, tiled=True)  41.1 us
    all_gather x1, blocking collectives, gather_history(): x = lax.all_gather(x, 'zh', axis=0, tiled=True)  19.3 us
    conv_general_dilated x1, matrix products, per_device(): lax.conv_general_dilated(window[None], weights, window_strides=(1,), padd...  10.8 us
    ppermute x1, starting transfers between devices, extended(): lax.ppermute(tail, 'band', [(i, (i + 1) % count) for i in range(ends)])  4.26 us
    ppermute x1, waiting for transfers between devices, extended(): lax.ppermute(head, 'band', [((i + 1) % count, i) for i in range(ends)])  4.2 us
  transfers between devices with their start and end apart: 3, of which 2 were waited for; matrix products, arithmetic and copies ran while one was open for 1% of the time, Pallas kernels for 0%

profile of v1, /device:TPU:16, one launch (start us, length us, event | category | flops | bytes accessed | tf_op | source)
XLA Modules:
  0.0 146.2 jit_solution(13191528856447470988)
XLA Ops:
  6.5 0.0 all-gather.2.cloned.1.call-start
  6.5 0.7 fusion.16
  7.3 4.3 %collective-permute-start = (bf16[32,128]{1,0:T(8,128)(2,1)S(1)}, bf16[32,128]{1,0:T(8,128)(2,1)S(1)}, u32[]{:S(2)}, u32[]{:S(2)}) collective-permute-start(bf16[32,128]{1,0:T(8,128)(2,1)S(1)} %get-tuple-element.7), channel_id=1, source_target_pairs={{0,64},{64,128},{128,192},{192,256},{256,320},{320,384},{384,448},... | collective-permute-start | bytes 24584 | tf_op jit(solution)/shard_map/ppermute | solution.py:17
  11.5 1.3 collective-permute-start.1
  12.8 0.0 collective-permute-done
  12.9 4.2 %collective-permute-done.1 = bf16[32,128]{1,0:T(8,128)(2,1)S(1)} collective-permute-done((bf16[32,128]{1,0:T(8,128)(2,1)S(1)}, bf16[32,128]{1,0:T(8,128)(2,1)S(1)}, u32[]{:S(2)}, u32[]{:S(2)}) %collective-permute-start.1) | collective-permute-done | bytes 8224 | tf_op jit(solution)/shard_map/ppermute | solution.py:19
  17.1 0.7 pad_maximum_fusion
  17.8 1.8 %all_gather.9 = bf16[64,512]{1,0:T(8,128)(2,1)S(1)} all-gather(bf16[32,512]{1,0:T(8,128)(2,1)S(1)} %pad_maximum_fusion), channel_id=1, replica_groups=mesh['band'=8,'y'=8,'zh'=4,'core'=2] {'core'}, dimensions={0}, use_global_device_ids=true | all-gather | bytes 98304 | tf_op jit(solution)/shard_map/all_gather | solution.py:43
  19.6 19.3 %all_gather.10 = bf16[256,512]{1,0:T(8,128)(2,1)} all-gather(bf16[64,512]{1,0:T(8,128)(2,1)S(1)} %all_gather.9), channel_id=1, replica_groups=mesh['band'=8,'y'=8,'zh'=4,'core'=2] {'zh'}, dimensions={0}, use_global_device_ids=true | all-gather | bytes 327680 | tf_op jit(solution)/shard_map/all_gather | solution.py:44
  39.0 0.0 all-gather.2.cloned.1.call-update
  39.0 0.8 compare_reduce_fusion.1
  39.8 0.8 broadcast_compare_fusion
  40.6 0.2 select_select_fusion
  40.8 41.1 %all-gather.2.cloned.1.call-done = bf16[2048,512]{1,0:T(8,128)(2,1)} async-done(((bf16[256,512]{1,0:T(8,128)(2,1)}), bf16[2048,512]{1,0:T(8,128)(2,1)}) %all-gather.2.cloned.1.call-update) | async-done | bytes 2097168 | tf_op jit(solution)/shard_map/all_gather | solution.py:45
  81.9 1.5 %dynamic-slice_bitcast_fusion = bf16[1,1039,512]{2,1,0:T(8,128)(2,1)S(1)} fusion(bf16[2048,512]{1,0:T(8,128)(2,1)} %all-gather.2.cloned.1.call-done, s32[]{:T(128)S(6)} %select_n.23), kind=kLoop, calls=%fused_computation.13 | loop fusion | bytes 2127876 | tf_op jit(solution)/shard_map/broadcast_in_dim | solution.py:68
  83.3 0.1 pad
  83.4 0.3 reshape.111
  83.8 0.0 copy-start
  83.8 0.3 copy.6
  84.2 0.3 copy-done
  84.5 10.8 %fusion.5 = f32[8,130,256]{2,0,1:T(8,128)S(1)} fusion(bf16[16,512,256]{2,1,0:T(8,128)(2,1)} %param.5, pred[512,256]{1,0:T(8,128)(4,1)S(1)} %select_select_fusion, pred[16,256]{1,0:T(8,128)(4,1)S(1)} %broadcast_compare_fusion, bf16[1,7,15,512]{3,1,2,0:T(8,128)(2,1)S(1)} %slice.18, bf16[1,8,130,512]{3,1,2,0:T(8,128)(2,1)S(1)} %copy.6, ...), kind=kOutput, calls=%fused_computation.7 | convolution fusion | flops 4370100224 | bytes 6567952 | tf_op jit(solution)/shard_map/conv_general_dilated | solution.py:67
  95.3 0.3 copy.7
  95.6 0.1 reshape.115
  95.8 0.1 slice.19
  95.8 42.8 %all_to_all.5 = f32[64,16,256]{2,1,0:T(8,128)S(1)} all-to-all(f32[64,16,256]{2,1,0:T(8,128)S(1)} %bitcast.6), channel_id=1, replica_groups=mesh['band'=8,'y'=8,'zh'=4,'core'=2] {'y','zh','core'}, dimensions={0} | all-to-all | bytes 2097152 | tf_op jit(solution)/shard_map/all_to_all | solution.py:76
  138.6 0.7 reduce_sum.9
  (3 shorter events, 0.0 us)
Async XLA Ops:
  6.5 75.3 %all-gather.2.cloned.1.call-start = ((), (), s32[]{:S(2)}) async-start(), calls=%async_computation.1 | async-start | bytes 2359296 | tf_op jit(solution)/shard_map/all_gather | solution.py:45
  7.3 5.6 %collective-permute-start = (bf16[32,128]{1,0:T(8,128)(2,1)S(1)}, bf16[32,128]{1,0:T(8,128)(2,1)S(1)}, u32[]{:S(2)}, u32[]{:S(2)}) collective-permute-start(bf16[32,128]{1,0:T(8,128)(2,1)S(1)} %get-tuple-element.7), channel_id=1, source_target_pairs={{0,64},{64,128},{128,192},{192,256},{256,320},{320,384},{384,448},... | collective-permute-start | bytes 24584 | tf_op jit(solution)/shard_map/ppermute | solution.py:17
  11.5 5.5 %collective-permute-start.1 = (bf16[32,128]{1,0:T(8,128)(2,1)S(1)}, bf16[32,128]{1,0:T(8,128)(2,1)S(1)}, u32[]{:S(2)}, u32[]{:S(2)}) collective-permute-start(bf16[32,128]{1,0:T(8,128)(2,1)S(1)} %get-tuple-element.8), channel_id=1, source_target_pairs={{64,0},{128,64},{192,128},{256,192},{320,256},{384,320},{448,384},... | collective-permute-start | bytes 24584 | tf_op jit(solution)/shard_map/ppermute | solution.py:19
  83.8 0.7 copy-start
Sparse Core Ops, SparseCore 0:
  39.1 42.6 all-gather.1

commit v2 on v1

--- a/solution.py
+++ b/solution.py
@@ -39,10 +39,28 @@
     return jnp.where(keep_mask, responses, jnp.zeros_like(responses))
 
 
+def swap_core(x):
+    return lax.ppermute(x, "core", [(0, 1), (1, 0)])
+
+
 def gather_history(x):
-    x = lax.all_gather(x, "core", axis=0, tiled=True)
-    x = lax.all_gather(x, "zh", axis=0, tiled=True)
-    return lax.all_gather(x, "y", axis=0, tiled=True)
+    chips = lax.axis_size("y") * lax.axis_size("zh")
+    spread = jnp.broadcast_to(x[None], (chips,) + x.shape)
+    mine = lax.all_to_all(spread, ("y", "zh"), 0, 0, tiled=True)
+    other = swap_core(mine)
+    first = lax.axis_index("core") == 0
+    pair = jnp.stack([jnp.where(first, mine, other), jnp.where(first, other, mine)], 1)
+    return pair.reshape(-1, x.shape[1])
+
+
+def reduce_scatter(partial, n_tm):
+    chips = n_tm // 2
+    blocks = partial.reshape(chips, 2, partial.shape[0] // n_tm, partial.shape[1])
+    first = lax.axis_index("core") == 0
+    keep = jnp.where(first, blocks[:, 0], blocks[:, 1])
+    give = jnp.where(first, blocks[:, 1], blocks[:, 0])
+    combined = keep + swap_core(give)
+    return lax.all_to_all(combined, ("y", "zh"), 0, 0, tiled=True).sum(0)
 
 
 def tm_index():
@@ -72,8 +90,7 @@
         dimension_numbers=("NWC", "WIO", "NWC"),
         preferred_element_type=jnp.float32,
     )[0]
-    blocks = partial.reshape(n_tm, window_len // n_tm, group_ports)
-    summed = lax.all_to_all(blocks, TM, 0, 0, tiled=True).sum(0)
+    summed = reduce_scatter(partial, n_tm)
     return summed.astype(jnp.bfloat16)
 
 

time: 147 us -> 104 us (0.71)
  the two profiles are of different devices: /device:TPU:16 before, /device:TPU:14 now
where the time goes in v2:
time: 104 us; the launch traced here: 103 us
  blocking collectives  69.7 us (67%)
  matrix products  10.8 us (10%)
  starting transfers between devices  10.7 us (10%)
  waiting for transfers between devices  7.08 us (7%)
  local copies, waits for them, and re-layouts  2.42 us (2%)
  other arithmetic  2.25 us (2%)
    all_to_all x1, blocking collectives, gather_history(): mine = lax.all_to_all(spread, ('y', 'zh'), 0, 0, tiled=True)  43.5 us
    all_to_all x1, blocking collectives, reduce_scatter(): return lax.all_to_all(combined, ('y', 'zh'), 0, 0, tiled=True).sum(0)  26.2 us
    conv_general_dilated x1, matrix products, per_device(): lax.conv_general_dilated(window[None], weights, window_strides=(1,), padd...  10.8 us
    ppermute x1, starting transfers between devices, extended(): lax.ppermute(tail, 'band', [(i, (i + 1) % count) for i in range(ends)])  4.27 us
    ppermute x2, waiting for transfers between devices, swap_core(): return lax.ppermute(x, 'core', [(0, 1), (1, 0)])  4.01 us
    ppermute x2, starting transfers between devices, swap_core(): return lax.ppermute(x, 'core', [(0, 1), (1, 0)])  3.95 us
    ppermute x1, waiting for transfers between devices, extended(): lax.ppermute(head, 'band', [((i + 1) % count, i) for i in range(ends)])  3.07 us
    ppermute x1, starting transfers between devices, extended(): lax.ppermute(head, 'band', [((i + 1) % count, i) for i in range(ends)])  2.46 us
  transfers between devices with their start and end apart: 4, of which 3 were waited for; matrix products, arithmetic and copies ran while one was open for 0% of the time, Pallas kernels for 0%

profile of v2, /device:TPU:14, one launch (start us, length us, event | category | flops | bytes accessed | tf_op | source)
XLA Modules:
  0.0 103.1 jit_solution(17955386621250958415)
XLA Ops:
  0.0 0.0 copy-start
  0.0 0.0 copy-start.1
  0.0 0.7 fusion.18
  0.7 4.3 %collective-permute-start = (bf16[32,128]{1,0:T(8,128)(2,1)S(1)}, bf16[32,128]{1,0:T(8,128)(2,1)S(1)}, u32[]{:S(2)}, u32[]{:S(2)}) collective-permute-start(bf16[32,128]{1,0:T(8,128)(2,1)S(1)} %get-tuple-element.9), channel_id=1, source_target_pairs={{0,64},{64,128},{128,192},{192,256},{256,320},{320,384},{384,448},... | collective-permute-start | bytes 24584 | tf_op jit(solution)/shard_map/ppermute | solution.py:17
  5.0 2.5 %collective-permute-start.1 = (bf16[32,128]{1,0:T(8,128)(2,1)S(1)}, bf16[32,128]{1,0:T(8,128)(2,1)S(1)}, u32[]{:S(2)}, u32[]{:S(2)}) collective-permute-start(bf16[32,128]{1,0:T(8,128)(2,1)S(1)} %get-tuple-element.10), channel_id=1, source_target_pairs={{64,0},{128,64},{192,128},{256,192},{320,256},{384,320},{448,384},... | collective-permute-start | bytes 24584 | tf_op jit(solution)/shard_map/ppermute | solution.py:19
  7.5 0.0 collective-permute-done
  7.5 3.1 %collective-permute-done.1 = bf16[32,128]{1,0:T(8,128)(2,1)S(1)} collective-permute-done((bf16[32,128]{1,0:T(8,128)(2,1)S(1)}, bf16[32,128]{1,0:T(8,128)(2,1)S(1)}, u32[]{:S(2)}, u32[]{:S(2)}) %collective-permute-start.1) | collective-permute-done | bytes 8224 | tf_op jit(solution)/shard_map/ppermute | solution.py:19
  10.6 0.7 pad_maximum_fusion.1
  11.3 0.1 broadcast_in_dim.53
  11.4 43.5 %all_to_all.10 = bf16[32,32,512]{2,1,0:T(8,128)(2,1)S(1)} all-to-all(bf16[32,32,512]{2,1,0:T(8,128)(2,1)S(1)} %broadcast_in_dim.53), channel_id=1, replica_groups=mesh['band'=8,'y'=8,'zh'=4,'core'=2] {'y','zh'}, dimensions={0} | all-to-all | bytes 2097152 | tf_op jit(solution)/shard_map/all_to_all | solution.py:49
  54.9 1.9 %collective-permute-start.2 = (bf16[32,32,512]{2,1,0:T(8,128)(2,1)S(1)}, bf16[32,32,512]{2,1,0:T(8,128)(2,1)S(1)}, u32[]{:S(2)}, u32[]{:S(2)}) collective-permute-start(bf16[32,32,512]{2,1,0:T(8,128)(2,1)S(1)} %all_to_all.10), channel_id=1, source_target_pairs={{0,1},{1,0},{2,3},{3,2},{4,5},{5,4},{6,7},{7,6},{8,9},{9,8},{10,11... | collective-permute-start | bytes 3145736 | tf_op jit(solution)/shard_map/ppermute | solution.py:43
  56.9 0.0 copy-done
  56.9 0.0 copy-done.1
  56.9 0.1 broadcast_compare_fusion
  57.0 0.2 select_select_fusion
  57.2 2.3 %collective-permute-done.2 = bf16[32,32,512]{2,1,0:T(8,128)(2,1)S(1)} collective-permute-done((bf16[32,32,512]{2,1,0:T(8,128)(2,1)S(1)}, bf16[32,32,512]{2,1,0:T(8,128)(2,1)S(1)}, u32[]{:S(2)}, u32[]{:S(2)}) %collective-permute-start.2) | collective-permute-done | bytes 1048608 | tf_op jit(solution)/shard_map/ppermute | solution.py:43
  59.5 0.1 select_bitcast_fusion.1
  59.6 0.2 pad_maximum_fusion
  59.8 0.3 dynamic-slice_bitcast_fusion
  60.1 0.1 pad
  60.2 0.0 copy-start.2
  60.2 0.3 reshape.120
  60.5 0.3 copy.10
  60.9 0.0 copy-done.2
  60.9 10.8 %fusion.5 = f32[8,130,256]{2,0,1:T(8,128)S(1)} fusion(bf16[16,512,256]{2,1,0:T(8,128)(2,1)} %param.5, pred[512,256]{1,0:T(8,128)(4,1)S(1)} %select_select_fusion, pred[16,256]{1,0:T(8,128)(4,1)S(1)} %broadcast_compare_fusion, bf16[1,7,15,512]{3,1,2,0:T(8,128)(2,1)S(1)} %slice.28, bf16[1,8,130,512]{3,1,2,0:T(8,128)(2,1)S(1)} %copy.10, ...), kind=kOutput, calls=%fused_computation.8 | convolution fusion | flops 4370100224 | bytes 6567952 | tf_op jit(solution)/shard_map/conv_general_dilated | solution.py:85
  71.7 0.3 copy.11
  72.0 0.1 reshape.124
  72.2 0.1 slice.29
  72.3 0.1 select_bitcast_fusion.2
  72.3 2.0 %collective-permute-start.3 = (f32[32,16,256]{2,1,0:T(8,128)S(1)}, f32[32,16,256]{2,1,0:T(8,128)S(1)}, u32[]{:S(2)}, u32[]{:S(2)}) collective-permute-start(f32[32,16,256]{2,1,0:T(8,128)S(1)} %select_bitcast_fusion.2), channel_id=1, source_target_pairs={{0,1},{1,0},{2,3},{3,2},{4,5},{5,4},{6,7},{7,6},{8,9},{9,8},{10,11... | collective-permute-start | bytes 1572872 | tf_op jit(solution)/shard_map/ppermute | solution.py:43
  74.4 1.8 %collective-permute-done.3 = f32[32,16,256]{2,1,0:T(8,128)S(1)} collective-permute-done((f32[32,16,256]{2,1,0:T(8,128)S(1)}, f32[32,16,256]{2,1,0:T(8,128)S(1)}, u32[]{:S(2)}, u32[]{:S(2)}) %collective-permute-start.3) | collective-permute-done | bytes 524320 | tf_op jit(solution)/shard_map/ppermute | solution.py:43
  76.2 0.1 fusion.14
  76.3 26.2 %all_to_all.11 = f32[32,16,256]{2,1,0:T(8,128)S(1)} all-to-all(f32[32,16,256]{2,1,0:T(8,128)S(1)} %fusion.14), channel_id=1, replica_groups=mesh['band'=8,'y'=8,'zh'=4,'core'=2] {'y','zh'}, dimensions={0} | all-to-all | bytes 1048576 | tf_op jit(solution)/shard_map/all_to_all | solution.py:63
  102.5 0.6 reduce_sum.9
  (4 shorter events, 0.1 us)
Async XLA Ops:
  0.0 56.9 %copy-start = (s32[256,2]{0,1:T(2,128)S(1)}, s32[256,2]{0,1:T(2,128)}, u32[]{:S(2)}) copy-start(s32[256,2]{0,1:T(2,128)} %param.7) | copy-start | bytes 6148
  0.0 56.9 %copy-start.1 = (s32[256]{0:T(256)S(1)}, s32[256]{0:T(256)}, u32[]{:S(2)}) copy-start(s32[256]{0:T(256)} %param.6) | copy-start | bytes 3076
  0.7 6.7 %collective-permute-start = (bf16[32,128]{1,0:T(8,128)(2,1)S(1)}, bf16[32,128]{1,0:T(8,128)(2,1)S(1)}, u32[]{:S(2)}, u32[]{:S(2)}) collective-permute-start(bf16[32,128]{1,0:T(8,128)(2,1)S(1)} %get-tuple-element.9), channel_id=1, source_target_pairs={{0,64},{64,128},{128,192},{192,256},{256,320},{320,384},{384,448},... | collective-permute-start | bytes 24584 | tf_op jit(solution)/shard_map/ppermute | solution.py:17
  5.0 5.5 %collective-permute-start.1 = (bf16[32,128]{1,0:T(8,128)(2,1)S(1)}, bf16[32,128]{1,0:T(8,128)(2,1)S(1)}, u32[]{:S(2)}, u32[]{:S(2)}) collective-permute-start(bf16[32,128]{1,0:T(8,128)(2,1)S(1)} %get-tuple-element.10), channel_id=1, source_target_pairs={{64,0},{128,64},{192,128},{256,192},{320,256},{384,320},{448,384},... | collective-permute-start | bytes 24584 | tf_op jit(solution)/shard_map/ppermute | solution.py:19
  54.9 4.5 %collective-permute-start.2 = (bf16[32,32,512]{2,1,0:T(8,128)(2,1)S(1)}, bf16[32,32,512]{2,1,0:T(8,128)(2,1)S(1)}, u32[]{:S(2)}, u32[]{:S(2)}) collective-permute-start(bf16[32,32,512]{2,1,0:T(8,128)(2,1)S(1)} %all_to_all.10), channel_id=1, source_target_pairs={{0,1},{1,0},{2,3},{3,2},{4,5},{5,4},{6,7},{7,6},{8,9},{9,8},{10,11... | collective-permute-start | bytes 3145736 | tf_op jit(solution)/shard_map/ppermute | solution.py:43
  60.2 0.7 copy-start.2
  72.3 3.8 %collective-permute-start.3 = (f32[32,16,256]{2,1,0:T(8,128)S(1)}, f32[32,16,256]{2,1,0:T(8,128)S(1)}, u32[]{:S(2)}, u32[]{:S(2)}) collective-permute-start(f32[32,16,256]{2,1,0:T(8,128)S(1)} %select_bitcast_fusion.2), channel_id=1, source_target_pairs={{0,1},{1,0},{2,3},{3,2},{4,5},{5,4},{6,7},{7,6},{8,9},{9,8},{10,11... | collective-permute-start | bytes 1572872 | tf_op jit(solution)/shard_map/ppermute | solution.py:43

commit v3 on v2

--- a/solution.py
+++ b/solution.py
@@ -1,6 +1,8 @@
 import jax
 import jax.numpy as jnp
 from jax import lax
+from jax.experimental import pallas as pl
+from jax.experimental.pallas import tpu as pltpu
 from jax.sharding import Mesh
 from jax.sharding import PartitionSpec as P
 
@@ -69,6 +71,59 @@
     ) + lax.axis_index("core")
 
 
+ROW_TILE = 256
+
+
+def conv_kernel(x_ref, w_ref, m_ref, o_ref, wm_ref):
+    taps, coupled, ports = w_ref.shape
+    half = (coupled - ports) // 2
+    for k in range(taps):
+        marks = m_ref[k]
+        for lo, hi, row in ((0, half, 0), (half, half + ports, 1), (half + ports, coupled, 2)):
+            keep = marks[row : row + 1, :] != 0
+            block = w_ref[k, lo:hi, :]
+            wm_ref[k, lo:hi, :] = jnp.where(keep, block, jnp.zeros_like(block))
+    rows = o_ref.shape[0]
+    for r in range(rows // ROW_TILE):
+        start = r * ROW_TILE
+        acc = jnp.zeros((ROW_TILE, ports), jnp.float32)
+        for k in range(taps):
+            shift = taps - k
+            acc = acc + jnp.dot(
+                x_ref[start + shift : start + shift + ROW_TILE, :],
+                wm_ref[k],
+                preferred_element_type=jnp.float32,
+            )
+        o_ref[start : start + ROW_TILE, :] = acc
+
+
+def masked_conv(window, responses, marks, rows):
+    taps, coupled, ports = responses.shape
+    vmem = pl.BlockSpec(memory_space=pltpu.VMEM)
+    return pl.pallas_call(
+        conv_kernel,
+        out_shape=jax.ShapeDtypeStruct((rows, ports), jnp.float32),
+        in_specs=[vmem, vmem, vmem],
+        out_specs=vmem,
+        scratch_shapes=[pltpu.VMEM((taps, coupled, ports), responses.dtype)],
+        compiler_params=pltpu.CompilerParams(vmem_limit_bytes=48 * 1024 * 1024),
+        cost_estimate=pl.CostEstimate(
+            flops=2 * rows * taps * coupled * ports,
+            transcendentals=0,
+            bytes_accessed=window.size * 2 + responses.size * 2 + rows * ports * 4,
+        ),
+    )(window, responses, marks)
+
+
+def tap_marks(tap_counts, panel_links, first_tap, taps):
+    tap_index = first_tap + jnp.arange(taps, dtype=jnp.int32)
+    alive = tap_index[:, None] < tap_counts[None, :]
+    lower = alive & (panel_links[None, :, 0] == 1)
+    upper = alive & (panel_links[None, :, 1] == 1)
+    marks = jnp.stack([lower, alive, upper], 1).astype(jnp.int32)
+    return jnp.pad(marks, ((0, 0), (0, 5), (0, 0)))
+
+
 def per_device(driven_wave, responses, tap_counts, panel_links):
     tap_dev = responses.shape[0]
     group_ports = driven_wave.shape[1]
@@ -78,18 +133,11 @@
     window_len = driven_wave.shape[0] * n_tm - total_taps
     me = tm_index()
     first_tap = me * tap_dev
-    weights = masked_weights(responses, tap_counts, panel_links, first_tap)[::-1]
     history = gather_history(extended(driven_wave, half_width))
-    base = total_taps - first_tap - (tap_dev - 1)
-    window = lax.dynamic_slice_in_dim(history, base, window_len + tap_dev - 1, 0)
-    partial = lax.conv_general_dilated(
-        window[None],
-        weights,
-        window_strides=(1,),
-        padding="VALID",
-        dimension_numbers=("NWC", "WIO", "NWC"),
-        preferred_element_type=jnp.float32,
-    )[0]
+    base = total_taps - first_tap - tap_dev
+    window = lax.dynamic_slice_in_dim(history, base, window_len + tap_dev, 0)
+    marks = tap_marks(tap_counts, panel_links, first_tap, tap_dev)
+    partial = masked_conv(window, responses, marks, window_len)
     summed = reduce_scatter(partial, n_tm)
     return summed.astype(jnp.bfloat16)
 

time: 104 us -> 97.9 us (0.941)
  matrix products: 10.8 us -> 0 us
  Pallas kernels: 0 us -> 6.7 us
  local copies, waits for them, and re-layouts: 2.42 us -> 0.94 us
    conv_general_dilated x1 -> x0, matrix products: 10.8 us -> none  [per_device(): lax.conv_general_dilated(window[None], weights, window_strides=(1,), padd...]
    pallas_call x0 -> x1, Pallas kernels: none -> 6.7 us  [masked_conv(): pl.pallas_call(conv_kernel, out_shape=jax.ShapeDtypeStruct((rows, ports),...]
    conv_general_dilated x6 -> x0, local copies, waits for them, and re-layouts: 1.23 us -> none  [per_device(): lax.conv_general_dilated(window[None], weights, window_strides=(1,), padd...]
where the time goes in v3:
time: 97.9 us; the launch traced here: 97.5 us
  blocking collectives  69.7 us (71%)
  starting transfers between devices  10.7 us (11%)
  waiting for transfers between devices  7.16 us (7%)
  Pallas kernels  6.7 us (7%)
  other arithmetic  2.17 us (2%)
    all_to_all x1, blocking collectives, gather_history(): mine = lax.all_to_all(spread, ('y', 'zh'), 0, 0, tiled=True)  43.5 us
    all_to_all x1, blocking collectives, reduce_scatter(): return lax.all_to_all(combined, ('y', 'zh'), 0, 0, tiled=True).sum(0)  26.2 us
    pallas_call x1, Pallas kernels, masked_conv(): pl.pallas_call(conv_kernel, out_shape=jax.ShapeDtypeStruct((rows, ports),...  6.7 us
    ppermute x1, starting transfers between devices, extended(): lax.ppermute(tail, 'band', [(i, (i + 1) % count) for i in range(ends)])  4.27 us
    ppermute x2, waiting for transfers between devices, swap_core(): return lax.ppermute(x, 'core', [(0, 1), (1, 0)])  4.09 us
    ppermute x2, starting transfers between devices, swap_core(): return lax.ppermute(x, 'core', [(0, 1), (1, 0)])  3.95 us
    ppermute x1, waiting for transfers between devices, extended(): lax.ppermute(head, 'band', [((i + 1) % count, i) for i in range(ends)])  3.07 us
    ppermute x1, starting transfers between devices, extended(): lax.ppermute(head, 'band', [((i + 1) % count, i) for i in range(ends)])  2.46 us
  transfers between devices with their start and end apart: 4, of which 3 were waited for; matrix products, arithmetic and copies ran while one was open for 0% of the time, Pallas kernels for 0%

profile of v3, /device:TPU:14, one launch (start us, length us, event | category | flops | bytes accessed | tf_op | source)
XLA Modules:
  0.0 97.5 jit_solution(7270250539865653412)
XLA Ops:
  0.0 0.0 copy-start
  0.0 0.0 copy-start.1
  0.0 0.7 fusion.2
  0.7 4.3 %collective-permute-start = (bf16[32,128]{1,0:T(8,128)(2,1)S(1)}, bf16[32,128]{1,0:T(8,128)(2,1)S(1)}, u32[]{:S(2)}, u32[]{:S(2)}) collective-permute-start(bf16[32,128]{1,0:T(8,128)(2,1)S(1)} %get-tuple-element.9), channel_id=1, source_target_pairs={{0,64},{64,128},{128,192},{192,256},{256,320},{320,384},{384,448},... | collective-permute-start | bytes 24584 | tf_op jit(solution)/shard_map/ppermute | solution.py:19
  5.0 2.5 %collective-permute-start.1 = (bf16[32,128]{1,0:T(8,128)(2,1)S(1)}, bf16[32,128]{1,0:T(8,128)(2,1)S(1)}, u32[]{:S(2)}, u32[]{:S(2)}) collective-permute-start(bf16[32,128]{1,0:T(8,128)(2,1)S(1)} %get-tuple-element.10), channel_id=1, source_target_pairs={{64,0},{128,64},{192,128},{256,192},{320,256},{384,320},{448,384},... | collective-permute-start | bytes 24584 | tf_op jit(solution)/shard_map/ppermute | solution.py:21
  7.5 0.0 collective-permute-done
  7.5 3.1 %collective-permute-done.1 = bf16[32,128]{1,0:T(8,128)(2,1)S(1)} collective-permute-done((bf16[32,128]{1,0:T(8,128)(2,1)S(1)}, bf16[32,128]{1,0:T(8,128)(2,1)S(1)}, u32[]{:S(2)}, u32[]{:S(2)}) %collective-permute-start.1) | collective-permute-done | bytes 8224 | tf_op jit(solution)/shard_map/ppermute | solution.py:21
  10.6 0.7 pad_maximum_fusion.1
  11.3 0.1 broadcast_in_dim.2
  11.4 43.5 %all_to_all.10 = bf16[32,32,512]{2,1,0:T(8,128)(2,1)S(1)} all-to-all(bf16[32,32,512]{2,1,0:T(8,128)(2,1)S(1)} %broadcast_in_dim.2), channel_id=1, replica_groups=mesh['band'=8,'y'=8,'zh'=4,'core'=2] {'y','zh'}, dimensions={0} | all-to-all | bytes 2097152 | tf_op jit(solution)/shard_map/all_to_all | solution.py:51
  54.9 1.9 %collective-permute-start.2 = (bf16[32,32,512]{2,1,0:T(8,128)(2,1)S(1)}, bf16[32,32,512]{2,1,0:T(8,128)(2,1)S(1)}, u32[]{:S(2)}, u32[]{:S(2)}) collective-permute-start(bf16[32,32,512]{2,1,0:T(8,128)(2,1)S(1)} %all_to_all.10), channel_id=1, source_target_pairs={{0,1},{1,0},{2,3},{3,2},{4,5},{5,4},{6,7},{7,6},{8,9},{9,8},{10,11... | collective-permute-start | bytes 3145736 | tf_op jit(solution)/shard_map/ppermute | solution.py:45
  56.9 0.0 copy-done
  56.9 0.0 copy-done.1
  56.9 0.1 broadcast_and_fusion.1
  57.0 0.1 pad_add_fusion
  57.1 2.3 %collective-permute-done.2 = bf16[32,32,512]{2,1,0:T(8,128)(2,1)S(1)} collective-permute-done((bf16[32,32,512]{2,1,0:T(8,128)(2,1)S(1)}, bf16[32,32,512]{2,1,0:T(8,128)(2,1)S(1)}, u32[]{:S(2)}, u32[]{:S(2)}) %collective-permute-start.2) | collective-permute-done | bytes 1048608 | tf_op jit(solution)/shard_map/ppermute | solution.py:45
  59.5 0.1 select_bitcast_fusion.1
  59.6 0.2 pad_maximum_fusion
  59.8 0.1 constant_dynamic-slice_fusion.x_ref
  59.9 6.7 %shard_map.46 = f32[1024,256]{1,0:T(8,128)S(1)} custom-call(bf16[1040,512]{1,0:T(8,128)(2,1)S(1)} %constant_dynamic-slice_fusion.x_ref, bf16[16,512,256]{2,1,0:T(8,128)(2,1)} %w_ref.1, s32[16,8,256]{2,1,0:T(8,128)S(1)} %pad_convert_fusion.m_ref), custom_call_target="tpu_custom_call" | custom-call | flops 4294967296 | bytes 6307840 | tf_op jit(solution)/shard_map/pallas_call | solution.py:103
  66.6 0.1 select_bitcast_fusion.2
  66.7 2.0 %collective-permute-start.3 = (f32[32,16,256]{2,1,0:T(8,128)S(1)}, f32[32,16,256]{2,1,0:T(8,128)S(1)}, u32[]{:S(2)}, u32[]{:S(2)}) collective-permute-start(f32[32,16,256]{2,1,0:T(8,128)S(1)} %select_bitcast_fusion.2), channel_id=1, source_target_pairs={{0,1},{1,0},{2,3},{3,2},{4,5},{5,4},{6,7},{7,6},{8,9},{9,8},{10,11... | collective-permute-start | bytes 1572872 | tf_op jit(solution)/shard_map/ppermute | solution.py:45
  68.8 1.8 %collective-permute-done.3 = f32[32,16,256]{2,1,0:T(8,128)S(1)} collective-permute-done((f32[32,16,256]{2,1,0:T(8,128)S(1)}, f32[32,16,256]{2,1,0:T(8,128)S(1)}, u32[]{:S(2)}, u32[]{:S(2)}) %collective-permute-start.3) | collective-permute-done | bytes 524320 | tf_op jit(solution)/shard_map/ppermute | solution.py:45
  70.5 0.1 fusion.1
  70.7 26.2 %all_to_all.11 = f32[32,16,256]{2,1,0:T(8,128)S(1)} all-to-all(f32[32,16,256]{2,1,0:T(8,128)S(1)} %fusion.1), channel_id=1, replica_groups=mesh['band'=8,'y'=8,'zh'=4,'core'=2] {'y','zh'}, dimensions={0} | all-to-all | bytes 1048576 | tf_op jit(solution)/shard_map/all_to_all | solution.py:65
  96.8 0.6 reduce_sum.9
  (3 shorter events, 0.0 us)
Async XLA Ops:
  0.0 56.9 %copy-start = (s32[256,2]{0,1:T(2,128)S(1)}, s32[256,2]{0,1:T(2,128)}, u32[]{:S(2)}) copy-start(s32[256,2]{0,1:T(2,128)} %param.7) | copy-start | bytes 6148
  0.0 56.9 %copy-start.1 = (s32[256]{0:T(256)S(1)}, s32[256]{0:T(256)}, u32[]{:S(2)}) copy-start(s32[256]{0:T(256)} %param.6) | copy-start | bytes 3076
  0.7 6.7 %collective-permute-start = (bf16[32,128]{1,0:T(8,128)(2,1)S(1)}, bf16[32,128]{1,0:T(8,128)(2,1)S(1)}, u32[]{:S(2)}, u32[]{:S(2)}) collective-permute-start(bf16[32,128]{1,0:T(8,128)(2,1)S(1)} %get-tuple-element.9), channel_id=1, source_target_pairs={{0,64},{64,128},{128,192},{192,256},{256,320},{320,384},{384,448},... | collective-permute-start | bytes 24584 | tf_op jit(solution)/shard_map/ppermute | solution.py:19
  5.0 5.5 %collective-permute-start.1 = (bf16[32,128]{1,0:T(8,128)(2,1)S(1)}, bf16[32,128]{1,0:T(8,128)(2,1)S(1)}, u32[]{:S(2)}, u32[]{:S(2)}) collective-permute-start(bf16[32,128]{1,0:T(8,128)(2,1)S(1)} %get-tuple-element.10), channel_id=1, source_target_pairs={{64,0},{128,64},{192,128},{256,192},{320,256},{384,320},{448,384},... | collective-permute-start | bytes 24584 | tf_op jit(solution)/shard_map/ppermute | solution.py:21
  54.9 4.5 %collective-permute-start.2 = (bf16[32,32,512]{2,1,0:T(8,128)(2,1)S(1)}, bf16[32,32,512]{2,1,0:T(8,128)(2,1)S(1)}, u32[]{:S(2)}, u32[]{:S(2)}) collective-permute-start(bf16[32,32,512]{2,1,0:T(8,128)(2,1)S(1)} %all_to_all.10), channel_id=1, source_target_pairs={{0,1},{1,0},{2,3},{3,2},{4,5},{5,4},{6,7},{7,6},{8,9},{9,8},{10,11... | collective-permute-start | bytes 3145736 | tf_op jit(solution)/shard_map/ppermute | solution.py:45
  66.7 3.8 %collective-permute-start.3 = (f32[32,16,256]{2,1,0:T(8,128)S(1)}, f32[32,16,256]{2,1,0:T(8,128)S(1)}, u32[]{:S(2)}, u32[]{:S(2)}) collective-permute-start(f32[32,16,256]{2,1,0:T(8,128)S(1)} %select_bitcast_fusion.2), channel_id=1, source_target_pairs={{0,1},{1,0},{2,3},{3,2},{4,5},{5,4},{6,7},{7,6},{8,9},{9,8},{10,11... | collective-permute-start | bytes 1572872 | tf_op jit(solution)/shard_map/ppermute | solution.py:45

commit v4 on v3

--- a/solution.py
+++ b/solution.py
@@ -45,7 +45,7 @@
     return lax.ppermute(x, "core", [(0, 1), (1, 0)])
 
 
-def gather_history(x):
+def gather_own(x):
     chips = lax.axis_size("y") * lax.axis_size("zh")
     spread = jnp.broadcast_to(x[None], (chips,) + x.shape)
     mine = lax.all_to_all(spread, ("y", "zh"), 0, 0, tiled=True)
@@ -53,6 +53,16 @@
     first = lax.axis_index("core") == 0
     pair = jnp.stack([jnp.where(first, mine, other), jnp.where(first, other, mine)], 1)
     return pair.reshape(-1, x.shape[1])
+
+
+def halo_columns(cells, width):
+    count = lax.axis_size("band")
+    ends = count - 1
+    head = cells[:, :width]
+    tail = cells[:, cells.shape[1] - width :]
+    below = lax.ppermute(tail, "band", [(i, (i + 1) % count) for i in range(ends)])
+    above = lax.ppermute(head, "band", [((i + 1) % count, i) for i in range(ends)])
+    return jnp.concatenate([below, above], axis=1)
 
 
 def reduce_scatter(partial, n_tm):
@@ -74,15 +84,19 @@
 ROW_TILE = 256
 
 
-def conv_kernel(x_ref, w_ref, m_ref, o_ref, wm_ref):
+def conv_kernel(xo_ref, xh_ref, w_ref, m_ref, o_ref, wo_ref, wh_ref):
     taps, coupled, ports = w_ref.shape
     half = (coupled - ports) // 2
     for k in range(taps):
         marks = m_ref[k]
-        for lo, hi, row in ((0, half, 0), (half, half + ports, 1), (half + ports, coupled, 2)):
+        for lo, hi, row, dst, at in (
+            (0, half, 0, wh_ref, 0),
+            (half, half + ports, 1, wo_ref, 0),
+            (half + ports, coupled, 2, wh_ref, half),
+        ):
             keep = marks[row : row + 1, :] != 0
             block = w_ref[k, lo:hi, :]
-            wm_ref[k, lo:hi, :] = jnp.where(keep, block, jnp.zeros_like(block))
+            dst[k, at : at + hi - lo, :] = jnp.where(keep, block, jnp.zeros_like(block))
     rows = o_ref.shape[0]
     for r in range(rows // ROW_TILE):
         start = r * ROW_TILE
@@ -90,29 +104,37 @@
         for k in range(taps):
             shift = taps - k
             acc = acc + jnp.dot(
-                x_ref[start + shift : start + shift + ROW_TILE, :],
-                wm_ref[k],
+                xo_ref[start + shift : start + shift + ROW_TILE, :],
+                wo_ref[k],
+                preferred_element_type=jnp.float32,
+            )
+            acc = acc + jnp.dot(
+                xh_ref[start + shift : start + shift + ROW_TILE, :],
+                wh_ref[k],
                 preferred_element_type=jnp.float32,
             )
         o_ref[start : start + ROW_TILE, :] = acc
 
 
-def masked_conv(window, responses, marks, rows):
+def masked_conv(own, halo, responses, marks, rows):
     taps, coupled, ports = responses.shape
     vmem = pl.BlockSpec(memory_space=pltpu.VMEM)
     return pl.pallas_call(
         conv_kernel,
         out_shape=jax.ShapeDtypeStruct((rows, ports), jnp.float32),
-        in_specs=[vmem, vmem, vmem],
+        in_specs=[vmem, vmem, vmem, vmem],
         out_specs=vmem,
-        scratch_shapes=[pltpu.VMEM((taps, coupled, ports), responses.dtype)],
+        scratch_shapes=[
+            pltpu.VMEM((taps, ports, ports), responses.dtype),
+            pltpu.VMEM((taps, coupled - ports, ports), responses.dtype),
+        ],
         compiler_params=pltpu.CompilerParams(vmem_limit_bytes=48 * 1024 * 1024),
         cost_estimate=pl.CostEstimate(
             flops=2 * rows * taps * coupled * ports,
             transcendentals=0,
-            bytes_accessed=window.size * 2 + responses.size * 2 + rows * ports * 4,
+            bytes_accessed=(own.size + halo.size) * 2 + responses.size * 2 + rows * ports * 4,
         ),
-    )(window, responses, marks)
+    )(own, halo, responses, marks)
 
 
 def tap_marks(tap_counts, panel_links, first_tap, taps):
@@ -133,11 +155,13 @@
     window_len = driven_wave.shape[0] * n_tm - total_taps
     me = tm_index()
     first_tap = me * tap_dev
-    history = gather_history(extended(driven_wave, half_width))
+    halo = lax.all_gather(halo_columns(driven_wave, half_width), TM, axis=0, tiled=True)
+    own = gather_own(driven_wave)
     base = total_taps - first_tap - tap_dev
-    window = lax.dynamic_slice_in_dim(history, base, window_len + tap_dev, 0)
+    own_window = lax.dynamic_slice_in_dim(own, base, window_len + tap_dev, 0)
+    halo_window = lax.dynamic_slice_in_dim(halo, base, window_len + tap_dev, 0)
     marks = tap_marks(tap_counts, panel_links, first_tap, tap_dev)
-    partial = masked_conv(window, responses, marks, window_len)
+    partial = masked_conv(own_window, halo_window, responses, marks, window_len)
     summed = reduce_scatter(partial, n_tm)
     return summed.astype(jnp.bfloat16)
 

time: 97.9 us -> 170 us (1.74)
  waiting for transfers between devices: 7.16 us -> 86.7 us
  blocking collectives: 69.7 us -> 29.2 us
  starting transfers between devices: 10.7 us -> 26.1 us
  between operations: 0.15 us -> 13.5 us
  local copies, waits for them, and re-layouts: 0.94 us -> 3.43 us
    all_gather x0 -> x1, waiting for transfers between devices: none -> 72.7 us  [per_device(): lax.all_gather(halo_columns(driven_wave, half_width), TM, axis=0, tiled=T...]
    all_to_all x1 -> x0, blocking collectives: 43.5 us -> none  [gather_history(): mine = lax.all_to_all(spread, ('y', 'zh'), 0, 0, tiled=True)]
    all_to_all x0 -> x1, starting transfers between devices: none -> 16.2 us  [gather_own(): mine = lax.all_to_all(spread, ('y', 'zh'), 0, 0, tiled=True)]
    all_to_all x0 -> x1, waiting for transfers between devices: none -> 6.81 us  [gather_own(): mine = lax.all_to_all(spread, ('y', 'zh'), 0, 0, tiled=True)]
    all_to_all x1, blocking collectives: 26.2 us -> 29.2 us  [reduce_scatter(): return lax.all_to_all(combined, ('y', 'zh'), 0, 0, tiled=True).sum(0)]
  transfers between devices with their start and end apart: 4 -> 6, of which waited for: 3 -> 5; matrix products, arithmetic and copies ran while one was open for 0% -> 2% of each run, Pallas kernels for 0% -> 0%
where the time goes in v4:
time: 170 us; the launch traced here: 169 us
  waiting for transfers between devices  86.7 us (51%)
  blocking collectives  29.2 us (17%)
  starting transfers between devices  26.1 us (15%)
  between operations  13.5 us (8%)
  Pallas kernels  6.68 us (4%)
  local copies, waits for them, and re-layouts  3.43 us (2%)
  other arithmetic  3.31 us (2%)
    all_gather x1, waiting for transfers between devices, per_device(): lax.all_gather(halo_columns(driven_wave, half_width), TM, axis=0, tiled=T...  72.7 us
    all_to_all x1, blocking collectives, reduce_scatter(): return lax.all_to_all(combined, ('y', 'zh'), 0, 0, tiled=True).sum(0)  29.2 us
    all_to_all x1, starting transfers between devices, gather_own(): mine = lax.all_to_all(spread, ('y', 'zh'), 0, 0, tiled=True)  16.2 us
    all_to_all x1, waiting for transfers between devices, gather_own(): mine = lax.all_to_all(spread, ('y', 'zh'), 0, 0, tiled=True)  6.81 us
    pallas_call x1, Pallas kernels, masked_conv(): pl.pallas_call(conv_kernel, out_shape=jax.ShapeDtypeStruct((rows, ports),...  6.68 us
    ppermute x1, waiting for transfers between devices, halo_columns(): lax.ppermute(tail, 'band', [(i, (i + 1) % count) for i in range(ends)])  4.59 us
    ppermute x2, starting transfers between devices, swap_core(): return lax.ppermute(x, 'core', [(0, 1), (1, 0)])  4.08 us
    ppermute x1, starting transfers between devices, halo_columns(): lax.ppermute(head, 'band', [((i + 1) % count, i) for i in range(ends)])  3.63 us
  transfers between devices with their start and end apart: 6, of which 5 were waited for; matrix products, arithmetic and copies ran while one was open for 2% of the time, Pallas kernels for 0%

profile of v4, /device:TPU:14, one launch (start us, length us, event | category | flops | bytes accessed | tf_op | source)
XLA Modules:
  0.0 169.0 jit_solution(16203345461491871529)
XLA Ops:
  6.5 1.6 broadcast_in_dim.2
  8.1 16.2 %all-to-all-start = ((bf16[32,32,256]{2,1,0:T(8,128)(2,1)}), bf16[32,32,256]{2,1,0:T(8,128)(2,1)S(1)}, u32[]{:S(2)}, u32[]{:S(2)}) async-start(bf16[32,32,256]{2,1,0:T(8,128)(2,1)} %broadcast_in_dim.2), calls=%async_computation | async-start | bytes 1048576 | tf_op jit(solution)/shard_map/all_to_all | solution.py:51
  24.3 0.0 all-gather.2.cloned.1.call-start
  24.3 0.7 fusion.2
  25.1 3.6 %collective-permute-start.2 = (bf16[32,128]{1,0:T(8,128)(2,1)S(1)}, bf16[32,128]{1,0:T(8,128)(2,1)S(1)}, u32[]{:S(2)}, u32[]{:S(2)}) collective-permute-start(bf16[32,128]{1,0:T(8,128)(2,1)S(1)} %get-tuple-element.10), channel_id=1, source_target_pairs={{64,0},{128,64},{192,128},{256,192},{320,256},{384,320},{448,384},... | collective-permute-start | bytes 24584 | tf_op jit(solution)/shard_map/ppermute | solution.py:64
  28.7 2.2 %collective-permute-start.1 = (bf16[32,128]{1,0:T(8,128)(2,1)S(1)}, bf16[32,128]{1,0:T(8,128)(2,1)S(1)}, u32[]{:S(2)}, u32[]{:S(2)}) collective-permute-start(bf16[32,128]{1,0:T(8,128)(2,1)S(1)} %get-tuple-element.9), channel_id=1, source_target_pairs={{0,64},{64,128},{128,192},{192,256},{256,320},{320,384},{384,448},... | collective-permute-start | bytes 24584 | tf_op jit(solution)/shard_map/ppermute | solution.py:63
  30.9 0.0 collective-permute-done.2
  30.9 4.6 %collective-permute-done.1 = bf16[32,128]{1,0:T(8,128)(2,1)S(1)} collective-permute-done((bf16[32,128]{1,0:T(8,128)(2,1)S(1)}, bf16[32,128]{1,0:T(8,128)(2,1)S(1)}, u32[]{:S(2)}, u32[]{:S(2)}) %collective-permute-start.1) | collective-permute-done | bytes 8224 | tf_op jit(solution)/shard_map/ppermute | solution.py:63
  35.5 0.6 pad_maximum_fusion.1
  36.1 0.0 all-gather.2.cloned.1.call-update
  36.1 0.8 compare_reduce_fusion.1
  36.9 6.8 %all-to-all-done = bf16[32,32,256]{2,1,0:T(8,128)(2,1)S(1)} async-done(((bf16[32,32,256]{2,1,0:T(8,128)(2,1)}), bf16[32,32,256]{2,1,0:T(8,128)(2,1)S(1)}, u32[]{:S(2)}, u32[]{:S(2)}) %all-to-all-start) | async-done | bytes 524320 | tf_op jit(solution)/shard_map/all_to_all | solution.py:51
  43.7 1.9 %collective-permute-start = (bf16[32,32,256]{2,1,0:T(8,128)(2,1)S(1)}, bf16[32,32,256]{2,1,0:T(8,128)(2,1)S(1)}, u32[]{:S(2)}, u32[]{:S(2)}) collective-permute-start(bf16[32,32,256]{2,1,0:T(8,128)(2,1)S(1)} %all-to-all-done), channel_id=1, source_target_pairs={{0,1},{1,0},{2,3},{3,2},{4,5},{5,4},{6,7},{7,6},{8,9},{9,8},{10,11... | collective-permute-start | bytes 1572872 | tf_op jit(solution)/shard_map/ppermute | solution.py:45
  45.7 0.8 broadcast_and_fusion.1
  46.5 0.1 pad_add_fusion
  46.6 1.0 collective-permute-done
  47.5 0.1 select_bitcast_fusion.2
  47.6 0.1 pad_maximum_fusion
  47.8 72.7 %all-gather.2.cloned.1.call-done = bf16[2048,256]{1,0:T(8,128)(2,1)} async-done(((bf16[32,256]{1,0:T(8,128)(2,1)}), bf16[2048,256]{1,0:T(8,128)(2,1)}) %all-gather.2.cloned.1.call-update) | async-done | bytes 1048592 | tf_op jit(solution)/shard_map/all_gather | solution.py:158
  120.5 1.1 constant_dynamic-slice_fusion.xh_ref
  121.6 6.7 %shard_map.46 = f32[1024,256]{1,0:T(8,128)S(1)} custom-call(bf16[1040,256]{1,0:T(8,128)(2,1)S(1)} %constant_dynamic-slice_fusion.1.xo_ref, bf16[1040,256]{1,0:T(8,128)(2,1)S(1)} %constant_dynamic-slice_fusion.xh_ref, bf16[16,512,256]{2,1,0:T(8,128)(2,1)} %w_ref.1, s32[16,8,256]{2,1,0:T(8,128)S(1)} %pad_convert_fusion.m_ref), custom_call_target="tpu_custom_call" | custom-call | flops 4294967296 | bytes 6307840 | tf_op jit(solution)/shard_map/pallas_call | solution.py:122
  128.3 0.1 select_bitcast_fusion
  128.3 2.2 %collective-permute-start.3 = (f32[32,16,256]{2,1,0:T(8,128)S(1)}, f32[32,16,256]{2,1,0:T(8,128)S(1)}, u32[]{:S(2)}, u32[]{:S(2)}) collective-permute-start(f32[32,16,256]{2,1,0:T(8,128)S(1)} %select_bitcast_fusion), channel_id=1, source_target_pairs={{0,1},{1,0},{2,3},{3,2},{4,5},{5,4},{6,7},{7,6},{8,9},{9,8},{10,11... | collective-permute-start | bytes 1572872 | tf_op jit(solution)/shard_map/ppermute | solution.py:45
  130.5 1.6 collective-permute-done.3
  132.2 0.1 fusion.1
  132.3 29.2 %all_to_all.10 = f32[32,16,256]{2,1,0:T(8,128)S(1)} all-to-all(f32[32,16,256]{2,1,0:T(8,128)S(1)} %fusion.1), channel_id=1, replica_groups=mesh['band'=8,'y'=8,'zh'=4,'core'=2] {'y','zh'}, dimensions={0} | all-to-all | bytes 1048576 | tf_op jit(solution)/shard_map/all_to_all | solution.py:75
  161.5 0.6 reduce_sum.9
  (3 shorter events, 0.1 us)
Async XLA Ops:
  8.1 35.6 %all-to-all-start = ((bf16[32,32,256]{2,1,0:T(8,128)(2,1)}), bf16[32,32,256]{2,1,0:T(8,128)(2,1)S(1)}, u32[]{:S(2)}, u32[]{:S(2)}) async-start(bf16[32,32,256]{2,1,0:T(8,128)(2,1)} %broadcast_in_dim.2), calls=%async_computation | async-start | bytes 1048576 | tf_op jit(solution)/shard_map/all_to_all | solution.py:51
  24.3 96.2 %all-gather.2.cloned.1.call-start = ((), (), s32[]{:S(2)}) async-start(), calls=%async_computation.2 | async-start | bytes 1064960 | tf_op jit(solution)/shard_map/all_gather | solution.py:158
  25.1 5.8 %collective-permute-start.2 = (bf16[32,128]{1,0:T(8,128)(2,1)S(1)}, bf16[32,128]{1,0:T(8,128)(2,1)S(1)}, u32[]{:S(2)}, u32[]{:S(2)}) collective-permute-start(bf16[32,128]{1,0:T(8,128)(2,1)S(1)} %get-tuple-element.10), channel_id=1, source_target_pairs={{64,0},{128,64},{192,128},{256,192},{320,256},{384,320},{448,384},... | collective-permute-start | bytes 24584 | tf_op jit(solution)/shard_map/ppermute | solution.py:64
  28.7 6.8 %collective-permute-start.1 = (bf16[32,128]{1,0:T(8,128)(2,1)S(1)}, bf16[32,128]{1,0:T(8,128)(2,1)S(1)}, u32[]{:S(2)}, u32[]{:S(2)}) collective-permute-start(bf16[32,128]{1,0:T(8,128)(2,1)S(1)} %get-tuple-element.9), channel_id=1, source_target_pairs={{0,64},{64,128},{128,192},{192,256},{256,320},{320,384},{384,448},... | collective-permute-start | bytes 24584 | tf_op jit(solution)/shard_map/ppermute | solution.py:63
  43.7 3.8 %collective-permute-start = (bf16[32,32,256]{2,1,0:T(8,128)(2,1)S(1)}, bf16[32,32,256]{2,1,0:T(8,128)(2,1)S(1)}, u32[]{:S(2)}, u32[]{:S(2)}) collective-permute-start(bf16[32,32,256]{2,1,0:T(8,128)(2,1)S(1)} %all-to-all-done), channel_id=1, source_target_pairs={{0,1},{1,0},{2,3},{3,2},{4,5},{5,4},{6,7},{7,6},{8,9},{9,8},{10,11... | collective-permute-start | bytes 1572872 | tf_op jit(solution)/shard_map/ppermute | solution.py:45
  128.3 3.8 %collective-permute-start.3 = (f32[32,16,256]{2,1,0:T(8,128)S(1)}, f32[32,16,256]{2,1,0:T(8,128)S(1)}, u32[]{:S(2)}, u32[]{:S(2)}) collective-permute-start(f32[32,16,256]{2,1,0:T(8,128)S(1)} %select_bitcast_fusion), channel_id=1, source_target_pairs={{0,1},{1,0},{2,3},{3,2},{4,5},{5,4},{6,7},{7,6},{8,9},{9,8},{10,11... | collective-permute-start | bytes 1572872 | tf_op jit(solution)/shard_map/ppermute | solution.py:45
Sparse Core Ops, SparseCore 0:
  36.3 84.1 all-gather.1

commit v5 on v4

--- a/solution.py
+++ b/solution.py
@@ -155,8 +155,8 @@
     window_len = driven_wave.shape[0] * n_tm - total_taps
     me = tm_index()
     first_tap = me * tap_dev
-    halo = lax.all_gather(halo_columns(driven_wave, half_width), TM, axis=0, tiled=True)
     own = gather_own(driven_wave)
+    halo = gather_own(halo_columns(driven_wave, half_width))
     base = total_taps - first_tap - tap_dev
     own_window = lax.dynamic_slice_in_dim(own, base, window_len + tap_dev, 0)
     halo_window = lax.dynamic_slice_in_dim(halo, base, window_len + tap_dev, 0)

time: 170 us -> 104 us (0.61)
  the two profiles are of different devices: /device:TPU:14 before, /device:TPU:10 now
where the time goes in v5:
time: 104 us; the launch traced here: 103 us
  starting transfers between devices  34.4 us (33%)
  waiting for transfers between devices  31.3 us (30%)
  blocking collectives  24.6 us (24%)
  Pallas kernels  6.69 us (6%)
  local copies, waits for them, and re-layouts  3.31 us (3%)
  other arithmetic  2.89 us (3%)
    all_to_all x1, blocking collectives, reduce_scatter(): return lax.all_to_all(combined, ('y', 'zh'), 0, 0, tiled=True).sum(0)  24.6 us
    all_to_all x2, waiting for transfers between devices, gather_own(): mine = lax.all_to_all(spread, ('y', 'zh'), 0, 0, tiled=True)  24.4 us
    all_to_all x2, starting transfers between devices, gather_own(): mine = lax.all_to_all(spread, ('y', 'zh'), 0, 0, tiled=True)  21.8 us
    pallas_call x1, Pallas kernels, masked_conv(): pl.pallas_call(conv_kernel, out_shape=jax.ShapeDtypeStruct((rows, ports),...  6.69 us
    ppermute x3, starting transfers between devices, swap_core(): return lax.ppermute(x, 'core', [(0, 1), (1, 0)])  5.88 us
    ppermute x1, starting transfers between devices, halo_columns(): lax.ppermute(tail, 'band', [(i, (i + 1) % count) for i in range(ends)])  3.37 us
    ppermute x1, starting transfers between devices, halo_columns(): lax.ppermute(head, 'band', [((i + 1) % count, i) for i in range(ends)])  3.36 us
    ppermute x1, waiting for transfers between devices, halo_columns(): lax.ppermute(tail, 'band', [(i, (i + 1) % count) for i in range(ends)])  3.35 us
  transfers between devices with their start and end apart: 7, of which 6 were waited for; matrix products, arithmetic and copies ran while one was open for 3% of the time, Pallas kernels for 0%

profile of v5, /device:TPU:10, one launch (start us, length us, event | category | flops | bytes accessed | tf_op | source)
XLA Modules:
  0.0 103.3 jit_solution(5006170847293188001)
XLA Ops:
  0.0 1.6 %broadcast_in_dim.4 = bf16[32,32,256]{2,1,0:T(8,128)(2,1)} broadcast(bf16[32,256]{1,0:T(8,128)(2,1)} %param.4), dimensions={1,2} | broadcast | bytes 540672 | tf_op jit(solution)/shard_map/broadcast_in_dim | solution.py:50
  1.6 16.2 %all-to-all-start = ((bf16[32,32,256]{2,1,0:T(8,128)(2,1)}), bf16[32,32,256]{2,1,0:T(8,128)(2,1)S(1)}, u32[]{:S(2)}, u32[]{:S(2)}) async-start(bf16[32,32,256]{2,1,0:T(8,128)(2,1)} %broadcast_in_dim.4), calls=%async_computation | async-start | bytes 1048576 | tf_op jit(solution)/shard_map/all_to_all | solution.py:51
  17.7 0.7 fusion.2
  18.5 3.4 %collective-permute-start.1 = (bf16[32,128]{1,0:T(8,128)(2,1)S(1)}, bf16[32,128]{1,0:T(8,128)(2,1)S(1)}, u32[]{:S(2)}, u32[]{:S(2)}) collective-permute-start(bf16[32,128]{1,0:T(8,128)(2,1)S(1)} %get-tuple-element.11), channel_id=1, source_target_pairs={{0,64},{64,128},{128,192},{192,256},{256,320},{320,384},{384,448},... | collective-permute-start | bytes 24584 | tf_op jit(solution)/shard_map/ppermute | solution.py:63
  21.8 3.4 %collective-permute-start.2 = (bf16[32,128]{1,0:T(8,128)(2,1)S(1)}, bf16[32,128]{1,0:T(8,128)(2,1)S(1)}, u32[]{:S(2)}, u32[]{:S(2)}) collective-permute-start(bf16[32,128]{1,0:T(8,128)(2,1)S(1)} %get-tuple-element.12), channel_id=1, source_target_pairs={{64,0},{128,64},{192,128},{256,192},{320,256},{384,320},{448,384},... | collective-permute-start | bytes 24584 | tf_op jit(solution)/shard_map/ppermute | solution.py:64
  25.2 3.4 %collective-permute-done.1 = bf16[32,128]{1,0:T(8,128)(2,1)S(1)} collective-permute-done((bf16[32,128]{1,0:T(8,128)(2,1)S(1)}, bf16[32,128]{1,0:T(8,128)(2,1)S(1)}, u32[]{:S(2)}, u32[]{:S(2)}) %collective-permute-start.1) | collective-permute-done | bytes 8224 | tf_op jit(solution)/shard_map/ppermute | solution.py:63
  28.6 0.2 collective-permute-done.2
  28.8 8.4 %all-to-all-done = bf16[32,32,256]{2,1,0:T(8,128)(2,1)S(1)} async-done(((bf16[32,32,256]{2,1,0:T(8,128)(2,1)}), bf16[32,32,256]{2,1,0:T(8,128)(2,1)S(1)}, u32[]{:S(2)}, u32[]{:S(2)}) %all-to-all-start) | async-done | bytes 524320 | tf_op jit(solution)/shard_map/all_to_all | solution.py:51
  37.2 0.9 broadcast_in_dim.5
  38.0 5.6 %all-to-all-start.1 = ((bf16[32,32,256]{2,1,0:T(8,128)(2,1)}), bf16[32,32,256]{2,1,0:T(8,128)(2,1)S(1)}, u32[]{:S(2)}, u32[]{:S(2)}) async-start(bf16[32,32,256]{2,1,0:T(8,128)(2,1)} %broadcast_in_dim.5), calls=%async_computation.1 | async-start | bytes 1048576 | tf_op jit(solution)/shard_map/all_to_all | solution.py:51
  43.7 0.8 compare_reduce_fusion.1
  44.5 1.9 %collective-permute-start = (bf16[32,32,256]{2,1,0:T(8,128)(2,1)S(1)}, bf16[32,32,256]{2,1,0:T(8,128)(2,1)S(1)}, u32[]{:S(2)}, u32[]{:S(2)}) collective-permute-start(bf16[32,32,256]{2,1,0:T(8,128)(2,1)S(1)} %all-to-all-done), channel_id=1, source_target_pairs={{0,1},{1,0},{2,3},{3,2},{4,5},{5,4},{6,7},{7,6},{8,9},{9,8},{10,11... | collective-permute-start | bytes 1572872 | tf_op jit(solution)/shard_map/ppermute | solution.py:45
  46.4 0.8 broadcast_and_fusion.1
  47.2 0.1 pad_add_fusion
  47.3 16.0 %all-to-all-done.1 = bf16[32,32,256]{2,1,0:T(8,128)(2,1)S(1)} async-done(((bf16[32,32,256]{2,1,0:T(8,128)(2,1)}), bf16[32,32,256]{2,1,0:T(8,128)(2,1)S(1)}, u32[]{:S(2)}, u32[]{:S(2)}) %all-to-all-start.1) | async-done | bytes 524320 | tf_op jit(solution)/shard_map/all_to_all | solution.py:51
  63.3 1.9 %collective-permute-start.3 = (bf16[32,32,256]{2,1,0:T(8,128)(2,1)S(1)}, bf16[32,32,256]{2,1,0:T(8,128)(2,1)S(1)}, u32[]{:S(2)}, u32[]{:S(2)}) collective-permute-start(bf16[32,32,256]{2,1,0:T(8,128)(2,1)S(1)} %all-to-all-done.1), channel_id=1, source_target_pairs={{0,1},{1,0},{2,3},{3,2},{4,5},{5,4},{6,7},{7,6},{8,9},{9,8},{10,11... | collective-permute-start | bytes 1572872 | tf_op jit(solution)/shard_map/ppermute | solution.py:45
  65.2 0.0 collective-permute-done
  65.2 0.1 select_bitcast_fusion.4
  65.3 0.1 pad_maximum_fusion
  65.4 0.1 copy.11
  65.5 1.6 %collective-permute-done.3 = bf16[32,32,256]{2,1,0:T(8,128)(2,1)S(1)} collective-permute-done((bf16[32,32,256]{2,1,0:T(8,128)(2,1)S(1)}, bf16[32,32,256]{2,1,0:T(8,128)(2,1)S(1)}, u32[]{:S(2)}, u32[]{:S(2)}) %collective-permute-start.3) | collective-permute-done | bytes 524320 | tf_op jit(solution)/shard_map/ppermute | solution.py:45
  67.1 0.1 select_bitcast_fusion.2
  67.1 0.1 pad_maximum_fusion.1
  67.2 0.1 constant_dynamic-slice_fusion
  67.3 6.7 %shard_map.46 = f32[1024,256]{1,0:T(8,128)S(1)} custom-call(bf16[1040,256]{1,0:T(8,128)(2,1)S(1)} %get-tuple-element.17.xo_ref, bf16[1040,256]{1,0:T(8,128)(2,1)S(1)} %get-tuple-element.16.xh_ref, bf16[16,512,256]{2,1,0:T(8,128)(2,1)} %w_ref.1, s32[16,8,256]{2,1,0:T(8,128)S(1)} %pad_convert_fusion.m_ref), custom_call_target="tpu_custom_call" | custom-call | flops 4294967296 | bytes 6307840 | tf_op jit(solution)/shard_map/pallas_call | solution.py:122
  74.0 0.1 select_bitcast_fusion
  74.1 2.0 %collective-permute-start.4 = (f32[32,16,256]{2,1,0:T(8,128)S(1)}, f32[32,16,256]{2,1,0:T(8,128)S(1)}, u32[]{:S(2)}, u32[]{:S(2)}) collective-permute-start(f32[32,16,256]{2,1,0:T(8,128)S(1)} %select_bitcast_fusion), channel_id=1, source_target_pairs={{0,1},{1,0},{2,3},{3,2},{4,5},{5,4},{6,7},{7,6},{8,9},{9,8},{10,11... | collective-permute-start | bytes 1572872 | tf_op jit(solution)/shard_map/ppermute | solution.py:45
  76.2 1.7 %collective-permute-done.4 = f32[32,16,256]{2,1,0:T(8,128)S(1)} collective-permute-done((f32[32,16,256]{2,1,0:T(8,128)S(1)}, f32[32,16,256]{2,1,0:T(8,128)S(1)}, u32[]{:S(2)}, u32[]{:S(2)}) %collective-permute-start.4) | collective-permute-done | bytes 524320 | tf_op jit(solution)/shard_map/ppermute | solution.py:45
  77.9 0.1 fusion.1
  78.1 24.6 %all_to_all.15 = f32[32,16,256]{2,1,0:T(8,128)S(1)} all-to-all(f32[32,16,256]{2,1,0:T(8,128)S(1)} %fusion.1), channel_id=1, replica_groups=mesh['band'=8,'y'=8,'zh'=4,'core'=2] {'y','zh'}, dimensions={0} | all-to-all | bytes 1048576 | tf_op jit(solution)/shard_map/all_to_all | solution.py:75
  102.6 0.6 reduce_sum.9
  (3 shorter events, 0.0 us)
Async XLA Ops:
  1.6 35.6 %all-to-all-start = ((bf16[32,32,256]{2,1,0:T(8,128)(2,1)}), bf16[32,32,256]{2,1,0:T(8,128)(2,1)S(1)}, u32[]{:S(2)}, u32[]{:S(2)}) async-start(bf16[32,32,256]{2,1,0:T(8,128)(2,1)} %broadcast_in_dim.4), calls=%async_computation | async-start | bytes 1048576 | tf_op jit(solution)/shard_map/all_to_all | solution.py:51
  18.5 10.1 %collective-permute-start.1 = (bf16[32,128]{1,0:T(8,128)(2,1)S(1)}, bf16[32,128]{1,0:T(8,128)(2,1)S(1)}, u32[]{:S(2)}, u32[]{:S(2)}) collective-permute-start(bf16[32,128]{1,0:T(8,128)(2,1)S(1)} %get-tuple-element.11), channel_id=1, source_target_pairs={{0,64},{64,128},{128,192},{192,256},{256,320},{320,384},{384,448},... | collective-permute-start | bytes 24584 | tf_op jit(solution)/shard_map/ppermute | solution.py:63
  21.8 7.0 %collective-permute-start.2 = (bf16[32,128]{1,0:T(8,128)(2,1)S(1)}, bf16[32,128]{1,0:T(8,128)(2,1)S(1)}, u32[]{:S(2)}, u32[]{:S(2)}) collective-permute-start(bf16[32,128]{1,0:T(8,128)(2,1)S(1)} %get-tuple-element.12), channel_id=1, source_target_pairs={{64,0},{128,64},{192,128},{256,192},{320,256},{384,320},{448,384},... | collective-permute-start | bytes 24584 | tf_op jit(solution)/shard_map/ppermute | solution.py:64
  38.0 25.2 %all-to-all-start.1 = ((bf16[32,32,256]{2,1,0:T(8,128)(2,1)}), bf16[32,32,256]{2,1,0:T(8,128)(2,1)S(1)}, u32[]{:S(2)}, u32[]{:S(2)}) async-start(bf16[32,32,256]{2,1,0:T(8,128)(2,1)} %broadcast_in_dim.5), calls=%async_computation.1 | async-start | bytes 1048576 | tf_op jit(solution)/shard_map/all_to_all | solution.py:51
  44.5 20.8 %collective-permute-start = (bf16[32,32,256]{2,1,0:T(8,128)(2,1)S(1)}, bf16[32,32,256]{2,1,0:T(8,128)(2,1)S(1)}, u32[]{:S(2)}, u32[]{:S(2)}) collective-permute-start(bf16[32,32,256]{2,1,0:T(8,128)(2,1)S(1)} %all-to-all-done), channel_id=1, source_target_pairs={{0,1},{1,0},{2,3},{3,2},{4,5},{5,4},{6,7},{7,6},{8,9},{9,8},{10,11... | collective-permute-start | bytes 1572872 | tf_op jit(solution)/shard_map/ppermute | solution.py:45
  63.3 3.8 %collective-permute-start.3 = (bf16[32,32,256]{2,1,0:T(8,128)(2,1)S(1)}, bf16[32,32,256]{2,1,0:T(8,128)(2,1)S(1)}, u32[]{:S(2)}, u32[]{:S(2)}) collective-permute-start(bf16[32,32,256]{2,1,0:T(8,128)(2,1)S(1)} %all-to-all-done.1), channel_id=1, source_target_pairs={{0,1},{1,0},{2,3},{3,2},{4,5},{5,4},{6,7},{7,6},{8,9},{9,8},{10,11... | collective-permute-start | bytes 1572872 | tf_op jit(solution)/shard_map/ppermute | solution.py:45
  74.1 3.8 %collective-permute-start.4 = (f32[32,16,256]{2,1,0:T(8,128)S(1)}, f32[32,16,256]{2,1,0:T(8,128)S(1)}, u32[]{:S(2)}, u32[]{:S(2)}) collective-permute-start(f32[32,16,256]{2,1,0:T(8,128)S(1)} %select_bitcast_fusion), channel_id=1, source_target_pairs={{0,1},{1,0},{2,3},{3,2},{4,5},{5,4},{6,7},{7,6},{8,9},{9,8},{10,11... | collective-permute-start | bytes 1572872 | tf_op jit(solution)/shard_map/ppermute | solution.py:45

commit v6 on v3

--- a/solution.py
+++ b/solution.py
@@ -74,7 +74,7 @@
 ROW_TILE = 256
 
 
-def conv_kernel(x_ref, w_ref, m_ref, o_ref, wm_ref):
+def mask_kernel(w_ref, m_ref, wm_ref):
     taps, coupled, ports = w_ref.shape
     half = (coupled - ports) // 2
     for k in range(taps):
@@ -83,6 +83,24 @@
             keep = marks[row : row + 1, :] != 0
             block = w_ref[k, lo:hi, :]
             wm_ref[k, lo:hi, :] = jnp.where(keep, block, jnp.zeros_like(block))
+
+
+def masked_weights_kernel(responses, marks):
+    vmem = pl.BlockSpec(memory_space=pltpu.VMEM)
+    return pl.pallas_call(
+        mask_kernel,
+        out_shape=jax.ShapeDtypeStruct(responses.shape, responses.dtype),
+        in_specs=[vmem, vmem],
+        out_specs=vmem,
+        compiler_params=pltpu.CompilerParams(vmem_limit_bytes=48 * 1024 * 1024),
+        cost_estimate=pl.CostEstimate(
+            flops=0, transcendentals=0, bytes_accessed=responses.size * 4
+        ),
+    )(responses, marks)
+
+
+def conv_kernel(x_ref, wm_ref, o_ref):
+    taps, coupled, ports = wm_ref.shape
     rows = o_ref.shape[0]
     for r in range(rows // ROW_TILE):
         start = r * ROW_TILE
@@ -99,20 +117,20 @@
 
 def masked_conv(window, responses, marks, rows):
     taps, coupled, ports = responses.shape
+    weights = masked_weights_kernel(responses, marks)
     vmem = pl.BlockSpec(memory_space=pltpu.VMEM)
     return pl.pallas_call(
         conv_kernel,
         out_shape=jax.ShapeDtypeStruct((rows, ports), jnp.float32),
-        in_specs=[vmem, vmem, vmem],
+        in_specs=[vmem, vmem],
         out_specs=vmem,
-        scratch_shapes=[pltpu.VMEM((taps, coupled, ports), responses.dtype)],
         compiler_params=pltpu.CompilerParams(vmem_limit_bytes=48 * 1024 * 1024),
         cost_estimate=pl.CostEstimate(
             flops=2 * rows * taps * coupled * ports,
             transcendentals=0,
             bytes_accessed=window.size * 2 + responses.size * 2 + rows * ports * 4,
         ),
-    )(window, responses, marks)
+    )(window, weights)
 
 
 def tap_marks(tap_counts, panel_links, first_tap, taps):

time: 97.9 us -> 100 us (1.021)
  waiting for transfers between devices: 7.16 us -> 4.59 us
  Pallas kernels: 6.7 us -> 9.21 us
  local copies, waits for them, and re-layouts: 0.94 us -> 2.7 us
    ppermute x2, waiting for transfers between devices: 4.09 us -> 1.52 us  [swap_core(): return lax.ppermute(x, 'core', [(0, 1), (1, 0)])]
    pallas_call x0 -> x1, Pallas kernels: none -> 2.52 us  [masked_weights_kernel(): pl.pallas_call(mask_kernel, out_shape=jax.ShapeDtypeStruct(responses.shap...]
    unnamed x4 -> x6, local copies, waits for them, and re-layouts: 0.01 us -> 1.77 us
  transfers between devices with their start and end apart: 4 -> 4, of which waited for: 3 -> 2; matrix products, arithmetic and copies ran while one was open for 0% -> 0% of each run, Pallas kernels for 0% -> 3%
where the time goes in v6:
time: 100 us; the launch traced here: 99.8 us
  blocking collectives  69.9 us (70%)
  starting transfers between devices  11 us (11%)
  Pallas kernels  9.21 us (9%)
  waiting for transfers between devices  4.59 us (5%)
  local copies, waits for them, and re-layouts  2.7 us (3%)
  other arithmetic  2.17 us (2%)
    all_to_all x1, blocking collectives, gather_history(): mine = lax.all_to_all(spread, ('y', 'zh'), 0, 0, tiled=True)  43.5 us
    all_to_all x1, blocking collectives, reduce_scatter(): return lax.all_to_all(combined, ('y', 'zh'), 0, 0, tiled=True).sum(0)  26.4 us
    pallas_call x1, Pallas kernels, masked_conv(): pl.pallas_call(conv_kernel, out_shape=jax.ShapeDtypeStruct((rows, ports),...  6.69 us
    ppermute x2, starting transfers between devices, swap_core(): return lax.ppermute(x, 'core', [(0, 1), (1, 0)])  4.31 us
    ppermute x1, starting transfers between devices, extended(): lax.ppermute(tail, 'band', [(i, (i + 1) % count) for i in range(ends)])  4.27 us
    ppermute x1, waiting for transfers between devices, extended(): lax.ppermute(head, 'band', [((i + 1) % count, i) for i in range(ends)])  3.07 us
    pallas_call x1, Pallas kernels, masked_weights_kernel(): pl.pallas_call(mask_kernel, out_shape=jax.ShapeDtypeStruct(responses.shap...  2.52 us
    ppermute x1, starting transfers between devices, extended(): lax.ppermute(head, 'band', [((i + 1) % count, i) for i in range(ends)])  2.46 us
  transfers between devices with their start and end apart: 4, of which 2 were waited for; matrix products, arithmetic and copies ran while one was open for 0% of the time, Pallas kernels for 3%

profile of v6, /device:TPU:14, one launch (start us, length us, event | category | flops | bytes accessed | tf_op | source)
XLA Modules:
  0.0 99.8 jit_solution(7792533685628753693)
XLA Ops:
  0.0 0.0 copy-start.1
  0.0 0.0 copy-start.2
  0.0 0.7 fusion.2
  0.7 4.3 %collective-permute-start = (bf16[32,128]{1,0:T(8,128)(2,1)S(1)}, bf16[32,128]{1,0:T(8,128)(2,1)S(1)}, u32[]{:S(2)}, u32[]{:S(2)}) collective-permute-start(bf16[32,128]{1,0:T(8,128)(2,1)S(1)} %get-tuple-element.9), channel_id=1, source_target_pairs={{0,64},{64,128},{128,192},{192,256},{256,320},{320,384},{384,448},... | collective-permute-start | bytes 24584 | tf_op jit(solution)/shard_map/ppermute | solution.py:19
  5.0 2.5 %collective-permute-start.1 = (bf16[32,128]{1,0:T(8,128)(2,1)S(1)}, bf16[32,128]{1,0:T(8,128)(2,1)S(1)}, u32[]{:S(2)}, u32[]{:S(2)}) collective-permute-start(bf16[32,128]{1,0:T(8,128)(2,1)S(1)} %get-tuple-element.10), channel_id=1, source_target_pairs={{64,0},{128,64},{192,128},{256,192},{320,256},{384,320},{448,384},... | collective-permute-start | bytes 24584 | tf_op jit(solution)/shard_map/ppermute | solution.py:21
  7.5 0.0 collective-permute-done
  7.5 3.1 %collective-permute-done.1 = bf16[32,128]{1,0:T(8,128)(2,1)S(1)} collective-permute-done((bf16[32,128]{1,0:T(8,128)(2,1)S(1)}, bf16[32,128]{1,0:T(8,128)(2,1)S(1)}, u32[]{:S(2)}, u32[]{:S(2)}) %collective-permute-start.1) | collective-permute-done | bytes 8224 | tf_op jit(solution)/shard_map/ppermute | solution.py:21
  10.6 0.7 pad_maximum_fusion.1
  11.3 0.1 broadcast_in_dim.2
  11.4 43.5 %all_to_all.10 = bf16[32,32,512]{2,1,0:T(8,128)(2,1)S(1)} all-to-all(bf16[32,32,512]{2,1,0:T(8,128)(2,1)S(1)} %broadcast_in_dim.2), channel_id=1, replica_groups=mesh['band'=8,'y'=8,'zh'=4,'core'=2] {'y','zh'}, dimensions={0} | all-to-all | bytes 2097152 | tf_op jit(solution)/shard_map/all_to_all | solution.py:51
  54.9 1.9 %collective-permute-start.2 = (bf16[32,32,512]{2,1,0:T(8,128)(2,1)S(1)}, bf16[32,32,512]{2,1,0:T(8,128)(2,1)S(1)}, u32[]{:S(2)}, u32[]{:S(2)}) collective-permute-start(bf16[32,32,512]{2,1,0:T(8,128)(2,1)S(1)} %all_to_all.10), channel_id=1, source_target_pairs={{0,1},{1,0},{2,3},{3,2},{4,5},{5,4},{6,7},{7,6},{8,9},{9,8},{10,11... | collective-permute-start | bytes 3145736 | tf_op jit(solution)/shard_map/ppermute | solution.py:45
  56.9 0.0 copy-done.1
  56.9 0.0 copy-done.2
  56.9 0.1 broadcast_and_fusion.1
  57.0 0.1 pad_add_fusion
  57.1 2.5 %shard_map.46.wm_ref = bf16[16,512,256]{2,1,0:T(8,128)(2,1)S(1)} custom-call(bf16[16,512,256]{2,1,0:T(8,128)(2,1)} %w_ref.1, s32[16,8,256]{2,1,0:T(8,128)S(1)} %pad_convert_fusion.m_ref), custom_call_target="tpu_custom_call" | custom-call | bytes 8388608 | tf_op jit(solution)/shard_map/pallas_call | solution.py:90
  59.6 0.0 copy-start
  59.7 0.0 collective-permute-done.2
  59.7 0.1 select_bitcast_fusion.1
  59.8 1.8 %copy-done = bf16[16,512,256]{2,1,0:T(8,128)(2,1)} copy-done((bf16[16,512,256]{2,1,0:T(8,128)(2,1)}, bf16[16,512,256]{2,1,0:T(8,128)(2,1)S(1)}, u32[]{:S(2)}) %copy-start) | copy-done | bytes 4194328
  61.6 0.2 pad_maximum_fusion
  61.8 0.1 constant_dynamic-slice_fusion.x_ref
  61.9 6.7 %shard_map.47 = f32[1024,256]{1,0:T(8,128)S(1)} custom-call(bf16[1040,512]{1,0:T(8,128)(2,1)S(1)} %constant_dynamic-slice_fusion.x_ref, bf16[16,512,256]{2,1,0:T(8,128)(2,1)} %copy-done), custom_call_target="tpu_custom_call" | custom-call | flops 4294967296 | bytes 6307840 | tf_op jit(solution)/shard_map/pallas_call | solution.py:122
  68.6 0.1 select_bitcast_fusion.2
  68.7 2.4 %collective-permute-start.3 = (f32[32,16,256]{2,1,0:T(8,128)S(1)}, f32[32,16,256]{2,1,0:T(8,128)S(1)}, u32[]{:S(2)}, u32[]{:S(2)}) collective-permute-start(f32[32,16,256]{2,1,0:T(8,128)S(1)} %select_bitcast_fusion.2), channel_id=1, source_target_pairs={{0,1},{1,0},{2,3},{3,2},{4,5},{5,4},{6,7},{7,6},{8,9},{9,8},{10,11... | collective-permute-start | bytes 1572872 | tf_op jit(solution)/shard_map/ppermute | solution.py:45
  71.1 1.5 %collective-permute-done.3 = f32[32,16,256]{2,1,0:T(8,128)S(1)} collective-permute-done((f32[32,16,256]{2,1,0:T(8,128)S(1)}, f32[32,16,256]{2,1,0:T(8,128)S(1)}, u32[]{:S(2)}, u32[]{:S(2)}) %collective-permute-start.3) | collective-permute-done | bytes 524320 | tf_op jit(solution)/shard_map/ppermute | solution.py:45
  72.6 0.1 fusion.1
  72.7 26.4 %all_to_all.11 = f32[32,16,256]{2,1,0:T(8,128)S(1)} all-to-all(f32[32,16,256]{2,1,0:T(8,128)S(1)} %fusion.1), channel_id=1, replica_groups=mesh['band'=8,'y'=8,'zh'=4,'core'=2] {'y','zh'}, dimensions={0} | all-to-all | bytes 1048576 | tf_op jit(solution)/shard_map/all_to_all | solution.py:65
  99.1 0.6 reduce_sum.9
  (3 shorter events, 0.0 us)
Async XLA Ops:
  0.0 56.9 %copy-start.1 = (s32[256,2]{0,1:T(2,128)S(1)}, s32[256,2]{0,1:T(2,128)}, u32[]{:S(2)}) copy-start(s32[256,2]{0,1:T(2,128)} %param.7) | copy-start | bytes 6148
  0.0 56.9 %copy-start.2 = (s32[256]{0:T(256)S(1)}, s32[256]{0:T(256)}, u32[]{:S(2)}) copy-start(s32[256]{0:T(256)} %param.6) | copy-start | bytes 3076
  0.7 6.7 %collective-permute-start = (bf16[32,128]{1,0:T(8,128)(2,1)S(1)}, bf16[32,128]{1,0:T(8,128)(2,1)S(1)}, u32[]{:S(2)}, u32[]{:S(2)}) collective-permute-start(bf16[32,128]{1,0:T(8,128)(2,1)S(1)} %get-tuple-element.9), channel_id=1, source_target_pairs={{0,64},{64,128},{128,192},{192,256},{256,320},{320,384},{384,448},... | collective-permute-start | bytes 24584 | tf_op jit(solution)/shard_map/ppermute | solution.py:19
  5.0 5.5 %collective-permute-start.1 = (bf16[32,128]{1,0:T(8,128)(2,1)S(1)}, bf16[32,128]{1,0:T(8,128)(2,1)S(1)}, u32[]{:S(2)}, u32[]{:S(2)}) collective-permute-start(bf16[32,128]{1,0:T(8,128)(2,1)S(1)} %get-tuple-element.10), channel_id=1, source_target_pairs={{64,0},{128,64},{192,128},{256,192},{320,256},{384,320},{448,384},... | collective-permute-start | bytes 24584 | tf_op jit(solution)/shard_map/ppermute | solution.py:21
  54.9 4.7 %collective-permute-start.2 = (bf16[32,32,512]{2,1,0:T(8,128)(2,1)S(1)}, bf16[32,32,512]{2,1,0:T(8,128)(2,1)S(1)}, u32[]{:S(2)}, u32[]{:S(2)}) collective-permute-start(bf16[32,32,512]{2,1,0:T(8,128)(2,1)S(1)} %all_to_all.10), channel_id=1, source_target_pairs={{0,1},{1,0},{2,3},{3,2},{4,5},{5,4},{6,7},{7,6},{8,9},{9,8},{10,11... | collective-permute-start | bytes 3145736 | tf_op jit(solution)/shard_map/ppermute | solution.py:45
  59.6 1.9 %copy-start = (bf16[16,512,256]{2,1,0:T(8,128)(2,1)}, bf16[16,512,256]{2,1,0:T(8,128)(2,1)S(1)}, u32[]{:S(2)}) copy-start(bf16[16,512,256]{2,1,0:T(8,128)(2,1)S(1)} %shard_map.46.wm_ref) | copy-start | bytes 12582916
  68.7 3.9 %collective-permute-start.3 = (f32[32,16,256]{2,1,0:T(8,128)S(1)}, f32[32,16,256]{2,1,0:T(8,128)S(1)}, u32[]{:S(2)}, u32[]{:S(2)}) collective-permute-start(f32[32,16,256]{2,1,0:T(8,128)S(1)} %select_bitcast_fusion.2), channel_id=1, source_target_pairs={{0,1},{1,0},{2,3},{3,2},{4,5},{5,4},{6,7},{7,6},{8,9},{9,8},{10,11... | collective-permute-start | bytes 1572872 | tf_op jit(solution)/shard_map/ppermute | solution.py:45

commit v7 on v3

--- a/solution.py
+++ b/solution.py
@@ -71,7 +71,7 @@
     ) + lax.axis_index("core")
 
 
-ROW_TILE = 256
+ROW_TILE = 512
 
 
 def conv_kernel(x_ref, w_ref, m_ref, o_ref, wm_ref):

time: 97.9 us -> 97.9 us (level)
  no operation moved by 1% of the time
where the time goes in v7:
time: 97.9 us; the launch traced here: 97.5 us
  blocking collectives  69.7 us (71%)
  starting transfers between devices  10.7 us (11%)
  waiting for transfers between devices  7.16 us (7%)
  Pallas kernels  6.69 us (7%)
  other arithmetic  2.17 us (2%)
    all_to_all x1, blocking collectives, gather_history(): mine = lax.all_to_all(spread, ('y', 'zh'), 0, 0, tiled=True)  43.5 us
    all_to_all x1, blocking collectives, reduce_scatter(): return lax.all_to_all(combined, ('y', 'zh'), 0, 0, tiled=True).sum(0)  26.2 us
    pallas_call x1, Pallas kernels, masked_conv(): pl.pallas_call(conv_kernel, out_shape=jax.ShapeDtypeStruct((rows, ports),...  6.69 us
    ppermute x1, starting transfers between devices, extended(): lax.ppermute(tail, 'band', [(i, (i + 1) % count) for i in range(ends)])  4.27 us
    ppermute x2, waiting for transfers between devices, swap_core(): return lax.ppermute(x, 'core', [(0, 1), (1, 0)])  4.09 us
    ppermute x2, starting transfers between devices, swap_core(): return lax.ppermute(x, 'core', [(0, 1), (1, 0)])  3.95 us
    ppermute x1, waiting for transfers between devices, extended(): lax.ppermute(head, 'band', [((i + 1) % count, i) for i in range(ends)])  3.07 us
    ppermute x1, starting transfers between devices, extended(): lax.ppermute(head, 'band', [((i + 1) % count, i) for i in range(ends)])  2.46 us
  transfers between devices with their start and end apart: 4, of which 3 were waited for; matrix products, arithmetic and copies ran while one was open for 0% of the time, Pallas kernels for 0%

profile of v7, /device:TPU:14, one launch (start us, length us, event | category | flops | bytes accessed | tf_op | source)
XLA Modules:
  0.0 97.5 jit_solution(17569757216780439758)
XLA Ops:
  0.0 0.0 copy-start
  0.0 0.0 copy-start.1
  0.0 0.7 fusion.2
  0.7 4.3 %collective-permute-start = (bf16[32,128]{1,0:T(8,128)(2,1)S(1)}, bf16[32,128]{1,0:T(8,128)(2,1)S(1)}, u32[]{:S(2)}, u32[]{:S(2)}) collective-permute-start(bf16[32,128]{1,0:T(8,128)(2,1)S(1)} %get-tuple-element.9), channel_id=1, source_target_pairs={{0,64},{64,128},{128,192},{192,256},{256,320},{320,384},{384,448},... | collective-permute-start | bytes 24584 | tf_op jit(solution)/shard_map/ppermute | solution.py:19
  5.0 2.5 %collective-permute-start.1 = (bf16[32,128]{1,0:T(8,128)(2,1)S(1)}, bf16[32,128]{1,0:T(8,128)(2,1)S(1)}, u32[]{:S(2)}, u32[]{:S(2)}) collective-permute-start(bf16[32,128]{1,0:T(8,128)(2,1)S(1)} %get-tuple-element.10), channel_id=1, source_target_pairs={{64,0},{128,64},{192,128},{256,192},{320,256},{384,320},{448,384},... | collective-permute-start | bytes 24584 | tf_op jit(solution)/shard_map/ppermute | solution.py:21
  7.5 0.0 collective-permute-done
  7.5 3.1 %collective-permute-done.1 = bf16[32,128]{1,0:T(8,128)(2,1)S(1)} collective-permute-done((bf16[32,128]{1,0:T(8,128)(2,1)S(1)}, bf16[32,128]{1,0:T(8,128)(2,1)S(1)}, u32[]{:S(2)}, u32[]{:S(2)}) %collective-permute-start.1) | collective-permute-done | bytes 8224 | tf_op jit(solution)/shard_map/ppermute | solution.py:21
  10.6 0.7 pad_maximum_fusion.1
  11.3 0.1 broadcast_in_dim.2
  11.4 43.5 %all_to_all.10 = bf16[32,32,512]{2,1,0:T(8,128)(2,1)S(1)} all-to-all(bf16[32,32,512]{2,1,0:T(8,128)(2,1)S(1)} %broadcast_in_dim.2), channel_id=1, replica_groups=mesh['band'=8,'y'=8,'zh'=4,'core'=2] {'y','zh'}, dimensions={0} | all-to-all | bytes 2097152 | tf_op jit(solution)/shard_map/all_to_all | solution.py:51
  54.9 1.9 %collective-permute-start.2 = (bf16[32,32,512]{2,1,0:T(8,128)(2,1)S(1)}, bf16[32,32,512]{2,1,0:T(8,128)(2,1)S(1)}, u32[]{:S(2)}, u32[]{:S(2)}) collective-permute-start(bf16[32,32,512]{2,1,0:T(8,128)(2,1)S(1)} %all_to_all.10), channel_id=1, source_target_pairs={{0,1},{1,0},{2,3},{3,2},{4,5},{5,4},{6,7},{7,6},{8,9},{9,8},{10,11... | collective-permute-start | bytes 3145736 | tf_op jit(solution)/shard_map/ppermute | solution.py:45
  56.9 0.0 copy-done
  56.9 0.0 copy-done.1
  56.9 0.1 broadcast_and_fusion.1
  57.0 0.1 pad_add_fusion
  57.1 2.3 %collective-permute-done.2 = bf16[32,32,512]{2,1,0:T(8,128)(2,1)S(1)} collective-permute-done((bf16[32,32,512]{2,1,0:T(8,128)(2,1)S(1)}, bf16[32,32,512]{2,1,0:T(8,128)(2,1)S(1)}, u32[]{:S(2)}, u32[]{:S(2)}) %collective-permute-start.2) | collective-permute-done | bytes 1048608 | tf_op jit(solution)/shard_map/ppermute | solution.py:45
  59.5 0.1 select_bitcast_fusion.1
  59.6 0.2 pad_maximum_fusion
  59.8 0.1 constant_dynamic-slice_fusion.x_ref
  59.9 6.7 %shard_map.46 = f32[1024,256]{1,0:T(8,128)S(1)} custom-call(bf16[1040,512]{1,0:T(8,128)(2,1)S(1)} %constant_dynamic-slice_fusion.x_ref, bf16[16,512,256]{2,1,0:T(8,128)(2,1)} %w_ref.1, s32[16,8,256]{2,1,0:T(8,128)S(1)} %pad_convert_fusion.m_ref), custom_call_target="tpu_custom_call" | custom-call | flops 4294967296 | bytes 6307840 | tf_op jit(solution)/shard_map/pallas_call | solution.py:103
  66.6 0.1 select_bitcast_fusion.2
  66.7 2.0 %collective-permute-start.3 = (f32[32,16,256]{2,1,0:T(8,128)S(1)}, f32[32,16,256]{2,1,0:T(8,128)S(1)}, u32[]{:S(2)}, u32[]{:S(2)}) collective-permute-start(f32[32,16,256]{2,1,0:T(8,128)S(1)} %select_bitcast_fusion.2), channel_id=1, source_target_pairs={{0,1},{1,0},{2,3},{3,2},{4,5},{5,4},{6,7},{7,6},{8,9},{9,8},{10,11... | collective-permute-start | bytes 1572872 | tf_op jit(solution)/shard_map/ppermute | solution.py:45
  68.7 1.8 %collective-permute-done.3 = f32[32,16,256]{2,1,0:T(8,128)S(1)} collective-permute-done((f32[32,16,256]{2,1,0:T(8,128)S(1)}, f32[32,16,256]{2,1,0:T(8,128)S(1)}, u32[]{:S(2)}, u32[]{:S(2)}) %collective-permute-start.3) | collective-permute-done | bytes 524320 | tf_op jit(solution)/shard_map/ppermute | solution.py:45
  70.5 0.1 fusion.1
  70.6 26.2 %all_to_all.11 = f32[32,16,256]{2,1,0:T(8,128)S(1)} all-to-all(f32[32,16,256]{2,1,0:T(8,128)S(1)} %fusion.1), channel_id=1, replica_groups=mesh['band'=8,'y'=8,'zh'=4,'core'=2] {'y','zh'}, dimensions={0} | all-to-all | bytes 1048576 | tf_op jit(solution)/shard_map/all_to_all | solution.py:65
  96.8 0.6 reduce_sum.9
  (3 shorter events, 0.0 us)
Async XLA Ops:
  0.0 56.9 %copy-start = (s32[256,2]{0,1:T(2,128)S(1)}, s32[256,2]{0,1:T(2,128)}, u32[]{:S(2)}) copy-start(s32[256,2]{0,1:T(2,128)} %param.7) | copy-start | bytes 6148
  0.0 56.9 %copy-start.1 = (s32[256]{0:T(256)S(1)}, s32[256]{0:T(256)}, u32[]{:S(2)}) copy-start(s32[256]{0:T(256)} %param.6) | copy-start | bytes 3076
  0.7 6.7 %collective-permute-start = (bf16[32,128]{1,0:T(8,128)(2,1)S(1)}, bf16[32,128]{1,0:T(8,128)(2,1)S(1)}, u32[]{:S(2)}, u32[]{:S(2)}) collective-permute-start(bf16[32,128]{1,0:T(8,128)(2,1)S(1)} %get-tuple-element.9), channel_id=1, source_target_pairs={{0,64},{64,128},{128,192},{192,256},{256,320},{320,384},{384,448},... | collective-permute-start | bytes 24584 | tf_op jit(solution)/shard_map/ppermute | solution.py:19
  5.0 5.5 %collective-permute-start.1 = (bf16[32,128]{1,0:T(8,128)(2,1)S(1)}, bf16[32,128]{1,0:T(8,128)(2,1)S(1)}, u32[]{:S(2)}, u32[]{:S(2)}) collective-permute-start(bf16[32,128]{1,0:T(8,128)(2,1)S(1)} %get-tuple-element.10), channel_id=1, source_target_pairs={{64,0},{128,64},{192,128},{256,192},{320,256},{384,320},{448,384},... | collective-permute-start | bytes 24584 | tf_op jit(solution)/shard_map/ppermute | solution.py:21
  54.9 4.5 %collective-permute-start.2 = (bf16[32,32,512]{2,1,0:T(8,128)(2,1)S(1)}, bf16[32,32,512]{2,1,0:T(8,128)(2,1)S(1)}, u32[]{:S(2)}, u32[]{:S(2)}) collective-permute-start(bf16[32,32,512]{2,1,0:T(8,128)(2,1)S(1)} %all_to_all.10), channel_id=1, source_target_pairs={{0,1},{1,0},{2,3},{3,2},{4,5},{5,4},{6,7},{7,6},{8,9},{9,8},{10,11... | collective-permute-start | bytes 3145736 | tf_op jit(solution)/shard_map/ppermute | solution.py:45
  66.7 3.8 %collective-permute-start.3 = (f32[32,16,256]{2,1,0:T(8,128)S(1)}, f32[32,16,256]{2,1,0:T(8,128)S(1)}, u32[]{:S(2)}, u32[]{:S(2)}) collective-permute-start(f32[32,16,256]{2,1,0:T(8,128)S(1)} %select_bitcast_fusion.2), channel_id=1, source_target_pairs={{0,1},{1,0},{2,3},{3,2},{4,5},{5,4},{6,7},{7,6},{8,9},{9,8},{10,11... | collective-permute-start | bytes 1572872 | tf_op jit(solution)/shard_map/ppermute | solution.py:45

commit v8 on v7

--- a/solution.py
+++ b/solution.py
@@ -45,14 +45,19 @@
     return lax.ppermute(x, "core", [(0, 1), (1, 0)])
 
 
-def gather_history(x):
+def gather_window(x, base, length, align):
     chips = lax.axis_size("y") * lax.axis_size("zh")
     spread = jnp.broadcast_to(x[None], (chips,) + x.shape)
     mine = lax.all_to_all(spread, ("y", "zh"), 0, 0, tiled=True)
-    other = swap_core(mine)
+    pair_rows = 2 * x.shape[0]
+    span = (length + 2 * pair_rows - align - 1) // pair_rows
+    first_pair = jnp.minimum(base // pair_rows, chips - span)
+    needed = lax.dynamic_slice_in_dim(mine, first_pair, span, 0)
+    other = swap_core(needed)
     first = lax.axis_index("core") == 0
-    pair = jnp.stack([jnp.where(first, mine, other), jnp.where(first, other, mine)], 1)
-    return pair.reshape(-1, x.shape[1])
+    pair = jnp.stack([jnp.where(first, needed, other), jnp.where(first, other, needed)], 1)
+    rows = pair.reshape(-1, x.shape[1])
+    return lax.dynamic_slice_in_dim(rows, base - first_pair * pair_rows, length, 0)
 
 
 def reduce_scatter(partial, n_tm):
@@ -133,9 +138,8 @@
     window_len = driven_wave.shape[0] * n_tm - total_taps
     me = tm_index()
     first_tap = me * tap_dev
-    history = gather_history(extended(driven_wave, half_width))
     base = total_taps - first_tap - tap_dev
-    window = lax.dynamic_slice_in_dim(history, base, window_len + tap_dev, 0)
+    window = gather_window(extended(driven_wave, half_width), base, window_len + tap_dev, tap_dev)
     marks = tap_marks(tap_counts, panel_links, first_tap, tap_dev)
     partial = masked_conv(window, responses, marks, window_len)
     summed = reduce_scatter(partial, n_tm)

time: 97.9 us -> 98.3 us (level)
  blocking collectives: 69.7 us -> 26.1 us
  waiting for transfers between devices: 7.16 us -> 34.9 us
  starting transfers between devices: 10.7 us -> 26.1 us
  local copies, waits for them, and re-layouts: 0.94 us -> 1.93 us
    all_to_all x1 -> x0, blocking collectives: 43.5 us -> none  [gather_history(): mine = lax.all_to_all(spread, ('y', 'zh'), 0, 0, tiled=True)]
    all_to_all x0 -> x1, waiting for transfers between devices: none -> 28.4 us  [gather_window(): mine = lax.all_to_all(spread, ('y', 'zh'), 0, 0, tiled=True)]
    all_to_all x0 -> x1, starting transfers between devices: none -> 15.4 us  [gather_window(): mine = lax.all_to_all(spread, ('y', 'zh'), 0, 0, tiled=True)]
  transfers between devices with their start and end apart: 4 -> 5, of which waited for: 3 -> 4; matrix products, arithmetic and copies ran while one was open for 0% -> 0% of each run, Pallas kernels for 0% -> 0%
where the time goes in v8:
time: 98.3 us; the launch traced here: 97.9 us
  waiting for transfers between devices  34.9 us (36%)
  starting transfers between devices  26.1 us (27%)
  blocking collectives  26.1 us (27%)
  Pallas kernels  6.69 us (7%)
  other arithmetic  2.01 us (2%)
  local copies, waits for them, and re-layouts  1.93 us (2%)
    all_to_all x1, waiting for transfers between devices, gather_window(): mine = lax.all_to_all(spread, ('y', 'zh'), 0, 0, tiled=True)  28.4 us
    all_to_all x1, blocking collectives, reduce_scatter(): return lax.all_to_all(combined, ('y', 'zh'), 0, 0, tiled=True).sum(0)  26.1 us
    all_to_all x1, starting transfers between devices, gather_window(): mine = lax.all_to_all(spread, ('y', 'zh'), 0, 0, tiled=True)  15.4 us
    pallas_call x1, Pallas kernels, masked_conv(): pl.pallas_call(conv_kernel, out_shape=jax.ShapeDtypeStruct((rows, ports),...  6.69 us
    ppermute x1, starting transfers between devices, extended(): lax.ppermute(tail, 'band', [(i, (i + 1) % count) for i in range(ends)])  4.27 us
    ppermute x2, starting transfers between devices, swap_core(): return lax.ppermute(x, 'core', [(0, 1), (1, 0)])  3.96 us
    ppermute x2, waiting for transfers between devices, swap_core(): return lax.ppermute(x, 'core', [(0, 1), (1, 0)])  3.43 us
    ppermute x1, waiting for transfers between devices, extended(): lax.ppermute(head, 'band', [((i + 1) % count, i) for i in range(ends)])  3.07 us
  transfers between devices with their start and end apart: 5, of which 4 were waited for; matrix products, arithmetic and copies ran while one was open for 0% of the time, Pallas kernels for 0%

profile of v8, /device:TPU:14, one launch (start us, length us, event | category | flops | bytes accessed | tf_op | source)
XLA Modules:
  0.0 97.9 jit_solution(11836995582759616651)
XLA Ops:
  0.0 0.7 fusion.2
  0.7 4.3 %collective-permute-start = (bf16[32,128]{1,0:T(8,128)(2,1)S(1)}, bf16[32,128]{1,0:T(8,128)(2,1)S(1)}, u32[]{:S(2)}, u32[]{:S(2)}) collective-permute-start(bf16[32,128]{1,0:T(8,128)(2,1)S(1)} %get-tuple-element.9), channel_id=1, source_target_pairs={{0,64},{64,128},{128,192},{192,256},{256,320},{320,384},{384,448},... | collective-permute-start | bytes 24584 | tf_op jit(solution)/shard_map/ppermute | solution.py:19
  5.0 2.5 %collective-permute-start.1 = (bf16[32,128]{1,0:T(8,128)(2,1)S(1)}, bf16[32,128]{1,0:T(8,128)(2,1)S(1)}, u32[]{:S(2)}, u32[]{:S(2)}) collective-permute-start(bf16[32,128]{1,0:T(8,128)(2,1)S(1)} %get-tuple-element.10), channel_id=1, source_target_pairs={{64,0},{128,64},{192,128},{256,192},{320,256},{384,320},{448,384},... | collective-permute-start | bytes 24584 | tf_op jit(solution)/shard_map/ppermute | solution.py:21
  7.5 0.0 collective-permute-done
  7.5 3.1 %collective-permute-done.1 = bf16[32,128]{1,0:T(8,128)(2,1)S(1)} collective-permute-done((bf16[32,128]{1,0:T(8,128)(2,1)S(1)}, bf16[32,128]{1,0:T(8,128)(2,1)S(1)}, u32[]{:S(2)}, u32[]{:S(2)}) %collective-permute-start.1) | collective-permute-done | bytes 8224 | tf_op jit(solution)/shard_map/ppermute | solution.py:21
  10.5 0.7 pad_maximum_fusion.1
  11.3 1.1 %broadcast_in_dim.2 = bf16[32,32,512]{2,1,0:T(8,128)(2,1)} broadcast(bf16[32,512]{1,0:T(8,128)(2,1)S(1)} %pad_maximum_fusion.1), dimensions={1,2} | broadcast | bytes 1081344 | tf_op jit(solution)/shard_map/broadcast_in_dim | solution.py:50
  12.3 0.0 copy-start
  12.4 15.4 %all-to-all-start = ((bf16[32,32,512]{2,1,0:T(8,128)(2,1)}), bf16[32,32,512]{2,1,0:T(8,128)(2,1)S(1)}, u32[]{:S(2)}, u32[]{:S(2)}) async-start(bf16[32,32,512]{2,1,0:T(8,128)(2,1)} %broadcast_in_dim.2), calls=%async_computation | async-start | bytes 2097152 | tf_op jit(solution)/shard_map/all_to_all | solution.py:51
  27.8 0.0 copy-start.1
  27.8 0.0 copy-done
  27.8 28.4 %all-to-all-done = bf16[32,32,512]{2,1,0:T(8,128)(2,1)S(1)} async-done(((bf16[32,32,512]{2,1,0:T(8,128)(2,1)}), bf16[32,32,512]{2,1,0:T(8,128)(2,1)S(1)}, u32[]{:S(2)}, u32[]{:S(2)}) %all-to-all-start) | async-done | bytes 1048608 | tf_op jit(solution)/shard_map/all_to_all | solution.py:51
  56.3 1.9 %collective-permute-start.2 = (bf16[17,32,512]{2,1,0:T(8,128)(2,1)S(1)}, bf16[17,32,512]{2,1,0:T(8,128)(2,1)S(1)}, u32[]{:S(2)}, u32[]{:S(2)}) collective-permute-start(bf16[17,32,512]{2,1,0:T(8,128)(2,1)S(1)} %constant_dynamic-slice_fusion.1), channel_id=1, source_target_pairs={{0,1},{1,0},{2,3},{3,2},{4,5},{5,4},{6,7},{7,6},{8,9},{9,8},{10,11... | collective-permute-start | bytes 1671176 | tf_op jit(solution)/shard_map/ppermute | solution.py:45
  58.2 0.0 copy-done.1
  58.2 0.1 broadcast_and_fusion.1
  58.3 0.1 pad_add_fusion
  58.4 1.7 %collective-permute-done.2 = bf16[17,32,512]{2,1,0:T(8,128)(2,1)S(1)} collective-permute-done((bf16[17,32,512]{2,1,0:T(8,128)(2,1)S(1)}, bf16[17,32,512]{2,1,0:T(8,128)(2,1)S(1)}, u32[]{:S(2)}, u32[]{:S(2)}) %collective-permute-start.2) | collective-permute-done | bytes 557088 | tf_op jit(solution)/shard_map/ppermute | solution.py:45
  60.1 0.1 select_bitcast_fusion.1
  60.2 0.1 pad_maximum_fusion
  60.3 0.1 constant_dynamic-slice_fusion.x_ref
  60.4 6.7 %shard_map.46 = f32[1024,256]{1,0:T(8,128)S(1)} custom-call(bf16[1040,512]{1,0:T(8,128)(2,1)S(1)} %constant_dynamic-slice_fusion.x_ref, bf16[16,512,256]{2,1,0:T(8,128)(2,1)} %w_ref.1, s32[16,8,256]{2,1,0:T(8,128)S(1)} %pad_convert_fusion.m_ref), custom_call_target="tpu_custom_call" | custom-call | flops 4294967296 | bytes 6307840 | tf_op jit(solution)/shard_map/pallas_call | solution.py:108
  67.1 0.1 select_bitcast_fusion.2
  67.2 2.0 %collective-permute-start.3 = (f32[32,16,256]{2,1,0:T(8,128)S(1)}, f32[32,16,256]{2,1,0:T(8,128)S(1)}, u32[]{:S(2)}, u32[]{:S(2)}) collective-permute-start(f32[32,16,256]{2,1,0:T(8,128)S(1)} %select_bitcast_fusion.2), channel_id=1, source_target_pairs={{0,1},{1,0},{2,3},{3,2},{4,5},{5,4},{6,7},{7,6},{8,9},{9,8},{10,11... | collective-permute-start | bytes 1572872 | tf_op jit(solution)/shard_map/ppermute | solution.py:45
  69.2 1.8 %collective-permute-done.3 = f32[32,16,256]{2,1,0:T(8,128)S(1)} collective-permute-done((f32[32,16,256]{2,1,0:T(8,128)S(1)}, f32[32,16,256]{2,1,0:T(8,128)S(1)}, u32[]{:S(2)}, u32[]{:S(2)}) %collective-permute-start.3) | collective-permute-done | bytes 524320 | tf_op jit(solution)/shard_map/ppermute | solution.py:45
  71.0 0.1 fusion.1
  71.1 26.1 %all_to_all.10 = f32[32,16,256]{2,1,0:T(8,128)S(1)} all-to-all(f32[32,16,256]{2,1,0:T(8,128)S(1)} %fusion.1), channel_id=1, replica_groups=mesh['band'=8,'y'=8,'zh'=4,'core'=2] {'y','zh'}, dimensions={0} | all-to-all | bytes 1048576 | tf_op jit(solution)/shard_map/all_to_all | solution.py:70
  97.2 0.6 reduce_sum.9
  (4 shorter events, 0.1 us)
Async XLA Ops:
  0.7 6.7 %collective-permute-start = (bf16[32,128]{1,0:T(8,128)(2,1)S(1)}, bf16[32,128]{1,0:T(8,128)(2,1)S(1)}, u32[]{:S(2)}, u32[]{:S(2)}) collective-permute-start(bf16[32,128]{1,0:T(8,128)(2,1)S(1)} %get-tuple-element.9), channel_id=1, source_target_pairs={{0,64},{64,128},{128,192},{192,256},{256,320},{320,384},{384,448},... | collective-permute-start | bytes 24584 | tf_op jit(solution)/shard_map/ppermute | solution.py:19
  5.0 5.5 %collective-permute-start.1 = (bf16[32,128]{1,0:T(8,128)(2,1)S(1)}, bf16[32,128]{1,0:T(8,128)(2,1)S(1)}, u32[]{:S(2)}, u32[]{:S(2)}) collective-permute-start(bf16[32,128]{1,0:T(8,128)(2,1)S(1)} %get-tuple-element.10), channel_id=1, source_target_pairs={{64,0},{128,64},{192,128},{256,192},{320,256},{384,320},{448,384},... | collective-permute-start | bytes 24584 | tf_op jit(solution)/shard_map/ppermute | solution.py:21
  12.3 15.5 %copy-start = (s32[256,2]{0,1:T(2,128)S(1)}, s32[256,2]{0,1:T(2,128)}, u32[]{:S(2)}) copy-start(s32[256,2]{0,1:T(2,128)} %param.7) | copy-start | bytes 6148
  12.4 43.8 %all-to-all-start = ((bf16[32,32,512]{2,1,0:T(8,128)(2,1)}), bf16[32,32,512]{2,1,0:T(8,128)(2,1)S(1)}, u32[]{:S(2)}, u32[]{:S(2)}) async-start(bf16[32,32,512]{2,1,0:T(8,128)(2,1)} %broadcast_in_dim.2), calls=%async_computation | async-start | bytes 2097152 | tf_op jit(solution)/shard_map/all_to_all | solution.py:51
  27.8 30.4 %copy-start.1 = (s32[256]{0:T(256)S(1)}, s32[256]{0:T(256)}, u32[]{:S(2)}) copy-start(s32[256]{0:T(256)} %param.6) | copy-start | bytes 3076
  56.3 3.9 %collective-permute-start.2 = (bf16[17,32,512]{2,1,0:T(8,128)(2,1)S(1)}, bf16[17,32,512]{2,1,0:T(8,128)(2,1)S(1)}, u32[]{:S(2)}, u32[]{:S(2)}) collective-permute-start(bf16[17,32,512]{2,1,0:T(8,128)(2,1)S(1)} %constant_dynamic-slice_fusion.1), channel_id=1, source_target_pairs={{0,1},{1,0},{2,3},{3,2},{4,5},{5,4},{6,7},{7,6},{8,9},{9,8},{10,11... | collective-permute-start | bytes 1671176 | tf_op jit(solution)/shard_map/ppermute | solution.py:45
  67.2 3.8 %collective-permute-start.3 = (f32[32,16,256]{2,1,0:T(8,128)S(1)}, f32[32,16,256]{2,1,0:T(8,128)S(1)}, u32[]{:S(2)}, u32[]{:S(2)}) collective-permute-start(f32[32,16,256]{2,1,0:T(8,128)S(1)} %select_bitcast_fusion.2), channel_id=1, source_target_pairs={{0,1},{1,0},{2,3},{3,2},{4,5},{5,4},{6,7},{7,6},{8,9},{9,8},{10,11... | collective-permute-start | bytes 1572872 | tf_op jit(solution)/shard_map/ppermute | solution.py:45

commit v9 on v8

--- a/solution.py
+++ b/solution.py
@@ -45,18 +45,28 @@
     return lax.ppermute(x, "core", [(0, 1), (1, 0)])
 
 
-def gather_window(x, base, length, align):
+def band_halo(cells, width):
+    count = lax.axis_size("band")
+    ends = count - 1
+    head = cells[..., :width]
+    tail = cells[..., cells.shape[-1] - width :]
+    below = lax.ppermute(tail, "band", [(i, (i + 1) % count) for i in range(ends)])
+    above = lax.ppermute(head, "band", [((i + 1) % count, i) for i in range(ends)])
+    return jnp.concatenate([below, cells, above], axis=-1)
+
+
+def gather_window(x, base, length, align, width):
     chips = lax.axis_size("y") * lax.axis_size("zh")
     spread = jnp.broadcast_to(x[None], (chips,) + x.shape)
     mine = lax.all_to_all(spread, ("y", "zh"), 0, 0, tiled=True)
     pair_rows = 2 * x.shape[0]
     span = (length + 2 * pair_rows - align - 1) // pair_rows
     first_pair = jnp.minimum(base // pair_rows, chips - span)
-    needed = lax.dynamic_slice_in_dim(mine, first_pair, span, 0)
+    needed = band_halo(lax.dynamic_slice_in_dim(mine, first_pair, span, 0), width)
     other = swap_core(needed)
     first = lax.axis_index("core") == 0
     pair = jnp.stack([jnp.where(first, needed, other), jnp.where(first, other, needed)], 1)
-    rows = pair.reshape(-1, x.shape[1])
+    rows = pair.reshape(-1, needed.shape[-1])
     return lax.dynamic_slice_in_dim(rows, base - first_pair * pair_rows, length, 0)
 
 
@@ -139,7 +149,7 @@
     me = tm_index()
     first_tap = me * tap_dev
     base = total_taps - first_tap - tap_dev
-    window = gather_window(extended(driven_wave, half_width), base, window_len + tap_dev, tap_dev)
+    window = gather_window(driven_wave, base, window_len + tap_dev, tap_dev, half_width)
     marks = tap_marks(tap_counts, panel_links, first_tap, tap_dev)
     partial = masked_conv(window, responses, marks, window_len)
     summed = reduce_scatter(partial, n_tm)

time: 98.3 us -> 89.2 us (0.907)
  the two profiles are of different devices: /device:TPU:14 before, /device:TPU:10 now
where the time goes in v9:
time: 89.2 us; the launch traced here: 88.7 us
  starting transfers between devices  26.9 us (30%)
  waiting for transfers between devices  26.3 us (29%)
  blocking collectives  25.4 us (28%)
  Pallas kernels  6.69 us (8%)
  local copies, waits for them, and re-layouts  1.75 us (2%)
  other arithmetic  1.53 us (2%)
    all_to_all x1, blocking collectives, reduce_scatter(): return lax.all_to_all(combined, ('y', 'zh'), 0, 0, tiled=True).sum(0)  25.4 us
    all_to_all x1, waiting for transfers between devices, gather_window(): mine = lax.all_to_all(spread, ('y', 'zh'), 0, 0, tiled=True)  19.4 us
    all_to_all x1, starting transfers between devices, gather_window(): mine = lax.all_to_all(spread, ('y', 'zh'), 0, 0, tiled=True)  16.2 us
    pallas_call x1, Pallas kernels, masked_conv(): pl.pallas_call(conv_kernel, out_shape=jax.ShapeDtypeStruct((rows, ports),...  6.69 us
    ppermute x2, starting transfers between devices, swap_core(): return lax.ppermute(x, 'core', [(0, 1), (1, 0)])  3.96 us
    ppermute x2, waiting for transfers between devices, swap_core(): return lax.ppermute(x, 'core', [(0, 1), (1, 0)])  3.43 us
    ppermute x1, starting transfers between devices, band_halo(): lax.ppermute(head, 'band', [((i + 1) % count, i) for i in range(ends)])  3.4 us
    ppermute x1, starting transfers between devices, band_halo(): lax.ppermute(tail, 'band', [(i, (i + 1) % count) for i in range(ends)])  3.34 us
  transfers between devices with their start and end apart: 5, of which 5 were waited for; matrix products, arithmetic and copies ran while one was open for 0% of the time, Pallas kernels for 0%

profile of v9, /device:TPU:10, one launch (start us, length us, event | category | flops | bytes accessed | tf_op | source)
XLA Modules:
  0.0 88.7 jit_solution(6486301711982223612)
XLA Ops:
  0.0 0.0 copy-start
  0.0 1.6 %broadcast_in_dim.2 = bf16[32,32,256]{2,1,0:T(8,128)(2,1)} broadcast(bf16[32,256]{1,0:T(8,128)(2,1)} %param.4), dimensions={1,2} | broadcast | bytes 540672 | tf_op jit(solution)/shard_map/broadcast_in_dim | solution.py:60
  1.6 16.2 %all-to-all-start = ((bf16[32,32,256]{2,1,0:T(8,128)(2,1)}), bf16[32,32,256]{2,1,0:T(8,128)(2,1)S(1)}, u32[]{:S(2)}, u32[]{:S(2)}) async-start(bf16[32,32,256]{2,1,0:T(8,128)(2,1)} %broadcast_in_dim.2), calls=%async_computation | async-start | bytes 1048576 | tf_op jit(solution)/shard_map/all_to_all | solution.py:61
  17.8 0.0 copy-start.1
  17.8 19.4 %all-to-all-done = bf16[32,32,256]{2,1,0:T(8,128)(2,1)S(1)} async-done(((bf16[32,32,256]{2,1,0:T(8,128)(2,1)}), bf16[32,32,256]{2,1,0:T(8,128)(2,1)S(1)}, u32[]{:S(2)}, u32[]{:S(2)}) %all-to-all-start) | async-done | bytes 524320 | tf_op jit(solution)/shard_map/all_to_all | solution.py:61
  37.2 0.1 constant_dynamic-slice_fusion.1
  37.3 3.3 %collective-permute-start = (bf16[17,32,128]{2,1,0:T(8,128)(2,1)S(1)}, bf16[17,32,128]{2,1,0:T(8,128)(2,1)S(1)}, u32[]{:S(2)}, u32[]{:S(2)}) collective-permute-start(bf16[17,32,128]{2,1,0:T(8,128)(2,1)S(1)} %get-tuple-element.9), channel_id=1, source_target_pairs={{0,64},{64,128},{128,192},{192,256},{256,320},{320,384},{384,448},... | collective-permute-start | bytes 417800 | tf_op jit(solution)/shard_map/ppermute | solution.py:53
  40.6 3.4 %collective-permute-start.1 = (bf16[17,32,128]{2,1,0:T(8,128)(2,1)S(1)}, bf16[17,32,128]{2,1,0:T(8,128)(2,1)S(1)}, u32[]{:S(2)}, u32[]{:S(2)}) collective-permute-start(bf16[17,32,128]{2,1,0:T(8,128)(2,1)S(1)} %get-tuple-element.10), channel_id=1, source_target_pairs={{64,0},{128,64},{192,128},{256,192},{320,256},{384,320},{448,384},... | collective-permute-start | bytes 417800 | tf_op jit(solution)/shard_map/ppermute | solution.py:54
  44.0 0.0 copy-done
  44.1 1.0 %collective-permute-done = bf16[17,32,128]{2,1,0:T(8,128)(2,1)S(1)} collective-permute-done((bf16[17,32,128]{2,1,0:T(8,128)(2,1)S(1)}, bf16[17,32,128]{2,1,0:T(8,128)(2,1)S(1)}, u32[]{:S(2)}, u32[]{:S(2)}) %collective-permute-start) | collective-permute-done | bytes 139296 | tf_op jit(solution)/shard_map/ppermute | solution.py:53
  45.1 2.5 %collective-permute-done.1 = bf16[17,32,128]{2,1,0:T(8,128)(2,1)S(1)} collective-permute-done((bf16[17,32,128]{2,1,0:T(8,128)(2,1)S(1)}, bf16[17,32,128]{2,1,0:T(8,128)(2,1)S(1)}, u32[]{:S(2)}, u32[]{:S(2)}) %collective-permute-start.1) | collective-permute-done | bytes 139296 | tf_op jit(solution)/shard_map/ppermute | solution.py:54
  47.6 0.1 pad_maximum_fusion.1
  47.6 1.9 %collective-permute-start.2 = (bf16[17,32,512]{2,1,0:T(8,128)(2,1)S(1)}, bf16[17,32,512]{2,1,0:T(8,128)(2,1)S(1)}, u32[]{:S(2)}, u32[]{:S(2)}) collective-permute-start(bf16[17,32,512]{2,1,0:T(8,128)(2,1)S(1)} %pad_maximum_fusion.1), channel_id=1, source_target_pairs={{0,1},{1,0},{2,3},{3,2},{4,5},{5,4},{6,7},{7,6},{8,9},{9,8},{10,11... | collective-permute-start | bytes 1671176 | tf_op jit(solution)/shard_map/ppermute | solution.py:45
  49.6 0.0 copy-done.1
  49.6 0.1 broadcast_and_fusion.1
  49.7 0.1 pad_add_fusion
  49.8 1.7 %collective-permute-done.2 = bf16[17,32,512]{2,1,0:T(8,128)(2,1)S(1)} collective-permute-done((bf16[17,32,512]{2,1,0:T(8,128)(2,1)S(1)}, bf16[17,32,512]{2,1,0:T(8,128)(2,1)S(1)}, u32[]{:S(2)}, u32[]{:S(2)}) %collective-permute-start.2) | collective-permute-done | bytes 557088 | tf_op jit(solution)/shard_map/ppermute | solution.py:45
  51.5 0.2 select_bitcast_fusion.1
  51.7 0.1 pad_maximum_fusion
  51.9 0.1 constant_dynamic-slice_fusion.2.x_ref
  52.0 6.7 %shard_map.46 = f32[1024,256]{1,0:T(8,128)S(1)} custom-call(bf16[1040,512]{1,0:T(8,128)(2,1)S(1)} %constant_dynamic-slice_fusion.2.x_ref, bf16[16,512,256]{2,1,0:T(8,128)(2,1)} %w_ref.1, s32[16,8,256]{2,1,0:T(8,128)S(1)} %pad_convert_fusion.m_ref), custom_call_target="tpu_custom_call" | custom-call | flops 4294967296 | bytes 6307840 | tf_op jit(solution)/shard_map/pallas_call | solution.py:118
  58.6 0.1 select_bitcast_fusion.2
  58.7 2.0 %collective-permute-start.3 = (f32[32,16,256]{2,1,0:T(8,128)S(1)}, f32[32,16,256]{2,1,0:T(8,128)S(1)}, u32[]{:S(2)}, u32[]{:S(2)}) collective-permute-start(f32[32,16,256]{2,1,0:T(8,128)S(1)} %select_bitcast_fusion.2), channel_id=1, source_target_pairs={{0,1},{1,0},{2,3},{3,2},{4,5},{5,4},{6,7},{7,6},{8,9},{9,8},{10,11... | collective-permute-start | bytes 1572872 | tf_op jit(solution)/shard_map/ppermute | solution.py:45
  60.8 1.8 %collective-permute-done.3 = f32[32,16,256]{2,1,0:T(8,128)S(1)} collective-permute-done((f32[32,16,256]{2,1,0:T(8,128)S(1)}, f32[32,16,256]{2,1,0:T(8,128)S(1)}, u32[]{:S(2)}, u32[]{:S(2)}) %collective-permute-start.3) | collective-permute-done | bytes 524320 | tf_op jit(solution)/shard_map/ppermute | solution.py:45
  62.5 0.1 fusion.1
  62.7 25.4 %all_to_all.10 = f32[32,16,256]{2,1,0:T(8,128)S(1)} all-to-all(f32[32,16,256]{2,1,0:T(8,128)S(1)} %fusion.1), channel_id=1, replica_groups=mesh['band'=8,'y'=8,'zh'=4,'core'=2] {'y','zh'}, dimensions={0} | all-to-all | bytes 1048576 | tf_op jit(solution)/shard_map/all_to_all | solution.py:80
  88.1 0.6 reduce_sum.9
  (4 shorter events, 0.1 us)
Async XLA Ops:
  0.0 44.0 %copy-start = (s32[256,2]{0,1:T(2,128)S(1)}, s32[256,2]{0,1:T(2,128)}, u32[]{:S(2)}) copy-start(s32[256,2]{0,1:T(2,128)} %param.7) | copy-start | bytes 6148
  1.6 35.6 %all-to-all-start = ((bf16[32,32,256]{2,1,0:T(8,128)(2,1)}), bf16[32,32,256]{2,1,0:T(8,128)(2,1)S(1)}, u32[]{:S(2)}, u32[]{:S(2)}) async-start(bf16[32,32,256]{2,1,0:T(8,128)(2,1)} %broadcast_in_dim.2), calls=%async_computation | async-start | bytes 1048576 | tf_op jit(solution)/shard_map/all_to_all | solution.py:61
  17.8 31.8 %copy-start.1 = (s32[256]{0:T(256)S(1)}, s32[256]{0:T(256)}, u32[]{:S(2)}) copy-start(s32[256]{0:T(256)} %param.6) | copy-start | bytes 3076
  37.3 7.8 %collective-permute-start = (bf16[17,32,128]{2,1,0:T(8,128)(2,1)S(1)}, bf16[17,32,128]{2,1,0:T(8,128)(2,1)S(1)}, u32[]{:S(2)}, u32[]{:S(2)}) collective-permute-start(bf16[17,32,128]{2,1,0:T(8,128)(2,1)S(1)} %get-tuple-element.9), channel_id=1, source_target_pairs={{0,64},{64,128},{128,192},{192,256},{256,320},{320,384},{384,448},... | collective-permute-start | bytes 417800 | tf_op jit(solution)/shard_map/ppermute | solution.py:53
  40.6 6.9 %collective-permute-start.1 = (bf16[17,32,128]{2,1,0:T(8,128)(2,1)S(1)}, bf16[17,32,128]{2,1,0:T(8,128)(2,1)S(1)}, u32[]{:S(2)}, u32[]{:S(2)}) collective-permute-start(bf16[17,32,128]{2,1,0:T(8,128)(2,1)S(1)} %get-tuple-element.10), channel_id=1, source_target_pairs={{64,0},{128,64},{192,128},{256,192},{320,256},{384,320},{448,384},... | collective-permute-start | bytes 417800 | tf_op jit(solution)/shard_map/ppermute | solution.py:54
  47.6 3.9 %collective-permute-start.2 = (bf16[17,32,512]{2,1,0:T(8,128)(2,1)S(1)}, bf16[17,32,512]{2,1,0:T(8,128)(2,1)S(1)}, u32[]{:S(2)}, u32[]{:S(2)}) collective-permute-start(bf16[17,32,512]{2,1,0:T(8,128)(2,1)S(1)} %pad_maximum_fusion.1), channel_id=1, source_target_pairs={{0,1},{1,0},{2,3},{3,2},{4,5},{5,4},{6,7},{7,6},{8,9},{9,8},{10,11... | collective-permute-start | bytes 1671176 | tf_op jit(solution)/shard_map/ppermute | solution.py:45
  58.7 3.8 %collective-permute-start.3 = (f32[32,16,256]{2,1,0:T(8,128)S(1)}, f32[32,16,256]{2,1,0:T(8,128)S(1)}, u32[]{:S(2)}, u32[]{:S(2)}) collective-permute-start(f32[32,16,256]{2,1,0:T(8,128)S(1)} %select_bitcast_fusion.2), channel_id=1, source_target_pairs={{0,1},{1,0},{2,3},{3,2},{4,5},{5,4},{6,7},{7,6},{8,9},{9,8},{10,11... | collective-permute-start | bytes 1572872 | tf_op jit(solution)/shard_map/ppermute | solution.py:45

commit v10 on v9

--- a/solution.py
+++ b/solution.py
@@ -45,14 +45,20 @@
     return lax.ppermute(x, "core", [(0, 1), (1, 0)])
 
 
-def band_halo(cells, width):
+def band_halo(cells, width, flip):
     count = lax.axis_size("band")
-    ends = count - 1
+    cores = lax.axis_size("core")
     head = cells[..., :width]
     tail = cells[..., cells.shape[-1] - width :]
-    below = lax.ppermute(tail, "band", [(i, (i + 1) % count) for i in range(ends)])
-    above = lax.ppermute(head, "band", [((i + 1) % count, i) for i in range(ends)])
-    return jnp.concatenate([below, cells, above], axis=-1)
+    up = [
+        (b * cores + k, (b + 1) * cores + (k + flip) % cores)
+        for b in range(count - 1)
+        for k in range(cores)
+    ]
+    down = [(dst, src) for src, dst in up]
+    below = lax.ppermute(tail, ("band", "core"), up)
+    above = lax.ppermute(head, ("band", "core"), down)
+    return below, above
 
 
 def gather_window(x, base, length, align, width):
@@ -62,8 +68,12 @@
     pair_rows = 2 * x.shape[0]
     span = (length + 2 * pair_rows - align - 1) // pair_rows
     first_pair = jnp.minimum(base // pair_rows, chips - span)
-    needed = band_halo(lax.dynamic_slice_in_dim(mine, first_pair, span, 0), width)
+    needed = lax.dynamic_slice_in_dim(mine, first_pair, span, 0)
     other = swap_core(needed)
+    below, above = band_halo(needed, width, 0)
+    below_other, above_other = band_halo(needed, width, 1)
+    needed = jnp.concatenate([below, needed, above], axis=-1)
+    other = jnp.concatenate([below_other, other, above_other], axis=-1)
     first = lax.axis_index("core") == 0
     pair = jnp.stack([jnp.where(first, needed, other), jnp.where(first, other, needed)], 1)
     rows = pair.reshape(-1, needed.shape[-1])

time: 89.2 us -> 93.9 us (1.053)
  starting transfers between devices: 26.9 us -> 32.2 us
  blocking collectives: 25.4 us -> 24.4 us
    ppermute x2 -> x4, starting transfers between devices: 6.74 us -> 12 us  [the longest x2 6.59 us: band_halo(): below = lax.ppermute(tail, ('band', 'core'), up)]
    ppermute x2 -> x4, waiting for transfers between devices: 3.46 us -> 5.65 us  [the longest x2 5.65 us: band_halo(): above = lax.ppermute(head, ('band', 'core'), down)]
    ppermute x2, waiting for transfers between devices: 3.43 us -> 1.75 us  [swap_core(): return lax.ppermute(x, 'core', [(0, 1), (1, 0)])]
    all_to_all x1, blocking collectives: 25.4 us -> 24.4 us  [reduce_scatter(): return lax.all_to_all(combined, ('y', 'zh'), 0, 0, tiled=True).sum(0)]
  transfers between devices with their start and end apart: 5 -> 7, of which waited for: 5 -> 4; matrix products, arithmetic and copies ran while one was open for 0% -> 0% of each run, Pallas kernels for 0% -> 0%
where the time goes in v10:
time: 93.9 us; the launch traced here: 93.3 us
  starting transfers between devices  32.2 us (34%)
  waiting for transfers between devices  26.6 us (28%)
  blocking collectives  24.4 us (26%)
  Pallas kernels  6.69 us (7%)
  local copies, waits for them, and re-layouts  1.78 us (2%)
  other arithmetic  1.51 us (2%)
    all_to_all x1, blocking collectives, reduce_scatter(): return lax.all_to_all(combined, ('y', 'zh'), 0, 0, tiled=True).sum(0)  24.4 us
    all_to_all x1, waiting for transfers between devices, gather_window(): mine = lax.all_to_all(spread, ('y', 'zh'), 0, 0, tiled=True)  19.2 us
    all_to_all x1, starting transfers between devices, gather_window(): mine = lax.all_to_all(spread, ('y', 'zh'), 0, 0, tiled=True)  16.2 us
    pallas_call x1, Pallas kernels, masked_conv(): pl.pallas_call(conv_kernel, out_shape=jax.ShapeDtypeStruct((rows, ports),...  6.69 us
    ppermute x2, starting transfers between devices, band_halo(): below = lax.ppermute(tail, ('band', 'core'), up)  6.59 us
    ppermute x2, waiting for transfers between devices, band_halo(): above = lax.ppermute(head, ('band', 'core'), down)  5.65 us
    ppermute x2, starting transfers between devices, band_halo(): above = lax.ppermute(head, ('band', 'core'), down)  5.44 us
    ppermute x2, starting transfers between devices, swap_core(): return lax.ppermute(x, 'core', [(0, 1), (1, 0)])  3.97 us
  transfers between devices with their start and end apart: 7, of which 4 were waited for; matrix products, arithmetic and copies ran while one was open for 0% of the time, Pallas kernels for 0%

profile of v10, /device:TPU:10, one launch (start us, length us, event | category | flops | bytes accessed | tf_op | source)
XLA Modules:
  0.0 93.3 jit_solution(3750127691807395428)
XLA Ops:
  0.0 0.0 copy-start
  0.0 0.0 copy-start.1
  0.0 1.6 %broadcast_in_dim.2 = bf16[32,32,256]{2,1,0:T(8,128)(2,1)} broadcast(bf16[32,256]{1,0:T(8,128)(2,1)} %param.4), dimensions={1,2} | broadcast | bytes 540672 | tf_op jit(solution)/shard_map/broadcast_in_dim | solution.py:66
  1.6 16.2 %all-to-all-start = ((bf16[32,32,256]{2,1,0:T(8,128)(2,1)}), bf16[32,32,256]{2,1,0:T(8,128)(2,1)S(1)}, u32[]{:S(2)}, u32[]{:S(2)}) async-start(bf16[32,32,256]{2,1,0:T(8,128)(2,1)} %broadcast_in_dim.2), calls=%async_computation | async-start | bytes 1048576 | tf_op jit(solution)/shard_map/all_to_all | solution.py:67
  17.8 0.0 copy-done
  17.8 0.0 copy-done.1
  17.9 0.1 broadcast_and_fusion.1
  18.0 0.1 pad_add_fusion
  18.1 19.2 %all-to-all-done = bf16[32,32,256]{2,1,0:T(8,128)(2,1)S(1)} async-done(((bf16[32,32,256]{2,1,0:T(8,128)(2,1)}), bf16[32,32,256]{2,1,0:T(8,128)(2,1)S(1)}, u32[]{:S(2)}, u32[]{:S(2)}) %all-to-all-start) | async-done | bytes 524320 | tf_op jit(solution)/shard_map/all_to_all | solution.py:67
  37.2 1.9 %collective-permute-start.3 = (bf16[17,32,256]{2,1,0:T(8,128)(2,1)S(1)}, bf16[17,32,256]{2,1,0:T(8,128)(2,1)S(1)}, u32[]{:S(2)}, u32[]{:S(2)}) collective-permute-start(bf16[17,32,256]{2,1,0:T(8,128)(2,1)S(1)} %constant_dynamic-slice_fusion.3), channel_id=1, source_target_pairs={{0,1},{1,0},{2,3},{3,2},{4,5},{5,4},{6,7},{7,6},{8,9},{9,8},{10,11... | collective-permute-start | bytes 835592 | tf_op jit(solution)/shard_map/ppermute | solution.py:45
  39.2 0.1 constant_dynamic-slice_fusion.1
  39.2 3.3 %collective-permute-start = (bf16[17,32,128]{2,1,0:T(8,128)(2,1)S(1)}, bf16[17,32,128]{2,1,0:T(8,128)(2,1)S(1)}, u32[]{:S(2)}, u32[]{:S(2)}) collective-permute-start(bf16[17,32,128]{2,1,0:T(8,128)(2,1)S(1)} %get-tuple-element.9), channel_id=1, source_target_pairs={{0,64},{1,65},{64,128},{65,129},{128,192},{129,193},{192,256},{193... | collective-permute-start | bytes 417800 | tf_op jit(solution)/shard_map/ppermute | solution.py:59
  42.6 3.2 %collective-permute-start.2 = (bf16[17,32,128]{2,1,0:T(8,128)(2,1)S(1)}, bf16[17,32,128]{2,1,0:T(8,128)(2,1)S(1)}, u32[]{:S(2)}, u32[]{:S(2)}) collective-permute-start(bf16[17,32,128]{2,1,0:T(8,128)(2,1)S(1)} %get-tuple-element.9), channel_id=1, source_target_pairs={{0,65},{1,64},{64,129},{65,128},{128,193},{129,192},{192,257},{193... | collective-permute-start | bytes 417800 | tf_op jit(solution)/shard_map/ppermute | solution.py:59
  45.8 3.3 %collective-permute-start.1 = (bf16[17,32,128]{2,1,0:T(8,128)(2,1)S(1)}, bf16[17,32,128]{2,1,0:T(8,128)(2,1)S(1)}, u32[]{:S(2)}, u32[]{:S(2)}) collective-permute-start(bf16[17,32,128]{2,1,0:T(8,128)(2,1)S(1)} %get-tuple-element.10), channel_id=1, source_target_pairs={{64,0},{65,1},{128,64},{129,65},{192,128},{193,129},{256,192},{257... | collective-permute-start | bytes 417800 | tf_op jit(solution)/shard_map/ppermute | solution.py:60
  49.2 2.1 %collective-permute-start.4 = (bf16[17,32,128]{2,1,0:T(8,128)(2,1)S(1)}, bf16[17,32,128]{2,1,0:T(8,128)(2,1)S(1)}, u32[]{:S(2)}, u32[]{:S(2)}) collective-permute-start(bf16[17,32,128]{2,1,0:T(8,128)(2,1)S(1)} %get-tuple-element.10), channel_id=1, source_target_pairs={{65,0},{64,1},{129,64},{128,65},{193,128},{192,129},{257,192},{256... | collective-permute-start | bytes 417800 | tf_op jit(solution)/shard_map/ppermute | solution.py:60
  51.4 0.0 collective-permute-done
  51.4 3.3 %collective-permute-done.1 = bf16[17,32,128]{2,1,0:T(8,128)(2,1)S(1)} collective-permute-done((bf16[17,32,128]{2,1,0:T(8,128)(2,1)S(1)}, bf16[17,32,128]{2,1,0:T(8,128)(2,1)S(1)}, u32[]{:S(2)}, u32[]{:S(2)}) %collective-permute-start.1) | collective-permute-done | bytes 139296 | tf_op jit(solution)/shard_map/ppermute | solution.py:60
  54.7 0.0 collective-permute-done.2
  54.7 2.4 %collective-permute-done.4 = bf16[17,32,128]{2,1,0:T(8,128)(2,1)S(1)} collective-permute-done((bf16[17,32,128]{2,1,0:T(8,128)(2,1)S(1)}, bf16[17,32,128]{2,1,0:T(8,128)(2,1)S(1)}, u32[]{:S(2)}, u32[]{:S(2)}) %collective-permute-start.4) | collective-permute-done | bytes 139296 | tf_op jit(solution)/shard_map/ppermute | solution.py:60
  57.0 0.0 collective-permute-done.3
  57.0 0.3 broadcast_select_fusion.1
  57.4 0.1 pad_maximum_fusion
  57.5 0.1 constant_dynamic-slice_fusion.2.x_ref
  57.6 6.7 %shard_map.46 = f32[1024,256]{1,0:T(8,128)S(1)} custom-call(bf16[1040,512]{1,0:T(8,128)(2,1)S(1)} %constant_dynamic-slice_fusion.2.x_ref, bf16[16,512,256]{2,1,0:T(8,128)(2,1)} %w_ref.1, s32[16,8,256]{2,1,0:T(8,128)S(1)} %pad_convert_fusion.m_ref), custom_call_target="tpu_custom_call" | custom-call | flops 4294967296 | bytes 6307840 | tf_op jit(solution)/shard_map/pallas_call | solution.py:128
  64.2 0.1 select_bitcast_fusion
  64.3 2.0 %collective-permute-start.5 = (f32[32,16,256]{2,1,0:T(8,128)S(1)}, f32[32,16,256]{2,1,0:T(8,128)S(1)}, u32[]{:S(2)}, u32[]{:S(2)}) collective-permute-start(f32[32,16,256]{2,1,0:T(8,128)S(1)} %select_bitcast_fusion), channel_id=1, source_target_pairs={{0,1},{1,0},{2,3},{3,2},{4,5},{5,4},{6,7},{7,6},{8,9},{9,8},{10,11... | collective-permute-start | bytes 1572872 | tf_op jit(solution)/shard_map/ppermute | solution.py:45
  66.4 1.7 %collective-permute-done.5 = f32[32,16,256]{2,1,0:T(8,128)S(1)} collective-permute-done((f32[32,16,256]{2,1,0:T(8,128)S(1)}, f32[32,16,256]{2,1,0:T(8,128)S(1)}, u32[]{:S(2)}, u32[]{:S(2)}) %collective-permute-start.5) | collective-permute-done | bytes 524320 | tf_op jit(solution)/shard_map/ppermute | solution.py:45
  68.1 0.1 fusion.1
  68.3 24.4 %all_to_all.10 = f32[32,16,256]{2,1,0:T(8,128)S(1)} all-to-all(f32[32,16,256]{2,1,0:T(8,128)S(1)} %fusion.1), channel_id=1, replica_groups=mesh['band'=8,'y'=8,'zh'=4,'core'=2] {'y','zh'}, dimensions={0} | all-to-all | bytes 1048576 | tf_op jit(solution)/shard_map/all_to_all | solution.py:90
  92.7 0.6 reduce_sum.9
  (5 shorter events, 0.1 us)
Async XLA Ops:
  0.0 17.8 %copy-start = (s32[256,2]{0,1:T(2,128)S(1)}, s32[256,2]{0,1:T(2,128)}, u32[]{:S(2)}) copy-start(s32[256,2]{0,1:T(2,128)} %param.7) | copy-start | bytes 6148
  0.0 17.8 %copy-start.1 = (s32[256]{0:T(256)S(1)}, s32[256]{0:T(256)}, u32[]{:S(2)}) copy-start(s32[256]{0:T(256)} %param.6) | copy-start | bytes 3076
  1.6 35.6 %all-to-all-start = ((bf16[32,32,256]{2,1,0:T(8,128)(2,1)}), bf16[32,32,256]{2,1,0:T(8,128)(2,1)S(1)}, u32[]{:S(2)}, u32[]{:S(2)}) async-start(bf16[32,32,256]{2,1,0:T(8,128)(2,1)} %broadcast_in_dim.2), calls=%async_computation | async-start | bytes 1048576 | tf_op jit(solution)/shard_map/all_to_all | solution.py:67
  37.2 19.8 %collective-permute-start.3 = (bf16[17,32,256]{2,1,0:T(8,128)(2,1)S(1)}, bf16[17,32,256]{2,1,0:T(8,128)(2,1)S(1)}, u32[]{:S(2)}, u32[]{:S(2)}) collective-permute-start(bf16[17,32,256]{2,1,0:T(8,128)(2,1)S(1)} %constant_dynamic-slice_fusion.3), channel_id=1, source_target_pairs={{0,1},{1,0},{2,3},{3,2},{4,5},{5,4},{6,7},{7,6},{8,9},{9,8},{10,11... | collective-permute-start | bytes 835592 | tf_op jit(solution)/shard_map/ppermute | solution.py:45
  39.2 12.1 %collective-permute-start = (bf16[17,32,128]{2,1,0:T(8,128)(2,1)S(1)}, bf16[17,32,128]{2,1,0:T(8,128)(2,1)S(1)}, u32[]{:S(2)}, u32[]{:S(2)}) collective-permute-start(bf16[17,32,128]{2,1,0:T(8,128)(2,1)S(1)} %get-tuple-element.9), channel_id=1, source_target_pairs={{0,64},{1,65},{64,128},{65,129},{128,192},{129,193},{192,256},{193... | collective-permute-start | bytes 417800 | tf_op jit(solution)/shard_map/ppermute | solution.py:59
  42.6 12.1 %collective-permute-start.2 = (bf16[17,32,128]{2,1,0:T(8,128)(2,1)S(1)}, bf16[17,32,128]{2,1,0:T(8,128)(2,1)S(1)}, u32[]{:S(2)}, u32[]{:S(2)}) collective-permute-start(bf16[17,32,128]{2,1,0:T(8,128)(2,1)S(1)} %get-tuple-element.9), channel_id=1, source_target_pairs={{0,65},{1,64},{64,129},{65,128},{128,193},{129,192},{192,257},{193... | collective-permute-start | bytes 417800 | tf_op jit(solution)/shard_map/ppermute | solution.py:59
  45.8 8.8 %collective-permute-start.1 = (bf16[17,32,128]{2,1,0:T(8,128)(2,1)S(1)}, bf16[17,32,128]{2,1,0:T(8,128)(2,1)S(1)}, u32[]{:S(2)}, u32[]{:S(2)}) collective-permute-start(bf16[17,32,128]{2,1,0:T(8,128)(2,1)S(1)} %get-tuple-element.10), channel_id=1, source_target_pairs={{64,0},{65,1},{128,64},{129,65},{192,128},{193,129},{256,192},{257... | collective-permute-start | bytes 417800 | tf_op jit(solution)/shard_map/ppermute | solution.py:60
  49.2 7.9 %collective-permute-start.4 = (bf16[17,32,128]{2,1,0:T(8,128)(2,1)S(1)}, bf16[17,32,128]{2,1,0:T(8,128)(2,1)S(1)}, u32[]{:S(2)}, u32[]{:S(2)}) collective-permute-start(bf16[17,32,128]{2,1,0:T(8,128)(2,1)S(1)} %get-tuple-element.10), channel_id=1, source_target_pairs={{65,0},{64,1},{129,64},{128,65},{193,128},{192,129},{257,192},{256... | collective-permute-start | bytes 417800 | tf_op jit(solution)/shard_map/ppermute | solution.py:60
  64.3 3.8 %collective-permute-start.5 = (f32[32,16,256]{2,1,0:T(8,128)S(1)}, f32[32,16,256]{2,1,0:T(8,128)S(1)}, u32[]{:S(2)}, u32[]{:S(2)}) collective-permute-start(f32[32,16,256]{2,1,0:T(8,128)S(1)} %select_bitcast_fusion), channel_id=1, source_target_pairs={{0,1},{1,0},{2,3},{3,2},{4,5},{5,4},{6,7},{7,6},{8,9},{9,8},{10,11... | collective-permute-start | bytes 1572872 | tf_op jit(solution)/shard_map/ppermute | solution.py:45

commit v11 on v9

--- a/solution.py
+++ b/solution.py
@@ -55,9 +55,27 @@
     return jnp.concatenate([below, cells, above], axis=-1)
 
 
+def copies_kernel(x_ref, o_ref):
+    for c in range(o_ref.shape[0]):
+        o_ref[c] = x_ref[...]
+
+
+def copies(x, count):
+    vmem = pl.BlockSpec(memory_space=pltpu.VMEM)
+    return pl.pallas_call(
+        copies_kernel,
+        out_shape=jax.ShapeDtypeStruct((count,) + x.shape, x.dtype),
+        in_specs=[vmem],
+        out_specs=vmem,
+        cost_estimate=pl.CostEstimate(
+            flops=0, transcendentals=0, bytes_accessed=(count + 1) * x.size * 2
+        ),
+    )(x)
+
+
 def gather_window(x, base, length, align, width):
     chips = lax.axis_size("y") * lax.axis_size("zh")
-    spread = jnp.broadcast_to(x[None], (chips,) + x.shape)
+    spread = copies(x, chips)
     mine = lax.all_to_all(spread, ("y", "zh"), 0, 0, tiled=True)
     pair_rows = 2 * x.shape[0]
     span = (length + 2 * pair_rows - align - 1) // pair_rows

time: 89.2 us -> 89.3 us (level)
  the two profiles are of different devices: /device:TPU:10 before, /device:TPU:8 now
where the time goes in v11:
time: 89.3 us; the launch traced here: 88.8 us
  waiting for transfers between devices  28.4 us (32%)
  blocking collectives  25.4 us (28%)
  starting transfers between devices  24.8 us (28%)
  Pallas kernels  8.24 us (9%)
  other arithmetic  1.53 us (2%)
    all_to_all x1, blocking collectives, reduce_scatter(): return lax.all_to_all(combined, ('y', 'zh'), 0, 0, tiled=True).sum(0)  25.4 us
    all_to_all x1, waiting for transfers between devices, gather_window(): mine = lax.all_to_all(spread, ('y', 'zh'), 0, 0, tiled=True)  19.4 us
    all_to_all x1, starting transfers between devices, gather_window(): mine = lax.all_to_all(spread, ('y', 'zh'), 0, 0, tiled=True)  16.2 us
    pallas_call x1, Pallas kernels, masked_conv(): pl.pallas_call(conv_kernel, out_shape=jax.ShapeDtypeStruct((rows, ports),...  6.69 us
    ppermute x1, waiting for transfers between devices, band_halo(): lax.ppermute(head, 'band', [((i + 1) % count, i) for i in range(ends)])  4.38 us
    ppermute x2, starting transfers between devices, swap_core(): return lax.ppermute(x, 'core', [(0, 1), (1, 0)])  3.97 us
    ppermute x2, waiting for transfers between devices, swap_core(): return lax.ppermute(x, 'core', [(0, 1), (1, 0)])  3.42 us
    ppermute x1, starting transfers between devices, band_halo(): lax.ppermute(tail, 'band', [(i, (i + 1) % count) for i in range(ends)])  3.35 us
  transfers between devices with their start and end apart: 5, of which 5 were waited for; matrix products, arithmetic and copies ran while one was open for 0% of the time, Pallas kernels for 0%

profile of v11, /device:TPU:8, one launch (start us, length us, event | category | flops | bytes accessed | tf_op | source)
XLA Modules:
  0.0 88.8 jit_solution(16593906298738666381)
XLA Ops:
  0.0 0.0 copy-start
  0.0 1.6 %shard_map.46 = bf16[32,32,256]{2,1,0:T(8,128)(2,1)} custom-call(bf16[32,256]{1,0:T(8,128)(2,1)} %x_ref.1), custom_call_target="tpu_custom_call" | custom-call | bytes 540672 | tf_op jit(solution)/shard_map/pallas_call | solution.py:65
  1.6 16.2 %all-to-all-start = ((bf16[32,32,256]{2,1,0:T(8,128)(2,1)}), bf16[32,32,256]{2,1,0:T(8,128)(2,1)S(1)}, u32[]{:S(2)}, u32[]{:S(2)}) async-start(bf16[32,32,256]{2,1,0:T(8,128)(2,1)} %shard_map.46), calls=%async_computation | async-start | bytes 1048576 | tf_op jit(solution)/shard_map/all_to_all | solution.py:79
  17.8 0.0 copy-start.1
  17.8 19.4 %all-to-all-done = bf16[32,32,256]{2,1,0:T(8,128)(2,1)S(1)} async-done(((bf16[32,32,256]{2,1,0:T(8,128)(2,1)}), bf16[32,32,256]{2,1,0:T(8,128)(2,1)S(1)}, u32[]{:S(2)}, u32[]{:S(2)}) %all-to-all-start) | async-done | bytes 524320 | tf_op jit(solution)/shard_map/all_to_all | solution.py:79
  37.2 0.1 constant_dynamic-slice_fusion.1
  37.2 3.3 %collective-permute-start = (bf16[17,32,128]{2,1,0:T(8,128)(2,1)S(1)}, bf16[17,32,128]{2,1,0:T(8,128)(2,1)S(1)}, u32[]{:S(2)}, u32[]{:S(2)}) collective-permute-start(bf16[17,32,128]{2,1,0:T(8,128)(2,1)S(1)} %get-tuple-element.9), channel_id=1, source_target_pairs={{0,64},{64,128},{128,192},{192,256},{256,320},{320,384},{384,448},... | collective-permute-start | bytes 417800 | tf_op jit(solution)/shard_map/ppermute | solution.py:53
  40.6 1.3 %collective-permute-start.1 = (bf16[17,32,128]{2,1,0:T(8,128)(2,1)S(1)}, bf16[17,32,128]{2,1,0:T(8,128)(2,1)S(1)}, u32[]{:S(2)}, u32[]{:S(2)}) collective-permute-start(bf16[17,32,128]{2,1,0:T(8,128)(2,1)S(1)} %get-tuple-element.10), channel_id=1, source_target_pairs={{64,0},{128,64},{192,128},{256,192},{320,256},{384,320},{448,384},... | collective-permute-start | bytes 417800 | tf_op jit(solution)/shard_map/ppermute | solution.py:54
  41.9 0.0 copy-done
  42.0 1.2 %collective-permute-done = bf16[17,32,128]{2,1,0:T(8,128)(2,1)S(1)} collective-permute-done((bf16[17,32,128]{2,1,0:T(8,128)(2,1)S(1)}, bf16[17,32,128]{2,1,0:T(8,128)(2,1)S(1)}, u32[]{:S(2)}, u32[]{:S(2)}) %collective-permute-start) | collective-permute-done | bytes 139296 | tf_op jit(solution)/shard_map/ppermute | solution.py:53
  43.2 4.4 %collective-permute-done.1 = bf16[17,32,128]{2,1,0:T(8,128)(2,1)S(1)} collective-permute-done((bf16[17,32,128]{2,1,0:T(8,128)(2,1)S(1)}, bf16[17,32,128]{2,1,0:T(8,128)(2,1)S(1)}, u32[]{:S(2)}, u32[]{:S(2)}) %collective-permute-start.1) | collective-permute-done | bytes 139296 | tf_op jit(solution)/shard_map/ppermute | solution.py:54
  47.5 0.1 pad_maximum_fusion.1
  47.6 1.9 %collective-permute-start.2 = (bf16[17,32,512]{2,1,0:T(8,128)(2,1)S(1)}, bf16[17,32,512]{2,1,0:T(8,128)(2,1)S(1)}, u32[]{:S(2)}, u32[]{:S(2)}) collective-permute-start(bf16[17,32,512]{2,1,0:T(8,128)(2,1)S(1)} %pad_maximum_fusion.1), channel_id=1, source_target_pairs={{0,1},{1,0},{2,3},{3,2},{4,5},{5,4},{6,7},{7,6},{8,9},{9,8},{10,11... | collective-permute-start | bytes 1671176 | tf_op jit(solution)/shard_map/ppermute | solution.py:45
  49.6 0.0 copy-done.1
  49.6 0.1 broadcast_and_fusion.1
  49.7 0.1 pad_add_fusion
  49.8 1.7 %collective-permute-done.2 = bf16[17,32,512]{2,1,0:T(8,128)(2,1)S(1)} collective-permute-done((bf16[17,32,512]{2,1,0:T(8,128)(2,1)S(1)}, bf16[17,32,512]{2,1,0:T(8,128)(2,1)S(1)}, u32[]{:S(2)}, u32[]{:S(2)}) %collective-permute-start.2) | collective-permute-done | bytes 557088 | tf_op jit(solution)/shard_map/ppermute | solution.py:45
  51.5 0.2 select_bitcast_fusion.1
  51.7 0.1 pad_maximum_fusion
  51.8 0.1 copy.10
  52.0 0.1 constant_dynamic-slice_fusion.2.x_ref
  52.0 6.7 %shard_map.47 = f32[1024,256]{1,0:T(8,128)S(1)} custom-call(bf16[1040,512]{1,0:T(8,128)(2,1)S(1)} %constant_dynamic-slice_fusion.2.x_ref, bf16[16,512,256]{2,1,0:T(8,128)(2,1)} %w_ref.1, s32[16,8,256]{2,1,0:T(8,128)S(1)} %pad_convert_fusion.m_ref), custom_call_target="tpu_custom_call" | custom-call | flops 4294967296 | bytes 6307840 | tf_op jit(solution)/shard_map/pallas_call | solution.py:136
  58.7 0.1 select_bitcast_fusion.2
  58.8 2.0 %collective-permute-start.3 = (f32[32,16,256]{2,1,0:T(8,128)S(1)}, f32[32,16,256]{2,1,0:T(8,128)S(1)}, u32[]{:S(2)}, u32[]{:S(2)}) collective-permute-start(f32[32,16,256]{2,1,0:T(8,128)S(1)} %select_bitcast_fusion.2), channel_id=1, source_target_pairs={{0,1},{1,0},{2,3},{3,2},{4,5},{5,4},{6,7},{7,6},{8,9},{9,8},{10,11... | collective-permute-start | bytes 1572872 | tf_op jit(solution)/shard_map/ppermute | solution.py:45
  60.9 1.7 %collective-permute-done.3 = f32[32,16,256]{2,1,0:T(8,128)S(1)} collective-permute-done((f32[32,16,256]{2,1,0:T(8,128)S(1)}, f32[32,16,256]{2,1,0:T(8,128)S(1)}, u32[]{:S(2)}, u32[]{:S(2)}) %collective-permute-start.3) | collective-permute-done | bytes 524320 | tf_op jit(solution)/shard_map/ppermute | solution.py:45
  62.6 0.1 fusion.1
  62.8 25.4 %all_to_all.10 = f32[32,16,256]{2,1,0:T(8,128)S(1)} all-to-all(f32[32,16,256]{2,1,0:T(8,128)S(1)} %fusion.1), channel_id=1, replica_groups=mesh['band'=8,'y'=8,'zh'=4,'core'=2] {'y','zh'}, dimensions={0} | all-to-all | bytes 1048576 | tf_op jit(solution)/shard_map/all_to_all | solution.py:98
  88.2 0.6 reduce_sum.9
  (4 shorter events, 0.1 us)
Async XLA Ops:
  0.0 41.9 %copy-start = (s32[256,2]{0,1:T(2,128)S(1)}, s32[256,2]{0,1:T(2,128)}, u32[]{:S(2)}) copy-start(s32[256,2]{0,1:T(2,128)} %param.7) | copy-start | bytes 6148
  1.6 35.6 %all-to-all-start = ((bf16[32,32,256]{2,1,0:T(8,128)(2,1)}), bf16[32,32,256]{2,1,0:T(8,128)(2,1)S(1)}, u32[]{:S(2)}, u32[]{:S(2)}) async-start(bf16[32,32,256]{2,1,0:T(8,128)(2,1)} %shard_map.46), calls=%async_computation | async-start | bytes 1048576 | tf_op jit(solution)/shard_map/all_to_all | solution.py:79
  17.8 31.8 %copy-start.1 = (s32[256]{0:T(256)S(1)}, s32[256]{0:T(256)}, u32[]{:S(2)}) copy-start(s32[256]{0:T(256)} %param.6) | copy-start | bytes 3076
  37.2 5.9 %collective-permute-start = (bf16[17,32,128]{2,1,0:T(8,128)(2,1)S(1)}, bf16[17,32,128]{2,1,0:T(8,128)(2,1)S(1)}, u32[]{:S(2)}, u32[]{:S(2)}) collective-permute-start(bf16[17,32,128]{2,1,0:T(8,128)(2,1)S(1)} %get-tuple-element.9), channel_id=1, source_target_pairs={{0,64},{64,128},{128,192},{192,256},{256,320},{320,384},{384,448},... | collective-permute-start | bytes 417800 | tf_op jit(solution)/shard_map/ppermute | solution.py:53
  40.6 6.9 %collective-permute-start.1 = (bf16[17,32,128]{2,1,0:T(8,128)(2,1)S(1)}, bf16[17,32,128]{2,1,0:T(8,128)(2,1)S(1)}, u32[]{:S(2)}, u32[]{:S(2)}) collective-permute-start(bf16[17,32,128]{2,1,0:T(8,128)(2,1)S(1)} %get-tuple-element.10), channel_id=1, source_target_pairs={{64,0},{128,64},{192,128},{256,192},{320,256},{384,320},{448,384},... | collective-permute-start | bytes 417800 | tf_op jit(solution)/shard_map/ppermute | solution.py:54
  47.6 3.9 %collective-permute-start.2 = (bf16[17,32,512]{2,1,0:T(8,128)(2,1)S(1)}, bf16[17,32,512]{2,1,0:T(8,128)(2,1)S(1)}, u32[]{:S(2)}, u32[]{:S(2)}) collective-permute-start(bf16[17,32,512]{2,1,0:T(8,128)(2,1)S(1)} %pad_maximum_fusion.1), channel_id=1, source_target_pairs={{0,1},{1,0},{2,3},{3,2},{4,5},{5,4},{6,7},{7,6},{8,9},{9,8},{10,11... | collective-permute-start | bytes 1671176 | tf_op jit(solution)/shard_map/ppermute | solution.py:45
  58.8 3.8 %collective-permute-start.3 = (f32[32,16,256]{2,1,0:T(8,128)S(1)}, f32[32,16,256]{2,1,0:T(8,128)S(1)}, u32[]{:S(2)}, u32[]{:S(2)}) collective-permute-start(f32[32,16,256]{2,1,0:T(8,128)S(1)} %select_bitcast_fusion.2), channel_id=1, source_target_pairs={{0,1},{1,0},{2,3},{3,2},{4,5},{5,4},{6,7},{7,6},{8,9},{9,8},{10,11... | collective-permute-start | bytes 1572872 | tf_op jit(solution)/shard_map/ppermute | solution.py:45

commit v12 on v9

--- a/solution.py
+++ b/solution.py
@@ -1,3 +1,5 @@
+import functools
+
 import jax
 import jax.numpy as jnp
 from jax import lax
@@ -52,22 +54,28 @@
     tail = cells[..., cells.shape[-1] - width :]
     below = lax.ppermute(tail, "band", [(i, (i + 1) % count) for i in range(ends)])
     above = lax.ppermute(head, "band", [((i + 1) % count, i) for i in range(ends)])
-    return jnp.concatenate([below, cells, above], axis=-1)
+    return jnp.concatenate([below, above], axis=-1)
 
 
-def gather_window(x, base, length, align, width):
+def assemble(needed, base, first_pair, pair_rows, length):
+    other = swap_core(needed)
+    first = lax.axis_index("core") == 0
+    pair = jnp.stack([jnp.where(first, needed, other), jnp.where(first, other, needed)], 1)
+    rows = pair.reshape(-1, needed.shape[-1])
+    return lax.dynamic_slice_in_dim(rows, base - first_pair * pair_rows, length, 0)
+
+
+def split_windows(x, base, length, align, width):
     chips = lax.axis_size("y") * lax.axis_size("zh")
     spread = jnp.broadcast_to(x[None], (chips,) + x.shape)
     mine = lax.all_to_all(spread, ("y", "zh"), 0, 0, tiled=True)
     pair_rows = 2 * x.shape[0]
     span = (length + 2 * pair_rows - align - 1) // pair_rows
     first_pair = jnp.minimum(base // pair_rows, chips - span)
-    needed = band_halo(lax.dynamic_slice_in_dim(mine, first_pair, span, 0), width)
-    other = swap_core(needed)
-    first = lax.axis_index("core") == 0
-    pair = jnp.stack([jnp.where(first, needed, other), jnp.where(first, other, needed)], 1)
-    rows = pair.reshape(-1, needed.shape[-1])
-    return lax.dynamic_slice_in_dim(rows, base - first_pair * pair_rows, length, 0)
+    needed = lax.dynamic_slice_in_dim(mine, first_pair, span, 0)
+    edges = band_halo(needed, width)
+    own = assemble(needed, base, first_pair, pair_rows, length)
+    return own, lambda edges: assemble(edges, base, first_pair, pair_rows, length), edges
 
 
 def reduce_scatter(partial, n_tm):
@@ -89,19 +97,27 @@
 ROW_TILE = 512
 
 
-def conv_kernel(x_ref, w_ref, m_ref, o_ref, wm_ref):
-    taps, coupled, ports = w_ref.shape
-    half = (coupled - ports) // 2
+def conv_kernel(segments, x_ref, w_ref, m_ref, *refs):
+    if len(refs) == 3:
+        acc_ref, o_ref, wm_ref = refs
+    else:
+        acc_ref = None
+        o_ref, wm_ref = refs
+    taps = w_ref.shape[0]
+    ports = o_ref.shape[1]
     for k in range(taps):
         marks = m_ref[k]
-        for lo, hi, row in ((0, half, 0), (half, half + ports, 1), (half + ports, coupled, 2)):
+        for lo, hi, row, at in segments:
             keep = marks[row : row + 1, :] != 0
             block = w_ref[k, lo:hi, :]
-            wm_ref[k, lo:hi, :] = jnp.where(keep, block, jnp.zeros_like(block))
+            wm_ref[k, at : at + hi - lo, :] = jnp.where(keep, block, jnp.zeros_like(block))
     rows = o_ref.shape[0]
     for r in range(rows // ROW_TILE):
         start = r * ROW_TILE
-        acc = jnp.zeros((ROW_TILE, ports), jnp.float32)
+        if acc_ref is None:
+            acc = jnp.zeros((ROW_TILE, ports), jnp.float32)
+        else:
+            acc = acc_ref[start : start + ROW_TILE, :]
         for k in range(taps):
             shift = taps - k
             acc = acc + jnp.dot(
@@ -112,22 +128,25 @@
         o_ref[start : start + ROW_TILE, :] = acc
 
 
-def masked_conv(window, responses, marks, rows):
+def conv_part(window, responses, marks, rows, segments, acc=None):
     taps, coupled, ports = responses.shape
+    depth = window.shape[1]
     vmem = pl.BlockSpec(memory_space=pltpu.VMEM)
+    operands = [window, responses, marks] + ([] if acc is None else [acc])
     return pl.pallas_call(
-        conv_kernel,
+        functools.partial(conv_kernel, segments),
         out_shape=jax.ShapeDtypeStruct((rows, ports), jnp.float32),
-        in_specs=[vmem, vmem, vmem],
+        in_specs=[vmem] * len(operands),
         out_specs=vmem,
-        scratch_shapes=[pltpu.VMEM((taps, coupled, ports), responses.dtype)],
+        scratch_shapes=[pltpu.VMEM((taps, depth, ports), responses.dtype)],
+        input_output_aliases={} if acc is None else {3: 0},
         compiler_params=pltpu.CompilerParams(vmem_limit_bytes=48 * 1024 * 1024),
         cost_estimate=pl.CostEstimate(
-            flops=2 * rows * taps * coupled * ports,
+            flops=2 * rows * taps * depth * ports,
             transcendentals=0,
-            bytes_accessed=window.size * 2 + responses.size * 2 + rows * ports * 4,
+            bytes_accessed=window.size * 2 + taps * depth * ports * 2 + rows * ports * 4,
         ),
-    )(window, responses, marks)
+    )(*operands)
 
 
 def tap_marks(tap_counts, panel_links, first_tap, taps):
@@ -149,9 +168,19 @@
     me = tm_index()
     first_tap = me * tap_dev
     base = total_taps - first_tap - tap_dev
-    window = gather_window(driven_wave, base, window_len + tap_dev, tap_dev, half_width)
+    own, halo_of, edges = split_windows(driven_wave, base, window_len + tap_dev, tap_dev, half_width)
     marks = tap_marks(tap_counts, panel_links, first_tap, tap_dev)
-    partial = masked_conv(window, responses, marks, window_len)
+    ports = group_ports
+    partial = conv_part(own, responses, marks, window_len, ((half_width, half_width + ports, 1, 0),))
+    partial, edges = lax.optimization_barrier((partial, edges))
+    partial = conv_part(
+        halo_of(edges),
+        responses,
+        marks,
+        window_len,
+        ((0, half_width, 0, 0), (half_width + ports, 2 * ports, 2, half_width)),
+        partial,
+    )
     summed = reduce_scatter(partial, n_tm)
     return summed.astype(jnp.bfloat16)
 

time: 89.2 us -> 86.8 us (0.973)
  waiting for transfers between devices: 26.3 us -> 21.9 us
  starting transfers between devices: 26.9 us -> 29.5 us
  Pallas kernels: 6.69 us -> 4.74 us
  other arithmetic: 1.53 us -> 2.8 us
    ppermute x2 -> x3, starting transfers between devices: 3.96 us -> 6.61 us  [swap_core(): return lax.ppermute(x, 'core', [(0, 1), (1, 0)])]
    pallas_call x1 -> x2, Pallas kernels: 6.69 us -> 4.74 us  [conv_part(): pl.pallas_call(functools.partial(conv_kernel, segments), out_shape=jax.Sh...]
    all_to_all x1, waiting for transfers between devices: 19.4 us -> 17.8 us  [split_windows(): mine = lax.all_to_all(spread, ('y', 'zh'), 0, 0, tiled=True)]
    ppermute x1, waiting for transfers between devices: 2.45 us -> 1.44 us  [band_halo(): lax.ppermute(head, 'band', [((i + 1) % count, i) for i in range(ends)])]
    ppermute x1, waiting for transfers between devices: 1.01 us -> 0.01 us  [band_halo(): lax.ppermute(tail, 'band', [(i, (i + 1) % count) for i in range(ends)])]
    ppermute x2 -> x3, waiting for transfers between devices: 3.43 us -> 2.68 us  [swap_core(): return lax.ppermute(x, 'core', [(0, 1), (1, 0)])]
  transfers between devices with their start and end apart: 5 -> 6, of which waited for: 5 -> 4; matrix products, arithmetic and copies ran while one was open for 0% -> 2% of each run, Pallas kernels for 0% -> 0%
where the time goes in v12:
time: 86.8 us; the launch traced here: 86.3 us
  starting transfers between devices  29.5 us (34%)
  blocking collectives  24.8 us (29%)
  waiting for transfers between devices  21.9 us (25%)
  Pallas kernels  4.74 us (5%)
  other arithmetic  2.8 us (3%)
  local copies, waits for them, and re-layouts  2.23 us (3%)
    all_to_all x1, blocking collectives, reduce_scatter(): return lax.all_to_all(combined, ('y', 'zh'), 0, 0, tiled=True).sum(0)  24.8 us
    all_to_all x1, waiting for transfers between devices, split_windows(): mine = lax.all_to_all(spread, ('y', 'zh'), 0, 0, tiled=True)  17.8 us
    all_to_all x1, starting transfers between devices, split_windows(): mine = lax.all_to_all(spread, ('y', 'zh'), 0, 0, tiled=True)  16.2 us
    ppermute x3, starting transfers between devices, swap_core(): return lax.ppermute(x, 'core', [(0, 1), (1, 0)])  6.61 us
    pallas_call x2, Pallas kernels, conv_part(): pl.pallas_call(functools.partial(conv_kernel, segments), out_shape=jax.Sh...  4.74 us
    ppermute x1, starting transfers between devices, band_halo(): lax.ppermute(head, 'band', [((i + 1) % count, i) for i in range(ends)])  3.4 us
    ppermute x1, starting transfers between devices, band_halo(): lax.ppermute(tail, 'band', [(i, (i + 1) % count) for i in range(ends)])  3.34 us
    ppermute x3, waiting for transfers between devices, swap_core(): return lax.ppermute(x, 'core', [(0, 1), (1, 0)])  2.68 us
  transfers between devices with their start and end apart: 6, of which 4 were waited for; matrix products, arithmetic and copies ran while one was open for 2% of the time, Pallas kernels for 0%

profile of v12, /device:TPU:10, one launch (start us, length us, event | category | flops | bytes accessed | tf_op | source)
XLA Modules:
  0.0 86.3 jit_solution(17445128133600170755)
XLA Ops:
  0.0 1.6 %broadcast_in_dim.2 = bf16[32,32,256]{2,1,0:T(8,128)(2,1)} broadcast(bf16[32,256]{1,0:T(8,128)(2,1)} %param.4), dimensions={1,2} | broadcast | bytes 540672 | tf_op jit(solution)/shard_map/broadcast_in_dim | solution.py:70
  1.6 16.2 %all-to-all-start = ((bf16[32,32,256]{2,1,0:T(8,128)(2,1)}), bf16[32,32,256]{2,1,0:T(8,128)(2,1)S(1)}, u32[]{:S(2)}, u32[]{:S(2)}) async-start(bf16[32,32,256]{2,1,0:T(8,128)(2,1)} %broadcast_in_dim.2), calls=%async_computation | async-start | bytes 1048576 | tf_op jit(solution)/shard_map/all_to_all | solution.py:71
  17.8 0.8 compare_reduce_fusion.1
  18.6 0.8 broadcast_and_fusion.1
  19.4 17.8 %all-to-all-done = bf16[32,32,256]{2,1,0:T(8,128)(2,1)S(1)} async-done(((bf16[32,32,256]{2,1,0:T(8,128)(2,1)}), bf16[32,32,256]{2,1,0:T(8,128)(2,1)S(1)}, u32[]{:S(2)}, u32[]{:S(2)}) %all-to-all-start) | async-done | bytes 524320 | tf_op jit(solution)/shard_map/all_to_all | solution.py:71
  37.2 0.1 constant_dynamic-slice_fusion.1
  37.3 3.3 %collective-permute-start.1 = (bf16[17,32,128]{2,1,0:T(8,128)(2,1)S(1)}, bf16[17,32,128]{2,1,0:T(8,128)(2,1)S(1)}, u32[]{:S(2)}, u32[]{:S(2)}) collective-permute-start(bf16[17,32,128]{2,1,0:T(8,128)(2,1)S(1)} %get-tuple-element.15), channel_id=1, source_target_pairs={{0,64},{64,128},{128,192},{192,256},{256,320},{320,384},{384,448},... | collective-permute-start | bytes 417800 | tf_op jit(solution)/shard_map/ppermute | solution.py:55
  40.6 3.4 %collective-permute-start.2 = (bf16[17,32,128]{2,1,0:T(8,128)(2,1)S(1)}, bf16[17,32,128]{2,1,0:T(8,128)(2,1)S(1)}, u32[]{:S(2)}, u32[]{:S(2)}) collective-permute-start(bf16[17,32,128]{2,1,0:T(8,128)(2,1)S(1)} %get-tuple-element.16), channel_id=1, source_target_pairs={{64,0},{128,64},{192,128},{256,192},{320,256},{384,320},{448,384},... | collective-permute-start | bytes 417800 | tf_op jit(solution)/shard_map/ppermute | solution.py:56
  44.0 1.9 %collective-permute-start = (bf16[17,32,256]{2,1,0:T(8,128)(2,1)S(1)}, bf16[17,32,256]{2,1,0:T(8,128)(2,1)S(1)}, u32[]{:S(2)}, u32[]{:S(2)}) collective-permute-start(bf16[17,32,256]{2,1,0:T(8,128)(2,1)S(1)} %constant_dynamic-slice_fusion.4), channel_id=1, source_target_pairs={{0,1},{1,0},{2,3},{3,2},{4,5},{5,4},{6,7},{7,6},{8,9},{9,8},{10,11... | collective-permute-start | bytes 835592 | tf_op jit(solution)/shard_map/ppermute | solution.py:47
  46.0 0.1 pad_add_fusion
  46.1 0.0 copy-start
  46.1 0.0 collective-permute-done.1
  46.1 1.4 %collective-permute-done.2 = bf16[17,32,128]{2,1,0:T(8,128)(2,1)S(1)} collective-permute-done((bf16[17,32,128]{2,1,0:T(8,128)(2,1)S(1)}, bf16[17,32,128]{2,1,0:T(8,128)(2,1)S(1)}, u32[]{:S(2)}, u32[]{:S(2)}) %collective-permute-start.2) | collective-permute-done | bytes 139296 | tf_op jit(solution)/shard_map/ppermute | solution.py:56
  47.6 0.0 collective-permute-done
  47.7 0.1 pad_maximum_fusion
  47.8 0.4 copy-done
  48.3 2.4 %shard_map.46.refs_0_ = f32[1024,256]{1,0:T(8,128)S(1)} custom-call(bf16[1040,256]{1,0:T(8,128)(2,1)S(1)} %constant_dynamic-slice_fusion.3.x_ref, bf16[16,512,256]{2,1,0:T(8,128)(2,1)S(1)} %copy-done, s32[16,8,256]{2,1,0:T(8,128)S(1)} %pad_convert_fusion.m_ref), custom_call_target="tpu_custom_call" | custom-call | flops 2147483648 | bytes 3678208 | tf_op jit(solution)/shard_map/pallas_call | solution.py:136
  50.6 2.4 %collective-permute-start.3 = (bf16[17,32,256]{2,1,0:T(8,128)(2,1)S(1)}, bf16[17,32,256]{2,1,0:T(8,128)(2,1)S(1)}, u32[]{:S(2)}, u32[]{:S(2)}) collective-permute-start(bf16[17,32,256]{2,1,0:T(8,128)(2,1)S(1)} %pad_maximum_fusion.2), channel_id=1, source_target_pairs={{0,1},{1,0},{2,3},{3,2},{4,5},{5,4},{6,7},{7,6},{8,9},{9,8},{10,11... | collective-permute-start | bytes 835592 | tf_op jit(solution)/shard_map/ppermute | solution.py:47
  53.0 1.2 %collective-permute-done.3 = bf16[17,32,256]{2,1,0:T(8,128)(2,1)S(1)} collective-permute-done((bf16[17,32,256]{2,1,0:T(8,128)(2,1)S(1)}, bf16[17,32,256]{2,1,0:T(8,128)(2,1)S(1)}, u32[]{:S(2)}, u32[]{:S(2)}) %collective-permute-start.3) | collective-permute-done | bytes 278560 | tf_op jit(solution)/shard_map/ppermute | solution.py:47
  54.3 0.1 pad_maximum_fusion.1
  54.4 2.4 %shard_map.47 = f32[1024,256]{1,0:T(8,128)S(1)} custom-call(bf16[1040,256]{1,0:T(8,128)(2,1)S(1)} %constant_dynamic-slice_fusion.2.x_ref, bf16[16,512,256]{2,1,0:T(8,128)(2,1)S(1)} %copy-done, s32[16,8,256]{2,1,0:T(8,128)S(1)} %pad_convert_fusion.m_ref, f32[1024,256]{1,0:T(8,128)S(1)} %shard_map.46.refs_0_), custom_call_target="tpu_custom_call", output_to_operand_aliasing={{}: (3, {})} | custom-call | flops 2147483648 | bytes 3678208 | tf_op jit(solution)/shard_map/pallas_call | solution.py:136
  56.8 0.1 select_bitcast_fusion
  56.8 2.3 %collective-permute-start.4 = (f32[32,16,256]{2,1,0:T(8,128)S(1)}, f32[32,16,256]{2,1,0:T(8,128)S(1)}, u32[]{:S(2)}, u32[]{:S(2)}) collective-permute-start(f32[32,16,256]{2,1,0:T(8,128)S(1)} %select_bitcast_fusion), channel_id=1, source_target_pairs={{0,1},{1,0},{2,3},{3,2},{4,5},{5,4},{6,7},{7,6},{8,9},{9,8},{10,11... | collective-permute-start | bytes 1572872 | tf_op jit(solution)/shard_map/ppermute | solution.py:47
  59.1 1.5 %collective-permute-done.4 = f32[32,16,256]{2,1,0:T(8,128)S(1)} collective-permute-done((f32[32,16,256]{2,1,0:T(8,128)S(1)}, f32[32,16,256]{2,1,0:T(8,128)S(1)}, u32[]{:S(2)}, u32[]{:S(2)}) %collective-permute-start.4) | collective-permute-done | bytes 524320 | tf_op jit(solution)/shard_map/ppermute | solution.py:47
  60.6 0.2 fusion.1
  60.8 24.8 %all_to_all.10 = f32[32,16,256]{2,1,0:T(8,128)S(1)} all-to-all(f32[32,16,256]{2,1,0:T(8,128)S(1)} %fusion.1), channel_id=1, replica_groups=mesh['band'=8,'y'=8,'zh'=4,'core'=2] {'y','zh'}, dimensions={0} | all-to-all | bytes 1048576 | tf_op jit(solution)/shard_map/all_to_all | solution.py:88
  85.6 0.6 reduce_sum.9
  (9 shorter events, 0.3 us)
Async XLA Ops:
  1.6 35.6 %all-to-all-start = ((bf16[32,32,256]{2,1,0:T(8,128)(2,1)}), bf16[32,32,256]{2,1,0:T(8,128)(2,1)S(1)}, u32[]{:S(2)}, u32[]{:S(2)}) async-start(bf16[32,32,256]{2,1,0:T(8,128)(2,1)} %broadcast_in_dim.2), calls=%async_computation | async-start | bytes 1048576 | tf_op jit(solution)/shard_map/all_to_all | solution.py:71
  37.3 8.9 %collective-permute-start.1 = (bf16[17,32,128]{2,1,0:T(8,128)(2,1)S(1)}, bf16[17,32,128]{2,1,0:T(8,128)(2,1)S(1)}, u32[]{:S(2)}, u32[]{:S(2)}) collective-permute-start(bf16[17,32,128]{2,1,0:T(8,128)(2,1)S(1)} %get-tuple-element.15), channel_id=1, source_target_pairs={{0,64},{64,128},{128,192},{192,256},{256,320},{320,384},{384,448},... | collective-permute-start | bytes 417800 | tf_op jit(solution)/shard_map/ppermute | solution.py:55
  40.6 6.9 %collective-permute-start.2 = (bf16[17,32,128]{2,1,0:T(8,128)(2,1)S(1)}, bf16[17,32,128]{2,1,0:T(8,128)(2,1)S(1)}, u32[]{:S(2)}, u32[]{:S(2)}) collective-permute-start(bf16[17,32,128]{2,1,0:T(8,128)(2,1)S(1)} %get-tuple-element.16), channel_id=1, source_target_pairs={{64,0},{128,64},{192,128},{256,192},{320,256},{384,320},{448,384},... | collective-permute-start | bytes 417800 | tf_op jit(solution)/shard_map/ppermute | solution.py:56
  44.0 3.5 %collective-permute-start = (bf16[17,32,256]{2,1,0:T(8,128)(2,1)S(1)}, bf16[17,32,256]{2,1,0:T(8,128)(2,1)S(1)}, u32[]{:S(2)}, u32[]{:S(2)}) collective-permute-start(bf16[17,32,256]{2,1,0:T(8,128)(2,1)S(1)} %constant_dynamic-slice_fusion.4), channel_id=1, source_target_pairs={{0,1},{1,0},{2,3},{3,2},{4,5},{5,4},{6,7},{7,6},{8,9},{9,8},{10,11... | collective-permute-start | bytes 835592 | tf_op jit(solution)/shard_map/ppermute | solution.py:47
  46.1 2.2 %copy-start = (bf16[16,512,256]{2,1,0:T(8,128)(2,1)S(1)}, bf16[16,512,256]{2,1,0:T(8,128)(2,1)}, u32[]{:S(2)}) copy-start(bf16[16,512,256]{2,1,0:T(8,128)(2,1)} %w_ref.3) | copy-start | bytes 12582916
  50.6 3.6 %collective-permute-start.3 = (bf16[17,32,256]{2,1,0:T(8,128)(2,1)S(1)}, bf16[17,32,256]{2,1,0:T(8,128)(2,1)S(1)}, u32[]{:S(2)}, u32[]{:S(2)}) collective-permute-start(bf16[17,32,256]{2,1,0:T(8,128)(2,1)S(1)} %pad_maximum_fusion.2), channel_id=1, source_target_pairs={{0,1},{1,0},{2,3},{3,2},{4,5},{5,4},{6,7},{7,6},{8,9},{9,8},{10,11... | collective-permute-start | bytes 835592 | tf_op jit(solution)/shard_map/ppermute | solution.py:47
  56.8 3.8 %collective-permute-start.4 = (f32[32,16,256]{2,1,0:T(8,128)S(1)}, f32[32,16,256]{2,1,0:T(8,128)S(1)}, u32[]{:S(2)}, u32[]{:S(2)}) collective-permute-start(f32[32,16,256]{2,1,0:T(8,128)S(1)} %select_bitcast_fusion), channel_id=1, source_target_pairs={{0,1},{1,0},{2,3},{3,2},{4,5},{5,4},{6,7},{7,6},{8,9},{9,8},{10,11... | collective-permute-start | bytes 1572872 | tf_op jit(solution)/shard_map/ppermute | solution.py:47

commit v13 on v12

--- a/solution.py
+++ b/solution.py
@@ -57,8 +57,9 @@
     return jnp.concatenate([below, above], axis=-1)
 
 
-def assemble(needed, base, first_pair, pair_rows, length):
-    other = swap_core(needed)
+def assemble(needed, base, first_pair, pair_rows, length, other=None):
+    if other is None:
+        other = swap_core(needed)
     first = lax.axis_index("core") == 0
     pair = jnp.stack([jnp.where(first, needed, other), jnp.where(first, other, needed)], 1)
     rows = pair.reshape(-1, needed.shape[-1])
@@ -75,7 +76,7 @@
     needed = lax.dynamic_slice_in_dim(mine, first_pair, span, 0)
     edges = band_halo(needed, width)
     own = assemble(needed, base, first_pair, pair_rows, length)
-    return own, lambda edges: assemble(edges, base, first_pair, pair_rows, length), edges
+    return own, lambda edges, other: assemble(edges, base, first_pair, pair_rows, length, other), edges
 
 
 def reduce_scatter(partial, n_tm):
@@ -172,9 +173,10 @@
     marks = tap_marks(tap_counts, panel_links, first_tap, tap_dev)
     ports = group_ports
     partial = conv_part(own, responses, marks, window_len, ((half_width, half_width + ports, 1, 0),))
-    partial, edges = lax.optimization_barrier((partial, edges))
+    other_edges = swap_core(edges)
+    partial, edges, other_edges = lax.optimization_barrier((partial, edges, other_edges))
     partial = conv_part(
-        halo_of(edges),
+        halo_of(edges, other_edges),
         responses,
         marks,
         window_len,

time: 86.8 us -> 85.8 us (0.988)
  the two profiles are of different devices: /device:TPU:10 before, /device:TPU:14 now
where the time goes in v13:
time: 85.8 us; the launch traced here: 85.3 us
  starting transfers between devices  28.3 us (33%)
  blocking collectives  24.5 us (29%)
  waiting for transfers between devices  22.9 us (27%)
  Pallas kernels  4.74 us (6%)
  other arithmetic  2.76 us (3%)
  local copies, waits for them, and re-layouts  1.85 us (2%)
    all_to_all x1, blocking collectives, reduce_scatter(): return lax.all_to_all(combined, ('y', 'zh'), 0, 0, tiled=True).sum(0)  24.5 us
    all_to_all x1, waiting for transfers between devices, split_windows(): mine = lax.all_to_all(spread, ('y', 'zh'), 0, 0, tiled=True)  17.8 us
    all_to_all x1, starting transfers between devices, split_windows(): mine = lax.all_to_all(spread, ('y', 'zh'), 0, 0, tiled=True)  16.2 us
    ppermute x3, starting transfers between devices, swap_core(): return lax.ppermute(x, 'core', [(0, 1), (1, 0)])  6.24 us
    pallas_call x2, Pallas kernels, conv_part(): pl.pallas_call(functools.partial(conv_kernel, segments), out_shape=jax.Sh...  4.74 us
    ppermute x1, starting transfers between devices, band_halo(): lax.ppermute(head, 'band', [((i + 1) % count, i) for i in range(ends)])  3.61 us
    ppermute x1, waiting for transfers between devices, band_halo(): lax.ppermute(tail, 'band', [(i, (i + 1) % count) for i in range(ends)])  3.58 us
    ppermute x1, starting transfers between devices, band_halo(): lax.ppermute(tail, 'band', [(i, (i + 1) % count) for i in range(ends)])  2.24 us
  transfers between devices with their start and end apart: 6, of which 3 were waited for; matrix products, arithmetic and copies ran while one was open for 2% of the time, Pallas kernels for 3%

profile of v13, /device:TPU:14, one launch (start us, length us, event | category | flops | bytes accessed | tf_op | source)
XLA Modules:
  0.0 85.3 jit_solution(13446309757864163612)
XLA Ops:
  0.0 1.6 %broadcast_in_dim.2 = bf16[32,32,256]{2,1,0:T(8,128)(2,1)} broadcast(bf16[32,256]{1,0:T(8,128)(2,1)} %param.4), dimensions={1,2} | broadcast | bytes 540672 | tf_op jit(solution)/shard_map/broadcast_in_dim | solution.py:71
  1.6 16.2 %all-to-all-start = ((bf16[32,32,256]{2,1,0:T(8,128)(2,1)}), bf16[32,32,256]{2,1,0:T(8,128)(2,1)S(1)}, u32[]{:S(2)}, u32[]{:S(2)}) async-start(bf16[32,32,256]{2,1,0:T(8,128)(2,1)} %broadcast_in_dim.2), calls=%async_computation | async-start | bytes 1048576 | tf_op jit(solution)/shard_map/all_to_all | solution.py:72
  17.8 0.8 compare_reduce_fusion.1
  18.6 0.8 broadcast_and_fusion.1
  19.4 0.1 pad_add_fusion
  19.4 17.8 %all-to-all-done = bf16[32,32,256]{2,1,0:T(8,128)(2,1)S(1)} async-done(((bf16[32,32,256]{2,1,0:T(8,128)(2,1)}), bf16[32,32,256]{2,1,0:T(8,128)(2,1)S(1)}, u32[]{:S(2)}, u32[]{:S(2)}) %all-to-all-start) | async-done | bytes 524320 | tf_op jit(solution)/shard_map/all_to_all | solution.py:72
  37.2 0.1 constant_dynamic-slice_fusion
  37.3 3.6 %collective-permute-start.2 = (bf16[17,32,128]{2,1,0:T(8,128)(2,1)S(1)}, bf16[17,32,128]{2,1,0:T(8,128)(2,1)S(1)}, u32[]{:S(2)}, u32[]{:S(2)}) collective-permute-start(bf16[17,32,128]{2,1,0:T(8,128)(2,1)S(1)} %get-tuple-element.17), channel_id=1, source_target_pairs={{64,0},{128,64},{192,128},{256,192},{320,256},{384,320},{448,384},... | collective-permute-start | bytes 417800 | tf_op jit(solution)/shard_map/ppermute | solution.py:56
  40.9 2.2 %collective-permute-start.1 = (bf16[17,32,128]{2,1,0:T(8,128)(2,1)S(1)}, bf16[17,32,128]{2,1,0:T(8,128)(2,1)S(1)}, u32[]{:S(2)}, u32[]{:S(2)}) collective-permute-start(bf16[17,32,128]{2,1,0:T(8,128)(2,1)S(1)} %get-tuple-element.18), channel_id=1, source_target_pairs={{0,64},{64,128},{128,192},{192,256},{256,320},{320,384},{384,448},... | collective-permute-start | bytes 417800 | tf_op jit(solution)/shard_map/ppermute | solution.py:55
  43.2 1.9 %collective-permute-start = (bf16[17,32,256]{2,1,0:T(8,128)(2,1)S(1)}, bf16[17,32,256]{2,1,0:T(8,128)(2,1)S(1)}, u32[]{:S(2)}, u32[]{:S(2)}) collective-permute-start(bf16[17,32,256]{2,1,0:T(8,128)(2,1)S(1)} %constant_dynamic-slice_fusion.4), channel_id=1, source_target_pairs={{0,1},{1,0},{2,3},{3,2},{4,5},{5,4},{6,7},{7,6},{8,9},{9,8},{10,11... | collective-permute-start | bytes 835592 | tf_op jit(solution)/shard_map/ppermute | solution.py:47
  45.1 0.0 copy-start
  45.1 3.6 %collective-permute-done.1 = bf16[17,32,128]{2,1,0:T(8,128)(2,1)S(1)} collective-permute-done((bf16[17,32,128]{2,1,0:T(8,128)(2,1)S(1)}, bf16[17,32,128]{2,1,0:T(8,128)(2,1)S(1)}, u32[]{:S(2)}, u32[]{:S(2)}) %collective-permute-start.1) | collective-permute-done | bytes 139296 | tf_op jit(solution)/shard_map/ppermute | solution.py:55
  48.8 0.0 collective-permute-done.2
  48.8 1.9 %collective-permute-start.3 = (bf16[17,32,256]{2,1,0:T(8,128)(2,1)S(1)}, bf16[17,32,256]{2,1,0:T(8,128)(2,1)S(1)}, u32[]{:S(2)}, u32[]{:S(2)}) collective-permute-start(bf16[17,32,256]{2,1,0:T(8,128)(2,1)S(1)} %constant_dynamic-update-slice_fusion), channel_id=1, source_target_pairs={{0,1},{1,0},{2,3},{3,2},{4,5},{5,4},{6,7},{7,6},{8,9},{9,8},{10,11... | collective-permute-start | bytes 835592 | tf_op jit(solution)/shard_map/ppermute | solution.py:47
  50.7 0.0 collective-permute-done
  50.8 0.1 pad_maximum_fusion
  51.0 0.0 copy-done
  51.0 2.4 %shard_map.46.refs_0_ = f32[1024,256]{1,0:T(8,128)S(1)} custom-call(bf16[1040,256]{1,0:T(8,128)(2,1)S(1)} %constant_dynamic-slice_fusion.3.x_ref, bf16[16,512,256]{2,1,0:T(8,128)(2,1)S(1)} %copy-done, s32[16,8,256]{2,1,0:T(8,128)S(1)} %pad_convert_fusion.m_ref), custom_call_target="tpu_custom_call" | custom-call | flops 2147483648 | bytes 3678208 | tf_op jit(solution)/shard_map/pallas_call | solution.py:137
  53.3 0.0 collective-permute-done.3
  53.4 0.1 pad_maximum_fusion.1
  53.5 2.4 %shard_map.47 = f32[1024,256]{1,0:T(8,128)S(1)} custom-call(bf16[1040,256]{1,0:T(8,128)(2,1)S(1)} %constant_dynamic-slice_fusion.2.x_ref, bf16[16,512,256]{2,1,0:T(8,128)(2,1)S(1)} %copy-done, s32[16,8,256]{2,1,0:T(8,128)S(1)} %pad_convert_fusion.m_ref, f32[1024,256]{1,0:T(8,128)S(1)} %shard_map.46.refs_0_), custom_call_target="tpu_custom_call", output_to_operand_aliasing={{}: (3, {})} | custom-call | flops 2147483648 | bytes 3678208 | tf_op jit(solution)/shard_map/pallas_call | solution.py:137
  55.9 0.1 select_bitcast_fusion
  56.0 2.4 %collective-permute-start.4 = (f32[32,16,256]{2,1,0:T(8,128)S(1)}, f32[32,16,256]{2,1,0:T(8,128)S(1)}, u32[]{:S(2)}, u32[]{:S(2)}) collective-permute-start(f32[32,16,256]{2,1,0:T(8,128)S(1)} %select_bitcast_fusion), channel_id=1, source_target_pairs={{0,1},{1,0},{2,3},{3,2},{4,5},{5,4},{6,7},{7,6},{8,9},{9,8},{10,11... | collective-permute-start | bytes 1572872 | tf_op jit(solution)/shard_map/ppermute | solution.py:47
  58.4 1.5 %collective-permute-done.4 = f32[32,16,256]{2,1,0:T(8,128)S(1)} collective-permute-done((f32[32,16,256]{2,1,0:T(8,128)S(1)}, f32[32,16,256]{2,1,0:T(8,128)S(1)}, u32[]{:S(2)}, u32[]{:S(2)}) %collective-permute-start.4) | collective-permute-done | bytes 524320 | tf_op jit(solution)/shard_map/ppermute | solution.py:47
  59.9 0.2 fusion.1
  60.1 24.5 %all_to_all.10 = f32[32,16,256]{2,1,0:T(8,128)S(1)} all-to-all(f32[32,16,256]{2,1,0:T(8,128)S(1)} %fusion.1), channel_id=1, replica_groups=mesh['band'=8,'y'=8,'zh'=4,'core'=2] {'y','zh'}, dimensions={0} | all-to-all | bytes 1048576 | tf_op jit(solution)/shard_map/all_to_all | solution.py:89
  84.6 0.6 reduce_sum.9
  (10 shorter events, 0.3 us)
Async XLA Ops:
  1.6 35.6 %all-to-all-start = ((bf16[32,32,256]{2,1,0:T(8,128)(2,1)}), bf16[32,32,256]{2,1,0:T(8,128)(2,1)S(1)}, u32[]{:S(2)}, u32[]{:S(2)}) async-start(bf16[32,32,256]{2,1,0:T(8,128)(2,1)} %broadcast_in_dim.2), calls=%async_computation | async-start | bytes 1048576 | tf_op jit(solution)/shard_map/all_to_all | solution.py:72
  37.3 11.5 %collective-permute-start.2 = (bf16[17,32,128]{2,1,0:T(8,128)(2,1)S(1)}, bf16[17,32,128]{2,1,0:T(8,128)(2,1)S(1)}, u32[]{:S(2)}, u32[]{:S(2)}) collective-permute-start(bf16[17,32,128]{2,1,0:T(8,128)(2,1)S(1)} %get-tuple-element.17), channel_id=1, source_target_pairs={{64,0},{128,64},{192,128},{256,192},{320,256},{384,320},{448,384},... | collective-permute-start | bytes 417800 | tf_op jit(solution)/shard_map/ppermute | solution.py:56
  40.9 7.8 %collective-permute-start.1 = (bf16[17,32,128]{2,1,0:T(8,128)(2,1)S(1)}, bf16[17,32,128]{2,1,0:T(8,128)(2,1)S(1)}, u32[]{:S(2)}, u32[]{:S(2)}) collective-permute-start(bf16[17,32,128]{2,1,0:T(8,128)(2,1)S(1)} %get-tuple-element.18), channel_id=1, source_target_pairs={{0,64},{64,128},{128,192},{192,256},{256,320},{320,384},{384,448},... | collective-permute-start | bytes 417800 | tf_op jit(solution)/shard_map/ppermute | solution.py:55
  43.2 7.6 %collective-permute-start = (bf16[17,32,256]{2,1,0:T(8,128)(2,1)S(1)}, bf16[17,32,256]{2,1,0:T(8,128)(2,1)S(1)}, u32[]{:S(2)}, u32[]{:S(2)}) collective-permute-start(bf16[17,32,256]{2,1,0:T(8,128)(2,1)S(1)} %constant_dynamic-slice_fusion.4), channel_id=1, source_target_pairs={{0,1},{1,0},{2,3},{3,2},{4,5},{5,4},{6,7},{7,6},{8,9},{9,8},{10,11... | collective-permute-start | bytes 835592 | tf_op jit(solution)/shard_map/ppermute | solution.py:47
  45.1 5.8 %copy-start = (bf16[16,512,256]{2,1,0:T(8,128)(2,1)S(1)}, bf16[16,512,256]{2,1,0:T(8,128)(2,1)}, u32[]{:S(2)}) copy-start(bf16[16,512,256]{2,1,0:T(8,128)(2,1)} %w_ref.3) | copy-start | bytes 12582916
  48.8 4.5 %collective-permute-start.3 = (bf16[17,32,256]{2,1,0:T(8,128)(2,1)S(1)}, bf16[17,32,256]{2,1,0:T(8,128)(2,1)S(1)}, u32[]{:S(2)}, u32[]{:S(2)}) collective-permute-start(bf16[17,32,256]{2,1,0:T(8,128)(2,1)S(1)} %constant_dynamic-update-slice_fusion), channel_id=1, source_target_pairs={{0,1},{1,0},{2,3},{3,2},{4,5},{5,4},{6,7},{7,6},{8,9},{9,8},{10,11... | collective-permute-start | bytes 835592 | tf_op jit(solution)/shard_map/ppermute | solution.py:47
  56.0 3.9 %collective-permute-start.4 = (f32[32,16,256]{2,1,0:T(8,128)S(1)}, f32[32,16,256]{2,1,0:T(8,128)S(1)}, u32[]{:S(2)}, u32[]{:S(2)}) collective-permute-start(f32[32,16,256]{2,1,0:T(8,128)S(1)} %select_bitcast_fusion), channel_id=1, source_target_pairs={{0,1},{1,0},{2,3},{3,2},{4,5},{5,4},{6,7},{7,6},{8,9},{9,8},{10,11... | collective-permute-start | bytes 1572872 | tf_op jit(solution)/shard_map/ppermute | solution.py:47

commit v14 on v13

--- a/solution.py
+++ b/solution.py
@@ -79,13 +79,15 @@
     return own, lambda edges, other: assemble(edges, base, first_pair, pair_rows, length, other), edges
 
 
-def reduce_scatter(partial, n_tm):
-    chips = n_tm // 2
-    blocks = partial.reshape(chips, 2, partial.shape[0] // n_tm, partial.shape[1])
+def core_combine(partial, rows_per):
+    blocks = partial.reshape(-1, 2, rows_per, partial.shape[1])
     first = lax.axis_index("core") == 0
     keep = jnp.where(first, blocks[:, 0], blocks[:, 1])
     give = jnp.where(first, blocks[:, 1], blocks[:, 0])
-    combined = keep + swap_core(give)
+    return keep + swap_core(give)
+
+
+def reduce_scatter(combined):
     return lax.all_to_all(combined, ("y", "zh"), 0, 0, tiled=True).sum(0)
 
 
@@ -175,15 +177,15 @@
     partial = conv_part(own, responses, marks, window_len, ((half_width, half_width + ports, 1, 0),))
     other_edges = swap_core(edges)
     partial, edges, other_edges = lax.optimization_barrier((partial, edges, other_edges))
-    partial = conv_part(
-        halo_of(edges, other_edges),
-        responses,
-        marks,
-        window_len,
-        ((0, half_width, 0, 0), (half_width + ports, 2 * ports, 2, half_width)),
-        partial,
-    )
-    summed = reduce_scatter(partial, n_tm)
+    halo = halo_of(edges, other_edges)
+    half = window_len // 2
+    segments = ((0, half_width, 0, 0), (half_width + ports, 2 * ports, 2, half_width))
+    rows_per = window_len // n_tm
+    first_half = conv_part(halo[: half + tap_dev], responses, marks, half, segments, partial[:half])
+    combined_first = core_combine(first_half, rows_per)
+    second_half = conv_part(halo[half:], responses, marks, half, segments, partial[half:])
+    combined = jnp.concatenate([combined_first, core_combine(second_half, rows_per)], 0)
+    summed = reduce_scatter(combined)
     return summed.astype(jnp.bfloat16)
 
 

time: 85.8 us -> 88 us (1.026)
  starting transfers between devices: 28.3 us -> 30.2 us
    ppermute x3 -> x4, starting transfers between devices: 6.24 us -> 8.17 us  [swap_core(): return lax.ppermute(x, 'core', [(0, 1), (1, 0)])]
    pallas_call x2 -> x3, Pallas kernels: 4.74 us -> 5.21 us  [conv_part(): pl.pallas_call(functools.partial(conv_kernel, segments), out_shape=jax.Sh...]
  transfers between devices with their start and end apart: 6 -> 7, of which waited for: 3 -> 3; matrix products, arithmetic and copies ran while one was open for 2% -> 2% of each run, Pallas kernels for 3% -> 4%
where the time goes in v14:
time: 88 us; the launch traced here: 87.4 us
  starting transfers between devices  30.2 us (34%)
  blocking collectives  24.3 us (28%)
  waiting for transfers between devices  22.8 us (26%)
  Pallas kernels  5.21 us (6%)
  other arithmetic  2.72 us (3%)
  local copies, waits for them, and re-layouts  1.91 us (2%)
    all_to_all x1, blocking collectives, reduce_scatter(): return lax.all_to_all(combined, ('y', 'zh'), 0, 0, tiled=True).sum(0)  24.3 us
    all_to_all x1, waiting for transfers between devices, split_windows(): mine = lax.all_to_all(spread, ('y', 'zh'), 0, 0, tiled=True)  17.8 us
    all_to_all x1, starting transfers between devices, split_windows(): mine = lax.all_to_all(spread, ('y', 'zh'), 0, 0, tiled=True)  16.2 us
    ppermute x4, starting transfers between devices, swap_core(): return lax.ppermute(x, 'core', [(0, 1), (1, 0)])  8.17 us
    pallas_call x3, Pallas kernels, conv_part(): pl.pallas_call(functools.partial(conv_kernel, segments), out_shape=jax.Sh...  5.21 us
    ppermute x1, starting transfers between devices, band_halo(): lax.ppermute(head, 'band', [((i + 1) % count, i) for i in range(ends)])  3.61 us
    ppermute x1, waiting for transfers between devices, band_halo(): lax.ppermute(tail, 'band', [(i, (i + 1) % count) for i in range(ends)])  3.58 us
    ppermute x1, starting transfers between devices, band_halo(): lax.ppermute(tail, 'band', [(i, (i + 1) % count) for i in range(ends)])  2.24 us
  transfers between devices with their start and end apart: 7, of which 3 were waited for; matrix products, arithmetic and copies ran while one was open for 2% of the time, Pallas kernels for 4%

profile of v14, /device:TPU:14, one launch (start us, length us, event | category | flops | bytes accessed | tf_op | source)
XLA Modules:
  0.0 87.4 jit_solution(3885149712563983040)
XLA Ops:
  0.0 1.6 %broadcast_in_dim.2 = bf16[32,32,256]{2,1,0:T(8,128)(2,1)} broadcast(bf16[32,256]{1,0:T(8,128)(2,1)} %param.4), dimensions={1,2} | broadcast | bytes 540672 | tf_op jit(solution)/shard_map/broadcast_in_dim | solution.py:71
  1.6 16.2 %all-to-all-start = ((bf16[32,32,256]{2,1,0:T(8,128)(2,1)}), bf16[32,32,256]{2,1,0:T(8,128)(2,1)S(1)}, u32[]{:S(2)}, u32[]{:S(2)}) async-start(bf16[32,32,256]{2,1,0:T(8,128)(2,1)} %broadcast_in_dim.2), calls=%async_computation | async-start | bytes 1048576 | tf_op jit(solution)/shard_map/all_to_all | solution.py:72
  17.8 0.8 compare_reduce_fusion.1
  18.6 0.8 broadcast_and_fusion.1
  19.4 0.1 pad_add_fusion
  19.4 17.8 %all-to-all-done = bf16[32,32,256]{2,1,0:T(8,128)(2,1)S(1)} async-done(((bf16[32,32,256]{2,1,0:T(8,128)(2,1)}), bf16[32,32,256]{2,1,0:T(8,128)(2,1)S(1)}, u32[]{:S(2)}, u32[]{:S(2)}) %all-to-all-start) | async-done | bytes 524320 | tf_op jit(solution)/shard_map/all_to_all | solution.py:72
  37.2 0.1 constant_dynamic-slice_fusion.1
  37.2 3.6 %collective-permute-start.2 = (bf16[17,32,128]{2,1,0:T(8,128)(2,1)S(1)}, bf16[17,32,128]{2,1,0:T(8,128)(2,1)S(1)}, u32[]{:S(2)}, u32[]{:S(2)}) collective-permute-start(bf16[17,32,128]{2,1,0:T(8,128)(2,1)S(1)} %get-tuple-element.21), channel_id=1, source_target_pairs={{64,0},{128,64},{192,128},{256,192},{320,256},{384,320},{448,384},... | collective-permute-start | bytes 417800 | tf_op jit(solution)/shard_map/ppermute | solution.py:56
  40.9 2.2 %collective-permute-start.1 = (bf16[17,32,128]{2,1,0:T(8,128)(2,1)S(1)}, bf16[17,32,128]{2,1,0:T(8,128)(2,1)S(1)}, u32[]{:S(2)}, u32[]{:S(2)}) collective-permute-start(bf16[17,32,128]{2,1,0:T(8,128)(2,1)S(1)} %get-tuple-element.22), channel_id=1, source_target_pairs={{0,64},{64,128},{128,192},{192,256},{256,320},{320,384},{384,448},... | collective-permute-start | bytes 417800 | tf_op jit(solution)/shard_map/ppermute | solution.py:55
  43.1 1.9 %collective-permute-start = (bf16[17,32,256]{2,1,0:T(8,128)(2,1)S(1)}, bf16[17,32,256]{2,1,0:T(8,128)(2,1)S(1)}, u32[]{:S(2)}, u32[]{:S(2)}) collective-permute-start(bf16[17,32,256]{2,1,0:T(8,128)(2,1)S(1)} %constant_dynamic-slice_fusion.5), channel_id=1, source_target_pairs={{0,1},{1,0},{2,3},{3,2},{4,5},{5,4},{6,7},{7,6},{8,9},{9,8},{10,11... | collective-permute-start | bytes 835592 | tf_op jit(solution)/shard_map/ppermute | solution.py:47
  45.1 0.0 copy-start
  45.1 3.6 %collective-permute-done.1 = bf16[17,32,128]{2,1,0:T(8,128)(2,1)S(1)} collective-permute-done((bf16[17,32,128]{2,1,0:T(8,128)(2,1)S(1)}, bf16[17,32,128]{2,1,0:T(8,128)(2,1)S(1)}, u32[]{:S(2)}, u32[]{:S(2)}) %collective-permute-start.1) | collective-permute-done | bytes 139296 | tf_op jit(solution)/shard_map/ppermute | solution.py:55
  48.7 0.0 collective-permute-done.2
  48.8 1.9 %collective-permute-start.3 = (bf16[17,32,256]{2,1,0:T(8,128)(2,1)S(1)}, bf16[17,32,256]{2,1,0:T(8,128)(2,1)S(1)}, u32[]{:S(2)}, u32[]{:S(2)}) collective-permute-start(bf16[17,32,256]{2,1,0:T(8,128)(2,1)S(1)} %constant_dynamic-update-slice_fusion), channel_id=1, source_target_pairs={{0,1},{1,0},{2,3},{3,2},{4,5},{5,4},{6,7},{7,6},{8,9},{9,8},{10,11... | collective-permute-start | bytes 835592 | tf_op jit(solution)/shard_map/ppermute | solution.py:47
  50.7 0.0 collective-permute-done
  50.8 0.1 pad_maximum_fusion
  51.0 0.0 copy-done
  51.0 2.4 %shard_map.46 = f32[1024,256]{1,0:T(8,128)S(1)} custom-call(bf16[1040,256]{1,0:T(8,128)(2,1)S(1)} %constant_dynamic-slice_fusion.4.x_ref, bf16[16,512,256]{2,1,0:T(8,128)(2,1)S(1)} %copy-done, s32[16,8,256]{2,1,0:T(8,128)S(1)} %pad_convert_fusion.m_ref), custom_call_target="tpu_custom_call" | custom-call | flops 2147483648 | bytes 3678208 | tf_op jit(solution)/shard_map/pallas_call | solution.py:139
  53.3 0.0 collective-permute-done.3
  53.4 0.1 fusion.2
  53.5 0.1 pad_maximum_fusion.1
  53.6 1.4 %shard_map.48 = f32[512,256]{1,0:T(8,128)S(1)} custom-call(bf16[528,256]{1,0:T(8,128)(2,1)S(1)} %get-tuple-element.16.x_ref, bf16[16,512,256]{2,1,0:T(8,128)(2,1)S(1)} %copy-done, s32[16,8,256]{2,1,0:T(8,128)S(1)} %pad_convert_fusion.m_ref, f32[512,256]{1,0:T(8,128)S(1)} %get-tuple-element.14.refs_0_), custom_call_target="tpu_custom_call", output_to_operand_aliasing={{}: (3, {})} | custom-call | flops 1073741824 | bytes 2891776 | tf_op jit(solution)/shard_map/pallas_call | solution.py:139
  55.1 2.4 %collective-permute-start.5 = (f32[16,16,256]{2,1,0:T(8,128)S(1)}, f32[16,16,256]{2,1,0:T(8,128)S(1)}, u32[]{:S(2)}, u32[]{:S(2)}) collective-permute-start(f32[16,16,256]{2,1,0:T(8,128)S(1)} %select_bitcast_fusion.4), channel_id=1, source_target_pairs={{0,1},{1,0},{2,3},{3,2},{4,5},{5,4},{6,7},{7,6},{8,9},{9,8},{10,11... | collective-permute-start | bytes 786440 | tf_op jit(solution)/shard_map/ppermute | solution.py:47
  57.5 1.4 %shard_map.47 = f32[512,256]{1,0:T(8,128)S(1)} custom-call(bf16[528,256]{1,0:T(8,128)(2,1)S(1)} %get-tuple-element.15.x_ref, bf16[16,512,256]{2,1,0:T(8,128)(2,1)S(1)} %copy-done, s32[16,8,256]{2,1,0:T(8,128)S(1)} %pad_convert_fusion.m_ref, f32[512,256]{1,0:T(8,128)S(1)} %get-tuple-element.13.refs_0_), custom_call_target="tpu_custom_call", output_to_operand_aliasing={{}: (3, {})} | custom-call | flops 1073741824 | bytes 2891776 | tf_op jit(solution)/shard_map/pallas_call | solution.py:139
  58.9 1.9 %collective-permute-start.4 = (f32[16,16,256]{2,1,0:T(8,128)S(1)}, f32[16,16,256]{2,1,0:T(8,128)S(1)}, u32[]{:S(2)}, u32[]{:S(2)}) collective-permute-start(f32[16,16,256]{2,1,0:T(8,128)S(1)} %select_bitcast_fusion.5), channel_id=1, source_target_pairs={{0,1},{1,0},{2,3},{3,2},{4,5},{5,4},{6,7},{7,6},{8,9},{9,8},{10,11... | collective-permute-start | bytes 786440 | tf_op jit(solution)/shard_map/ppermute | solution.py:47
  60.9 0.0 collective-permute-done.5
  60.9 0.1 fusion.1
  60.9 1.4 %collective-permute-done.4 = f32[16,16,256]{2,1,0:T(8,128)S(1)} collective-permute-done((f32[16,16,256]{2,1,0:T(8,128)S(1)}, f32[16,16,256]{2,1,0:T(8,128)S(1)}, u32[]{:S(2)}, u32[]{:S(2)}) %collective-permute-start.4) | collective-permute-done | bytes 262176 | tf_op jit(solution)/shard_map/ppermute | solution.py:47
  62.4 0.1 bitcast_add_fusion
  62.5 24.3 %all_to_all.10 = f32[32,16,256]{2,1,0:T(8,128)S(1)} all-to-all(f32[32,16,256]{2,1,0:T(8,128)S(1)} %pad_maximum_fusion.2), channel_id=1, replica_groups=mesh['band'=8,'y'=8,'zh'=4,'core'=2] {'y','zh'}, dimensions={0} | all-to-all | bytes 1048576 | tf_op jit(solution)/shard_map/all_to_all | solution.py:91
  86.8 0.6 reduce_sum.9
  (13 shorter events, 0.4 us)
Async XLA Ops:
  1.6 35.6 %all-to-all-start = ((bf16[32,32,256]{2,1,0:T(8,128)(2,1)}), bf16[32,32,256]{2,1,0:T(8,128)(2,1)S(1)}, u32[]{:S(2)}, u32[]{:S(2)}) async-start(bf16[32,32,256]{2,1,0:T(8,128)(2,1)} %broadcast_in_dim.2), calls=%async_computation | async-start | bytes 1048576 | tf_op jit(solution)/shard_map/all_to_all | solution.py:72
  37.2 11.5 %collective-permute-start.2 = (bf16[17,32,128]{2,1,0:T(8,128)(2,1)S(1)}, bf16[17,32,128]{2,1,0:T(8,128)(2,1)S(1)}, u32[]{:S(2)}, u32[]{:S(2)}) collective-permute-start(bf16[17,32,128]{2,1,0:T(8,128)(2,1)S(1)} %get-tuple-element.21), channel_id=1, source_target_pairs={{64,0},{128,64},{192,128},{256,192},{320,256},{384,320},{448,384},... | collective-permute-start | bytes 417800 | tf_op jit(solution)/shard_map/ppermute | solution.py:56
  40.9 7.8 %collective-permute-start.1 = (bf16[17,32,128]{2,1,0:T(8,128)(2,1)S(1)}, bf16[17,32,128]{2,1,0:T(8,128)(2,1)S(1)}, u32[]{:S(2)}, u32[]{:S(2)}) collective-permute-start(bf16[17,32,128]{2,1,0:T(8,128)(2,1)S(1)} %get-tuple-element.22), channel_id=1, source_target_pairs={{0,64},{64,128},{128,192},{192,256},{256,320},{320,384},{384,448},... | collective-permute-start | bytes 417800 | tf_op jit(solution)/shard_map/ppermute | solution.py:55
  43.1 7.6 %collective-permute-start = (bf16[17,32,256]{2,1,0:T(8,128)(2,1)S(1)}, bf16[17,32,256]{2,1,0:T(8,128)(2,1)S(1)}, u32[]{:S(2)}, u32[]{:S(2)}) collective-permute-start(bf16[17,32,256]{2,1,0:T(8,128)(2,1)S(1)} %constant_dynamic-slice_fusion.5), channel_id=1, source_target_pairs={{0,1},{1,0},{2,3},{3,2},{4,5},{5,4},{6,7},{7,6},{8,9},{9,8},{10,11... | collective-permute-start | bytes 835592 | tf_op jit(solution)/shard_map/ppermute | solution.py:47
  45.1 5.8 %copy-start = (bf16[16,512,256]{2,1,0:T(8,128)(2,1)S(1)}, bf16[16,512,256]{2,1,0:T(8,128)(2,1)}, u32[]{:S(2)}) copy-start(bf16[16,512,256]{2,1,0:T(8,128)(2,1)} %w_ref.5) | copy-start | bytes 12582916
  48.8 4.5 %collective-permute-start.3 = (bf16[17,32,256]{2,1,0:T(8,128)(2,1)S(1)}, bf16[17,32,256]{2,1,0:T(8,128)(2,1)S(1)}, u32[]{:S(2)}, u32[]{:S(2)}) collective-permute-start(bf16[17,32,256]{2,1,0:T(8,128)(2,1)S(1)} %constant_dynamic-update-slice_fusion), channel_id=1, source_target_pairs={{0,1},{1,0},{2,3},{3,2},{4,5},{5,4},{6,7},{7,6},{8,9},{9,8},{10,11... | collective-permute-start | bytes 835592 | tf_op jit(solution)/shard_map/ppermute | solution.py:47
  55.1 5.8 %collective-permute-start.5 = (f32[16,16,256]{2,1,0:T(8,128)S(1)}, f32[16,16,256]{2,1,0:T(8,128)S(1)}, u32[]{:S(2)}, u32[]{:S(2)}) collective-permute-start(f32[16,16,256]{2,1,0:T(8,128)S(1)} %select_bitcast_fusion.4), channel_id=1, source_target_pairs={{0,1},{1,0},{2,3},{3,2},{4,5},{5,4},{6,7},{7,6},{8,9},{9,8},{10,11... | collective-permute-start | bytes 786440 | tf_op jit(solution)/shard_map/ppermute | solution.py:47
  58.9 3.4 %collective-permute-start.4 = (f32[16,16,256]{2,1,0:T(8,128)S(1)}, f32[16,16,256]{2,1,0:T(8,128)S(1)}, u32[]{:S(2)}, u32[]{:S(2)}) collective-permute-start(f32[16,16,256]{2,1,0:T(8,128)S(1)} %select_bitcast_fusion.5), channel_id=1, source_target_pairs={{0,1},{1,0},{2,3},{3,2},{4,5},{5,4},{6,7},{7,6},{8,9},{9,8},{10,11... | collective-permute-start | bytes 786440 | tf_op jit(solution)/shard_map/ppermute | solution.py:47

commit v15 on v13

--- a/solution.py
+++ b/solution.py
@@ -74,9 +74,14 @@
     span = (length + 2 * pair_rows - align - 1) // pair_rows
     first_pair = jnp.minimum(base // pair_rows, chips - span)
     needed = lax.dynamic_slice_in_dim(mine, first_pair, span, 0)
-    edges = band_halo(needed, width)
-    own = assemble(needed, base, first_pair, pair_rows, length)
-    return own, lambda edges, other: assemble(edges, base, first_pair, pair_rows, length, other), edges
+    other = swap_core(needed)
+    first = lax.axis_index("core") == 0
+    pair = jnp.stack([jnp.where(first, needed, other), jnp.where(first, other, needed)], 1)
+    rows = pair.reshape(-1, needed.shape[-1])
+    offset = base - first_pair * pair_rows
+    own = lax.dynamic_slice_in_dim(rows, offset, length, 0)
+    edges = band_halo(rows, width)
+    return own, lambda edges: lax.dynamic_slice_in_dim(edges, offset, length, 0), edges
 
 
 def reduce_scatter(partial, n_tm):
@@ -173,10 +178,9 @@
     marks = tap_marks(tap_counts, panel_links, first_tap, tap_dev)
     ports = group_ports
     partial = conv_part(own, responses, marks, window_len, ((half_width, half_width + ports, 1, 0),))
-    other_edges = swap_core(edges)
-    partial, edges, other_edges = lax.optimization_barrier((partial, edges, other_edges))
+    partial, edges = lax.optimization_barrier((partial, edges))
     partial = conv_part(
-        halo_of(edges, other_edges),
+        halo_of(edges),
         responses,
         marks,
         window_len,

time: 85.8 us -> 90.9 us (1.059)
  the two profiles are of different devices: /device:TPU:14 before, /device:TPU:8 now
where the time goes in v15:
time: 90.9 us; the launch traced here: 90.4 us
  waiting for transfers between devices  32.9 us (36%)
  starting transfers between devices  24.9 us (27%)
  blocking collectives  24.6 us (27%)
  Pallas kernels  4.75 us (5%)
  local copies, waits for them, and re-layouts  1.76 us (2%)
  other arithmetic  1.28 us (1%)
    all_to_all x1, blocking collectives, reduce_scatter(): return lax.all_to_all(combined, ('y', 'zh'), 0, 0, tiled=True).sum(0)  24.6 us
    all_to_all x1, waiting for transfers between devices, split_windows(): mine = lax.all_to_all(spread, ('y', 'zh'), 0, 0, tiled=True)  19.4 us
    all_to_all x1, starting transfers between devices, split_windows(): mine = lax.all_to_all(spread, ('y', 'zh'), 0, 0, tiled=True)  16.2 us
    ppermute x1, waiting for transfers between devices, band_halo(): lax.ppermute(head, 'band', [((i + 1) % count, i) for i in range(ends)])  7.94 us
    pallas_call x2, Pallas kernels, conv_part(): pl.pallas_call(functools.partial(conv_kernel, segments), out_shape=jax.Sh...  4.75 us
    ppermute x2, starting transfers between devices, swap_core(): return lax.ppermute(x, 'core', [(0, 1), (1, 0)])  3.84 us
    ppermute x1, starting transfers between devices, band_halo(): lax.ppermute(tail, 'band', [(i, (i + 1) % count) for i in range(ends)])  3.62 us
    ppermute x2, waiting for transfers between devices, swap_core(): return lax.ppermute(x, 'core', [(0, 1), (1, 0)])  3.15 us
  transfers between devices with their start and end apart: 5, of which 5 were waited for; matrix products, arithmetic and copies ran while one was open for 0% of the time, Pallas kernels for 3%

profile of v15, /device:TPU:8, one launch (start us, length us, event | category | flops | bytes accessed | tf_op | source)
XLA Modules:
  0.0 90.4 jit_solution(5447598832900159343)
XLA Ops:
  0.0 0.0 copy-start.1
  0.0 0.0 copy-start.2
  0.0 1.6 %broadcast_in_dim.2 = bf16[32,32,256]{2,1,0:T(8,128)(2,1)} broadcast(bf16[32,256]{1,0:T(8,128)(2,1)} %param.4), dimensions={1,2} | broadcast | bytes 540672 | tf_op jit(solution)/shard_map/broadcast_in_dim | solution.py:71
  1.6 16.2 %all-to-all-start = ((bf16[32,32,256]{2,1,0:T(8,128)(2,1)}), bf16[32,32,256]{2,1,0:T(8,128)(2,1)S(1)}, u32[]{:S(2)}, u32[]{:S(2)}) async-start(bf16[32,32,256]{2,1,0:T(8,128)(2,1)} %broadcast_in_dim.2), calls=%async_computation | async-start | bytes 1048576 | tf_op jit(solution)/shard_map/all_to_all | solution.py:72
  17.8 0.0 copy-done.1
  17.9 19.4 %all-to-all-done = bf16[32,32,256]{2,1,0:T(8,128)(2,1)S(1)} async-done(((bf16[32,32,256]{2,1,0:T(8,128)(2,1)}), bf16[32,32,256]{2,1,0:T(8,128)(2,1)S(1)}, u32[]{:S(2)}, u32[]{:S(2)}) %all-to-all-start) | async-done | bytes 524320 | tf_op jit(solution)/shard_map/all_to_all | solution.py:72
  37.3 1.9 %collective-permute-start = (bf16[17,32,256]{2,1,0:T(8,128)(2,1)S(1)}, bf16[17,32,256]{2,1,0:T(8,128)(2,1)S(1)}, u32[]{:S(2)}, u32[]{:S(2)}) collective-permute-start(bf16[17,32,256]{2,1,0:T(8,128)(2,1)S(1)} %constant_dynamic-slice_fusion.2), channel_id=1, source_target_pairs={{0,1},{1,0},{2,3},{3,2},{4,5},{5,4},{6,7},{7,6},{8,9},{9,8},{10,11... | collective-permute-start | bytes 835592 | tf_op jit(solution)/shard_map/ppermute | solution.py:47
  39.2 0.0 copy-done.2
  39.2 0.1 broadcast_and_fusion.1
  39.3 0.1 pad_add_fusion
  39.4 1.3 %collective-permute-done = bf16[17,32,256]{2,1,0:T(8,128)(2,1)S(1)} collective-permute-done((bf16[17,32,256]{2,1,0:T(8,128)(2,1)S(1)}, bf16[17,32,256]{2,1,0:T(8,128)(2,1)S(1)}, u32[]{:S(2)}, u32[]{:S(2)}) %collective-permute-start) | collective-permute-done | bytes 278560 | tf_op jit(solution)/shard_map/ppermute | solution.py:47
  40.7 0.0 copy-start
  40.8 0.1 pad_maximum_fusion
  40.9 3.6 %collective-permute-start.1 = (bf16[1088,128]{1,0:T(8,128)(2,1)S(1)}, bf16[1088,128]{1,0:T(8,128)(2,1)S(1)}, u32[]{:S(2)}, u32[]{:S(2)}) collective-permute-start(bf16[1088,128]{1,0:T(8,128)(2,1)S(1)} %get-tuple-element.11), channel_id=1, source_target_pairs={{0,64},{64,128},{128,192},{192,256},{256,320},{320,384},{384,448},... | collective-permute-start | bytes 835592 | tf_op jit(solution)/shard_map/ppermute | solution.py:55
  44.5 1.3 %collective-permute-start.2 = (bf16[1088,128]{1,0:T(8,128)(2,1)S(1)}, bf16[1088,128]{1,0:T(8,128)(2,1)S(1)}, u32[]{:S(2)}, u32[]{:S(2)}) collective-permute-start(bf16[1088,128]{1,0:T(8,128)(2,1)S(1)} %get-tuple-element.12), channel_id=1, source_target_pairs={{64,0},{128,64},{192,128},{256,192},{320,256},{384,320},{448,384},... | collective-permute-start | bytes 835592 | tf_op jit(solution)/shard_map/ppermute | solution.py:56
  45.8 0.0 copy-done
  45.9 2.4 %shard_map.46.refs_0_ = f32[1024,256]{1,0:T(8,128)S(1)} custom-call(bf16[1040,256]{1,0:T(8,128)(2,1)S(1)} %constant_dynamic-slice_fusion.1.x_ref, bf16[16,512,256]{2,1,0:T(8,128)(2,1)S(1)} %copy-done, s32[16,8,256]{2,1,0:T(8,128)S(1)} %pad_convert_fusion.m_ref), custom_call_target="tpu_custom_call" | custom-call | flops 2147483648 | bytes 3678208 | tf_op jit(solution)/shard_map/pallas_call | solution.py:142
  48.2 2.4 %collective-permute-done.1 = bf16[1088,128]{1,0:T(8,128)(2,1)S(1)} collective-permute-done((bf16[1088,128]{1,0:T(8,128)(2,1)S(1)}, bf16[1088,128]{1,0:T(8,128)(2,1)S(1)}, u32[]{:S(2)}, u32[]{:S(2)}) %collective-permute-start.1) | collective-permute-done | bytes 278560 | tf_op jit(solution)/shard_map/ppermute | solution.py:55
  50.7 7.9 %collective-permute-done.2 = bf16[1088,128]{1,0:T(8,128)(2,1)S(1)} collective-permute-done((bf16[1088,128]{1,0:T(8,128)(2,1)S(1)}, bf16[1088,128]{1,0:T(8,128)(2,1)S(1)}, u32[]{:S(2)}, u32[]{:S(2)}) %collective-permute-start.2) | collective-permute-done | bytes 278560 | tf_op jit(solution)/shard_map/ppermute | solution.py:56
  58.6 0.1 pad_maximum_fusion.1
  58.7 2.4 %shard_map.47 = f32[1024,256]{1,0:T(8,128)S(1)} custom-call(bf16[1040,256]{1,0:T(8,128)(2,1)S(1)} %constant_dynamic-slice_fusion.x_ref, bf16[16,512,256]{2,1,0:T(8,128)(2,1)S(1)} %copy-done, s32[16,8,256]{2,1,0:T(8,128)S(1)} %pad_convert_fusion.m_ref, f32[1024,256]{1,0:T(8,128)S(1)} %shard_map.46.refs_0_), custom_call_target="tpu_custom_call", output_to_operand_aliasing={{}: (3, {})} | custom-call | flops 2147483648 | bytes 3678208 | tf_op jit(solution)/shard_map/pallas_call | solution.py:142
  61.1 0.1 select_bitcast_fusion
  61.2 1.9 %collective-permute-start.3 = (f32[32,16,256]{2,1,0:T(8,128)S(1)}, f32[32,16,256]{2,1,0:T(8,128)S(1)}, u32[]{:S(2)}, u32[]{:S(2)}) collective-permute-start(f32[32,16,256]{2,1,0:T(8,128)S(1)} %select_bitcast_fusion), channel_id=1, source_target_pairs={{0,1},{1,0},{2,3},{3,2},{4,5},{5,4},{6,7},{7,6},{8,9},{9,8},{10,11... | collective-permute-start | bytes 1572872 | tf_op jit(solution)/shard_map/ppermute | solution.py:47
  63.1 1.9 %collective-permute-done.3 = f32[32,16,256]{2,1,0:T(8,128)S(1)} collective-permute-done((f32[32,16,256]{2,1,0:T(8,128)S(1)}, f32[32,16,256]{2,1,0:T(8,128)S(1)}, u32[]{:S(2)}, u32[]{:S(2)}) %collective-permute-start.3) | collective-permute-done | bytes 524320 | tf_op jit(solution)/shard_map/ppermute | solution.py:47
  65.0 0.2 fusion.1
  65.2 24.6 %all_to_all.10 = f32[32,16,256]{2,1,0:T(8,128)S(1)} all-to-all(f32[32,16,256]{2,1,0:T(8,128)S(1)} %fusion.1), channel_id=1, replica_groups=mesh['band'=8,'y'=8,'zh'=4,'core'=2] {'y','zh'}, dimensions={0} | all-to-all | bytes 1048576 | tf_op jit(solution)/shard_map/all_to_all | solution.py:94
  89.8 0.6 reduce_sum.9
  (8 shorter events, 0.2 us)
Async XLA Ops:
  0.0 17.8 %copy-start.1 = (s32[256,2]{0,1:T(2,128)S(1)}, s32[256,2]{0,1:T(2,128)}, u32[]{:S(2)}) copy-start(s32[256,2]{0,1:T(2,128)} %param.7) | copy-start | bytes 6148
  0.0 39.2 %copy-start.2 = (s32[256]{0:T(256)S(1)}, s32[256]{0:T(256)}, u32[]{:S(2)}) copy-start(s32[256]{0:T(256)} %param.6) | copy-start | bytes 3076
  1.6 35.6 %all-to-all-start = ((bf16[32,32,256]{2,1,0:T(8,128)(2,1)}), bf16[32,32,256]{2,1,0:T(8,128)(2,1)S(1)}, u32[]{:S(2)}, u32[]{:S(2)}) async-start(bf16[32,32,256]{2,1,0:T(8,128)(2,1)} %broadcast_in_dim.2), calls=%async_computation | async-start | bytes 1048576 | tf_op jit(solution)/shard_map/all_to_all | solution.py:72
  37.3 3.5 %collective-permute-start = (bf16[17,32,256]{2,1,0:T(8,128)(2,1)S(1)}, bf16[17,32,256]{2,1,0:T(8,128)(2,1)S(1)}, u32[]{:S(2)}, u32[]{:S(2)}) collective-permute-start(bf16[17,32,256]{2,1,0:T(8,128)(2,1)S(1)} %constant_dynamic-slice_fusion.2), channel_id=1, source_target_pairs={{0,1},{1,0},{2,3},{3,2},{4,5},{5,4},{6,7},{7,6},{8,9},{9,8},{10,11... | collective-permute-start | bytes 835592 | tf_op jit(solution)/shard_map/ppermute | solution.py:47
  40.7 5.1 %copy-start = (bf16[16,512,256]{2,1,0:T(8,128)(2,1)S(1)}, bf16[16,512,256]{2,1,0:T(8,128)(2,1)}, u32[]{:S(2)}) copy-start(bf16[16,512,256]{2,1,0:T(8,128)(2,1)} %w_ref.3) | copy-start | bytes 12582916
  40.9 9.8 %collective-permute-start.1 = (bf16[1088,128]{1,0:T(8,128)(2,1)S(1)}, bf16[1088,128]{1,0:T(8,128)(2,1)S(1)}, u32[]{:S(2)}, u32[]{:S(2)}) collective-permute-start(bf16[1088,128]{1,0:T(8,128)(2,1)S(1)} %get-tuple-element.11), channel_id=1, source_target_pairs={{0,64},{64,128},{128,192},{192,256},{256,320},{320,384},{384,448},... | collective-permute-start | bytes 835592 | tf_op jit(solution)/shard_map/ppermute | solution.py:55
  44.5 14.1 %collective-permute-start.2 = (bf16[1088,128]{1,0:T(8,128)(2,1)S(1)}, bf16[1088,128]{1,0:T(8,128)(2,1)S(1)}, u32[]{:S(2)}, u32[]{:S(2)}) collective-permute-start(bf16[1088,128]{1,0:T(8,128)(2,1)S(1)} %get-tuple-element.12), channel_id=1, source_target_pairs={{64,0},{128,64},{192,128},{256,192},{320,256},{384,320},{448,384},... | collective-permute-start | bytes 835592 | tf_op jit(solution)/shard_map/ppermute | solution.py:56
  61.2 3.8 %collective-permute-start.3 = (f32[32,16,256]{2,1,0:T(8,128)S(1)}, f32[32,16,256]{2,1,0:T(8,128)S(1)}, u32[]{:S(2)}, u32[]{:S(2)}) collective-permute-start(f32[32,16,256]{2,1,0:T(8,128)S(1)} %select_bitcast_fusion), channel_id=1, source_target_pairs={{0,1},{1,0},{2,3},{3,2},{4,5},{5,4},{6,7},{7,6},{8,9},{9,8},{10,11... | collective-permute-start | bytes 1572872 | tf_op jit(solution)/shard_map/ppermute | solution.py:47

commit v16 on v13

--- a/solution.py
+++ b/solution.py
@@ -95,7 +95,7 @@
     ) + lax.axis_index("core")
 
 
-ROW_TILE = 512
+ROW_TILE = 256
 
 
 def conv_kernel(segments, x_ref, w_ref, m_ref, *refs):

time: 85.8 us -> 85.9 us (level)
  no operation moved by 1% of the time
where the time goes in v16:
time: 85.9 us; the launch traced here: 85.3 us
  starting transfers between devices  28.3 us (33%)
  blocking collectives  24.5 us (29%)
  waiting for transfers between devices  22.9 us (27%)
  Pallas kernels  4.81 us (6%)
  other arithmetic  2.76 us (3%)
  local copies, waits for them, and re-layouts  1.85 us (2%)
    all_to_all x1, blocking collectives, reduce_scatter(): return lax.all_to_all(combined, ('y', 'zh'), 0, 0, tiled=True).sum(0)  24.5 us
    all_to_all x1, waiting for transfers between devices, split_windows(): mine = lax.all_to_all(spread, ('y', 'zh'), 0, 0, tiled=True)  17.8 us
    all_to_all x1, starting transfers between devices, split_windows(): mine = lax.all_to_all(spread, ('y', 'zh'), 0, 0, tiled=True)  16.2 us
    ppermute x3, starting transfers between devices, swap_core(): return lax.ppermute(x, 'core', [(0, 1), (1, 0)])  6.25 us
    pallas_call x2, Pallas kernels, conv_part(): pl.pallas_call(functools.partial(conv_kernel, segments), out_shape=jax.Sh...  4.81 us
    ppermute x1, starting transfers between devices, band_halo(): lax.ppermute(head, 'band', [((i + 1) % count, i) for i in range(ends)])  3.61 us
    ppermute x1, waiting for transfers between devices, band_halo(): lax.ppermute(tail, 'band', [(i, (i + 1) % count) for i in range(ends)])  3.58 us
    ppermute x1, starting transfers between devices, band_halo(): lax.ppermute(tail, 'band', [(i, (i + 1) % count) for i in range(ends)])  2.24 us
  transfers between devices with their start and end apart: 6, of which 3 were waited for; matrix products, arithmetic and copies ran while one was open for 2% of the time, Pallas kernels for 3%

profile of v16, /device:TPU:14, one launch (start us, length us, event | category | flops | bytes accessed | tf_op | source)
XLA Modules:
  0.0 85.3 jit_solution(470909028415296276)
XLA Ops:
  0.0 1.6 %broadcast_in_dim.2 = bf16[32,32,256]{2,1,0:T(8,128)(2,1)} broadcast(bf16[32,256]{1,0:T(8,128)(2,1)} %param.4), dimensions={1,2} | broadcast | bytes 540672 | tf_op jit(solution)/shard_map/broadcast_in_dim | solution.py:71
  1.6 16.2 %all-to-all-start = ((bf16[32,32,256]{2,1,0:T(8,128)(2,1)}), bf16[32,32,256]{2,1,0:T(8,128)(2,1)S(1)}, u32[]{:S(2)}, u32[]{:S(2)}) async-start(bf16[32,32,256]{2,1,0:T(8,128)(2,1)} %broadcast_in_dim.2), calls=%async_computation | async-start | bytes 1048576 | tf_op jit(solution)/shard_map/all_to_all | solution.py:72
  17.8 0.8 compare_reduce_fusion.1
  18.6 0.8 broadcast_and_fusion.1
  19.4 0.1 pad_add_fusion
  19.4 17.8 %all-to-all-done = bf16[32,32,256]{2,1,0:T(8,128)(2,1)S(1)} async-done(((bf16[32,32,256]{2,1,0:T(8,128)(2,1)}), bf16[32,32,256]{2,1,0:T(8,128)(2,1)S(1)}, u32[]{:S(2)}, u32[]{:S(2)}) %all-to-all-start) | async-done | bytes 524320 | tf_op jit(solution)/shard_map/all_to_all | solution.py:72
  37.2 0.1 constant_dynamic-slice_fusion
  37.3 3.6 %collective-permute-start.2 = (bf16[17,32,128]{2,1,0:T(8,128)(2,1)S(1)}, bf16[17,32,128]{2,1,0:T(8,128)(2,1)S(1)}, u32[]{:S(2)}, u32[]{:S(2)}) collective-permute-start(bf16[17,32,128]{2,1,0:T(8,128)(2,1)S(1)} %get-tuple-element.17), channel_id=1, source_target_pairs={{64,0},{128,64},{192,128},{256,192},{320,256},{384,320},{448,384},... | collective-permute-start | bytes 417800 | tf_op jit(solution)/shard_map/ppermute | solution.py:56
  40.9 2.2 %collective-permute-start.1 = (bf16[17,32,128]{2,1,0:T(8,128)(2,1)S(1)}, bf16[17,32,128]{2,1,0:T(8,128)(2,1)S(1)}, u32[]{:S(2)}, u32[]{:S(2)}) collective-permute-start(bf16[17,32,128]{2,1,0:T(8,128)(2,1)S(1)} %get-tuple-element.18), channel_id=1, source_target_pairs={{0,64},{64,128},{128,192},{192,256},{256,320},{320,384},{384,448},... | collective-permute-start | bytes 417800 | tf_op jit(solution)/shard_map/ppermute | solution.py:55
  43.2 1.9 %collective-permute-start = (bf16[17,32,256]{2,1,0:T(8,128)(2,1)S(1)}, bf16[17,32,256]{2,1,0:T(8,128)(2,1)S(1)}, u32[]{:S(2)}, u32[]{:S(2)}) collective-permute-start(bf16[17,32,256]{2,1,0:T(8,128)(2,1)S(1)} %constant_dynamic-slice_fusion.4), channel_id=1, source_target_pairs={{0,1},{1,0},{2,3},{3,2},{4,5},{5,4},{6,7},{7,6},{8,9},{9,8},{10,11... | collective-permute-start | bytes 835592 | tf_op jit(solution)/shard_map/ppermute | solution.py:47
  45.1 0.0 copy-start
  45.1 3.6 %collective-permute-done.1 = bf16[17,32,128]{2,1,0:T(8,128)(2,1)S(1)} collective-permute-done((bf16[17,32,128]{2,1,0:T(8,128)(2,1)S(1)}, bf16[17,32,128]{2,1,0:T(8,128)(2,1)S(1)}, u32[]{:S(2)}, u32[]{:S(2)}) %collective-permute-start.1) | collective-permute-done | bytes 139296 | tf_op jit(solution)/shard_map/ppermute | solution.py:55
  48.8 0.0 collective-permute-done.2
  48.8 1.9 %collective-permute-start.3 = (bf16[17,32,256]{2,1,0:T(8,128)(2,1)S(1)}, bf16[17,32,256]{2,1,0:T(8,128)(2,1)S(1)}, u32[]{:S(2)}, u32[]{:S(2)}) collective-permute-start(bf16[17,32,256]{2,1,0:T(8,128)(2,1)S(1)} %constant_dynamic-update-slice_fusion), channel_id=1, source_target_pairs={{0,1},{1,0},{2,3},{3,2},{4,5},{5,4},{6,7},{7,6},{8,9},{9,8},{10,11... | collective-permute-start | bytes 835592 | tf_op jit(solution)/shard_map/ppermute | solution.py:47
  50.7 0.0 collective-permute-done
  50.8 0.1 pad_maximum_fusion
  51.0 0.0 copy-done
  51.0 2.4 %shard_map.46.refs_0_ = f32[1024,256]{1,0:T(8,128)S(1)} custom-call(bf16[1040,256]{1,0:T(8,128)(2,1)S(1)} %constant_dynamic-slice_fusion.3.x_ref, bf16[16,512,256]{2,1,0:T(8,128)(2,1)S(1)} %copy-done, s32[16,8,256]{2,1,0:T(8,128)S(1)} %pad_convert_fusion.m_ref), custom_call_target="tpu_custom_call" | custom-call | flops 2147483648 | bytes 3678208 | tf_op jit(solution)/shard_map/pallas_call | solution.py:137
  53.3 0.0 collective-permute-done.3
  53.4 0.1 pad_maximum_fusion.1
  53.5 2.4 %shard_map.47 = f32[1024,256]{1,0:T(8,128)S(1)} custom-call(bf16[1040,256]{1,0:T(8,128)(2,1)S(1)} %constant_dynamic-slice_fusion.2.x_ref, bf16[16,512,256]{2,1,0:T(8,128)(2,1)S(1)} %copy-done, s32[16,8,256]{2,1,0:T(8,128)S(1)} %pad_convert_fusion.m_ref, f32[1024,256]{1,0:T(8,128)S(1)} %shard_map.46.refs_0_), custom_call_target="tpu_custom_call", output_to_operand_aliasing={{}: (3, {})} | custom-call | flops 2147483648 | bytes 3678208 | tf_op jit(solution)/shard_map/pallas_call | solution.py:137
  56.0 0.1 select_bitcast_fusion
  56.1 2.4 %collective-permute-start.4 = (f32[32,16,256]{2,1,0:T(8,128)S(1)}, f32[32,16,256]{2,1,0:T(8,128)S(1)}, u32[]{:S(2)}, u32[]{:S(2)}) collective-permute-start(f32[32,16,256]{2,1,0:T(8,128)S(1)} %select_bitcast_fusion), channel_id=1, source_target_pairs={{0,1},{1,0},{2,3},{3,2},{4,5},{5,4},{6,7},{7,6},{8,9},{9,8},{10,11... | collective-permute-start | bytes 1572872 | tf_op jit(solution)/shard_map/ppermute | solution.py:47
  58.5 1.5 %collective-permute-done.4 = f32[32,16,256]{2,1,0:T(8,128)S(1)} collective-permute-done((f32[32,16,256]{2,1,0:T(8,128)S(1)}, f32[32,16,256]{2,1,0:T(8,128)S(1)}, u32[]{:S(2)}, u32[]{:S(2)}) %collective-permute-start.4) | collective-permute-done | bytes 524320 | tf_op jit(solution)/shard_map/ppermute | solution.py:47
  60.0 0.2 fusion.1
  60.2 24.5 %all_to_all.10 = f32[32,16,256]{2,1,0:T(8,128)S(1)} all-to-all(f32[32,16,256]{2,1,0:T(8,128)S(1)} %fusion.1), channel_id=1, replica_groups=mesh['band'=8,'y'=8,'zh'=4,'core'=2] {'y','zh'}, dimensions={0} | all-to-all | bytes 1048576 | tf_op jit(solution)/shard_map/all_to_all | solution.py:89
  84.7 0.6 reduce_sum.9
  (10 shorter events, 0.3 us)
Async XLA Ops:
  1.6 35.6 %all-to-all-start = ((bf16[32,32,256]{2,1,0:T(8,128)(2,1)}), bf16[32,32,256]{2,1,0:T(8,128)(2,1)S(1)}, u32[]{:S(2)}, u32[]{:S(2)}) async-start(bf16[32,32,256]{2,1,0:T(8,128)(2,1)} %broadcast_in_dim.2), calls=%async_computation | async-start | bytes 1048576 | tf_op jit(solution)/shard_map/all_to_all | solution.py:72
  37.3 11.5 %collective-permute-start.2 = (bf16[17,32,128]{2,1,0:T(8,128)(2,1)S(1)}, bf16[17,32,128]{2,1,0:T(8,128)(2,1)S(1)}, u32[]{:S(2)}, u32[]{:S(2)}) collective-permute-start(bf16[17,32,128]{2,1,0:T(8,128)(2,1)S(1)} %get-tuple-element.17), channel_id=1, source_target_pairs={{64,0},{128,64},{192,128},{256,192},{320,256},{384,320},{448,384},... | collective-permute-start | bytes 417800 | tf_op jit(solution)/shard_map/ppermute | solution.py:56
  40.9 7.8 %collective-permute-start.1 = (bf16[17,32,128]{2,1,0:T(8,128)(2,1)S(1)}, bf16[17,32,128]{2,1,0:T(8,128)(2,1)S(1)}, u32[]{:S(2)}, u32[]{:S(2)}) collective-permute-start(bf16[17,32,128]{2,1,0:T(8,128)(2,1)S(1)} %get-tuple-element.18), channel_id=1, source_target_pairs={{0,64},{64,128},{128,192},{192,256},{256,320},{320,384},{384,448},... | collective-permute-start | bytes 417800 | tf_op jit(solution)/shard_map/ppermute | solution.py:55
  43.2 7.6 %collective-permute-start = (bf16[17,32,256]{2,1,0:T(8,128)(2,1)S(1)}, bf16[17,32,256]{2,1,0:T(8,128)(2,1)S(1)}, u32[]{:S(2)}, u32[]{:S(2)}) collective-permute-start(bf16[17,32,256]{2,1,0:T(8,128)(2,1)S(1)} %constant_dynamic-slice_fusion.4), channel_id=1, source_target_pairs={{0,1},{1,0},{2,3},{3,2},{4,5},{5,4},{6,7},{7,6},{8,9},{9,8},{10,11... | collective-permute-start | bytes 835592 | tf_op jit(solution)/shard_map/ppermute | solution.py:47
  45.1 5.8 %copy-start = (bf16[16,512,256]{2,1,0:T(8,128)(2,1)S(1)}, bf16[16,512,256]{2,1,0:T(8,128)(2,1)}, u32[]{:S(2)}) copy-start(bf16[16,512,256]{2,1,0:T(8,128)(2,1)} %w_ref.3) | copy-start | bytes 12582916
  48.8 4.5 %collective-permute-start.3 = (bf16[17,32,256]{2,1,0:T(8,128)(2,1)S(1)}, bf16[17,32,256]{2,1,0:T(8,128)(2,1)S(1)}, u32[]{:S(2)}, u32[]{:S(2)}) collective-permute-start(bf16[17,32,256]{2,1,0:T(8,128)(2,1)S(1)} %constant_dynamic-update-slice_fusion), channel_id=1, source_target_pairs={{0,1},{1,0},{2,3},{3,2},{4,5},{5,4},{6,7},{7,6},{8,9},{9,8},{10,11... | collective-permute-start | bytes 835592 | tf_op jit(solution)/shard_map/ppermute | solution.py:47
  56.1 3.9 %collective-permute-start.4 = (f32[32,16,256]{2,1,0:T(8,128)S(1)}, f32[32,16,256]{2,1,0:T(8,128)S(1)}, u32[]{:S(2)}, u32[]{:S(2)}) collective-permute-start(f32[32,16,256]{2,1,0:T(8,128)S(1)} %select_bitcast_fusion), channel_id=1, source_target_pairs={{0,1},{1,0},{2,3},{3,2},{4,5},{5,4},{6,7},{7,6},{8,9},{9,8},{10,11... | collective-permute-start | bytes 1572872 | tf_op jit(solution)/shard_map/ppermute | solution.py:47

commit v17 on v16

--- a/solution.py
+++ b/solution.py
@@ -79,6 +79,23 @@
     return own, lambda edges, other: assemble(edges, base, first_pair, pair_rows, length, other), edges
 
 
+def sum_kernel(x_ref, o_ref):
+    acc = x_ref[0]
+    for c in range(1, x_ref.shape[0]):
+        acc = acc + x_ref[c]
+    o_ref[...] = acc.astype(o_ref.dtype)
+
+
+def sum_blocks(blocks):
+    vmem = pl.BlockSpec(memory_space=pltpu.VMEM)
+    return pl.pallas_call(
+        sum_kernel,
+        out_shape=jax.ShapeDtypeStruct(blocks.shape[1:], jnp.bfloat16),
+        in_specs=[vmem],
+        out_specs=vmem,
+    )(blocks)
+
+
 def reduce_scatter(partial, n_tm):
     chips = n_tm // 2
     blocks = partial.reshape(chips, 2, partial.shape[0] // n_tm, partial.shape[1])
@@ -86,7 +103,7 @@
     keep = jnp.where(first, blocks[:, 0], blocks[:, 1])
     give = jnp.where(first, blocks[:, 1], blocks[:, 0])
     combined = keep + swap_core(give)
-    return lax.all_to_all(combined, ("y", "zh"), 0, 0, tiled=True).sum(0)
+    return sum_blocks(lax.all_to_all(combined, ("y", "zh"), 0, 0, tiled=True))
 
 
 def tm_index():
@@ -183,8 +200,7 @@
         ((0, half_width, 0, 0), (half_width + ports, 2 * ports, 2, half_width)),
         partial,
     )
-    summed = reduce_scatter(partial, n_tm)
-    return summed.astype(jnp.bfloat16)
+    return reduce_scatter(partial, n_tm)
 
 
 def solution(mesh):

time: 85.9 us -> 87 us (1.013)
  Pallas kernels: 4.81 us -> 6.49 us
    pallas_call x0 -> x1, Pallas kernels: none -> 1.68 us  [sum_blocks(): pl.pallas_call(sum_kernel, out_shape=jax.ShapeDtypeStruct(blocks.shape[1:...]
where the time goes in v17:
time: 87 us; the launch traced here: 86.5 us
  starting transfers between devices  28.3 us (33%)
  blocking collectives  24.6 us (28%)
  waiting for transfers between devices  22.9 us (26%)
  Pallas kernels  6.49 us (7%)
  other arithmetic  2.11 us (2%)
  local copies, waits for them, and re-layouts  1.84 us (2%)
    all_to_all x1, blocking collectives, reduce_scatter(): return sum_blocks(lax.all_to_all(combined, ('y', 'zh'), 0, 0, tiled=True))  24.6 us
    all_to_all x1, waiting for transfers between devices, split_windows(): mine = lax.all_to_all(spread, ('y', 'zh'), 0, 0, tiled=True)  17.8 us
    all_to_all x1, starting transfers between devices, split_windows(): mine = lax.all_to_all(spread, ('y', 'zh'), 0, 0, tiled=True)  16.2 us
    ppermute x3, starting transfers between devices, swap_core(): return lax.ppermute(x, 'core', [(0, 1), (1, 0)])  6.25 us
    pallas_call x2, Pallas kernels, conv_part(): pl.pallas_call(functools.partial(conv_kernel, segments), out_shape=jax.Sh...  4.81 us
    ppermute x1, starting transfers between devices, band_halo(): lax.ppermute(head, 'band', [((i + 1) % count, i) for i in range(ends)])  3.61 us
    ppermute x1, waiting for transfers between devices, band_halo(): lax.ppermute(tail, 'band', [(i, (i + 1) % count) for i in range(ends)])  3.58 us
    ppermute x1, starting transfers between devices, band_halo(): lax.ppermute(tail, 'band', [(i, (i + 1) % count) for i in range(ends)])  2.24 us
  transfers between devices with their start and end apart: 6, of which 3 were waited for; matrix products, arithmetic and copies ran while one was open for 2% of the time, Pallas kernels for 3%

profile of v17, /device:TPU:14, one launch (start us, length us, event | category | flops | bytes accessed | tf_op | source)
XLA Modules:
  0.0 86.5 jit_solution(18355403956419810203)
XLA Ops:
  0.0 1.6 %broadcast_in_dim.2 = bf16[32,32,256]{2,1,0:T(8,128)(2,1)} broadcast(bf16[32,256]{1,0:T(8,128)(2,1)} %param.4), dimensions={1,2} | broadcast | bytes 540672 | tf_op jit(solution)/shard_map/broadcast_in_dim | solution.py:71
  1.6 16.2 %all-to-all-start = ((bf16[32,32,256]{2,1,0:T(8,128)(2,1)}), bf16[32,32,256]{2,1,0:T(8,128)(2,1)S(1)}, u32[]{:S(2)}, u32[]{:S(2)}) async-start(bf16[32,32,256]{2,1,0:T(8,128)(2,1)} %broadcast_in_dim.2), calls=%async_computation | async-start | bytes 1048576 | tf_op jit(solution)/shard_map/all_to_all | solution.py:72
  17.8 0.8 compare_reduce_fusion.1
  18.6 0.8 broadcast_and_fusion.1
  19.4 0.1 pad_add_fusion
  19.4 17.8 %all-to-all-done = bf16[32,32,256]{2,1,0:T(8,128)(2,1)S(1)} async-done(((bf16[32,32,256]{2,1,0:T(8,128)(2,1)}), bf16[32,32,256]{2,1,0:T(8,128)(2,1)S(1)}, u32[]{:S(2)}, u32[]{:S(2)}) %all-to-all-start) | async-done | bytes 524320 | tf_op jit(solution)/shard_map/all_to_all | solution.py:72
  37.2 0.1 constant_dynamic-slice_fusion
  37.2 3.6 %collective-permute-start.2 = (bf16[17,32,128]{2,1,0:T(8,128)(2,1)S(1)}, bf16[17,32,128]{2,1,0:T(8,128)(2,1)S(1)}, u32[]{:S(2)}, u32[]{:S(2)}) collective-permute-start(bf16[17,32,128]{2,1,0:T(8,128)(2,1)S(1)} %get-tuple-element.17), channel_id=1, source_target_pairs={{64,0},{128,64},{192,128},{256,192},{320,256},{384,320},{448,384},... | collective-permute-start | bytes 417800 | tf_op jit(solution)/shard_map/ppermute | solution.py:56
  40.9 2.2 %collective-permute-start.1 = (bf16[17,32,128]{2,1,0:T(8,128)(2,1)S(1)}, bf16[17,32,128]{2,1,0:T(8,128)(2,1)S(1)}, u32[]{:S(2)}, u32[]{:S(2)}) collective-permute-start(bf16[17,32,128]{2,1,0:T(8,128)(2,1)S(1)} %get-tuple-element.18), channel_id=1, source_target_pairs={{0,64},{64,128},{128,192},{192,256},{256,320},{320,384},{384,448},... | collective-permute-start | bytes 417800 | tf_op jit(solution)/shard_map/ppermute | solution.py:55
  43.1 1.9 %collective-permute-start = (bf16[17,32,256]{2,1,0:T(8,128)(2,1)S(1)}, bf16[17,32,256]{2,1,0:T(8,128)(2,1)S(1)}, u32[]{:S(2)}, u32[]{:S(2)}) collective-permute-start(bf16[17,32,256]{2,1,0:T(8,128)(2,1)S(1)} %constant_dynamic-slice_fusion.4), channel_id=1, source_target_pairs={{0,1},{1,0},{2,3},{3,2},{4,5},{5,4},{6,7},{7,6},{8,9},{9,8},{10,11... | collective-permute-start | bytes 835592 | tf_op jit(solution)/shard_map/ppermute | solution.py:47
  45.1 0.0 copy-start
  45.1 3.6 %collective-permute-done.1 = bf16[17,32,128]{2,1,0:T(8,128)(2,1)S(1)} collective-permute-done((bf16[17,32,128]{2,1,0:T(8,128)(2,1)S(1)}, bf16[17,32,128]{2,1,0:T(8,128)(2,1)S(1)}, u32[]{:S(2)}, u32[]{:S(2)}) %collective-permute-start.1) | collective-permute-done | bytes 139296 | tf_op jit(solution)/shard_map/ppermute | solution.py:55
  48.7 0.0 collective-permute-done.2
  48.8 1.9 %collective-permute-start.3 = (bf16[17,32,256]{2,1,0:T(8,128)(2,1)S(1)}, bf16[17,32,256]{2,1,0:T(8,128)(2,1)S(1)}, u32[]{:S(2)}, u32[]{:S(2)}) collective-permute-start(bf16[17,32,256]{2,1,0:T(8,128)(2,1)S(1)} %constant_dynamic-update-slice_fusion), channel_id=1, source_target_pairs={{0,1},{1,0},{2,3},{3,2},{4,5},{5,4},{6,7},{7,6},{8,9},{9,8},{10,11... | collective-permute-start | bytes 835592 | tf_op jit(solution)/shard_map/ppermute | solution.py:47
  50.7 0.0 collective-permute-done
  50.8 0.1 pad_maximum_fusion
  51.0 0.0 copy-done
  51.0 2.4 %shard_map.46.refs_0_ = f32[1024,256]{1,0:T(8,128)S(1)} custom-call(bf16[1040,256]{1,0:T(8,128)(2,1)S(1)} %constant_dynamic-slice_fusion.3.x_ref, bf16[16,512,256]{2,1,0:T(8,128)(2,1)S(1)} %copy-done, s32[16,8,256]{2,1,0:T(8,128)S(1)} %pad_convert_fusion.m_ref), custom_call_target="tpu_custom_call" | custom-call | flops 2147483648 | bytes 3678208 | tf_op jit(solution)/shard_map/pallas_call | solution.py:154
  53.3 0.0 collective-permute-done.3
  53.4 0.1 pad_maximum_fusion.1
  53.5 2.4 %shard_map.47 = f32[1024,256]{1,0:T(8,128)S(1)} custom-call(bf16[1040,256]{1,0:T(8,128)(2,1)S(1)} %constant_dynamic-slice_fusion.2.x_ref, bf16[16,512,256]{2,1,0:T(8,128)(2,1)S(1)} %copy-done, s32[16,8,256]{2,1,0:T(8,128)S(1)} %pad_convert_fusion.m_ref, f32[1024,256]{1,0:T(8,128)S(1)} %shard_map.46.refs_0_), custom_call_target="tpu_custom_call", output_to_operand_aliasing={{}: (3, {})} | custom-call | flops 2147483648 | bytes 3678208 | tf_op jit(solution)/shard_map/pallas_call | solution.py:154
  56.0 0.1 select_bitcast_fusion
  56.1 2.4 %collective-permute-start.4 = (f32[32,16,256]{2,1,0:T(8,128)S(1)}, f32[32,16,256]{2,1,0:T(8,128)S(1)}, u32[]{:S(2)}, u32[]{:S(2)}) collective-permute-start(f32[32,16,256]{2,1,0:T(8,128)S(1)} %select_bitcast_fusion), channel_id=1, source_target_pairs={{0,1},{1,0},{2,3},{3,2},{4,5},{5,4},{6,7},{7,6},{8,9},{9,8},{10,11... | collective-permute-start | bytes 1572872 | tf_op jit(solution)/shard_map/ppermute | solution.py:47
  58.5 1.5 %collective-permute-done.4 = f32[32,16,256]{2,1,0:T(8,128)S(1)} collective-permute-done((f32[32,16,256]{2,1,0:T(8,128)S(1)}, f32[32,16,256]{2,1,0:T(8,128)S(1)}, u32[]{:S(2)}, u32[]{:S(2)}) %collective-permute-start.4) | collective-permute-done | bytes 524320 | tf_op jit(solution)/shard_map/ppermute | solution.py:47
  60.0 0.2 bitcast_add_fusion
  60.2 24.6 %all_to_all.10.x_ref = f32[32,16,256]{2,1,0:T(8,128)} all-to-all(f32[32,16,256]{2,1,0:T(8,128)S(1)} %bitcast_add_fusion), channel_id=1, replica_groups=mesh['band'=8,'y'=8,'zh'=4,'core'=2] {'y','zh'}, dimensions={0} | all-to-all | bytes 1048576 | tf_op jit(solution)/shard_map/all_to_all | solution.py:106
  84.8 1.7 %shard_map.48 = bf16[16,256]{1,0:T(8,128)(2,1)} custom-call(f32[32,16,256]{2,1,0:T(8,128)} %all_to_all.10.x_ref), custom_call_target="tpu_custom_call" | custom-call | tf_op jit(solution)/shard_map/pallas_call | solution.py:91
  (10 shorter events, 0.3 us)
Async XLA Ops:
  1.6 35.6 %all-to-all-start = ((bf16[32,32,256]{2,1,0:T(8,128)(2,1)}), bf16[32,32,256]{2,1,0:T(8,128)(2,1)S(1)}, u32[]{:S(2)}, u32[]{:S(2)}) async-start(bf16[32,32,256]{2,1,0:T(8,128)(2,1)} %broadcast_in_dim.2), calls=%async_computation | async-start | bytes 1048576 | tf_op jit(solution)/shard_map/all_to_all | solution.py:72
  37.2 11.5 %collective-permute-start.2 = (bf16[17,32,128]{2,1,0:T(8,128)(2,1)S(1)}, bf16[17,32,128]{2,1,0:T(8,128)(2,1)S(1)}, u32[]{:S(2)}, u32[]{:S(2)}) collective-permute-start(bf16[17,32,128]{2,1,0:T(8,128)(2,1)S(1)} %get-tuple-element.17), channel_id=1, source_target_pairs={{64,0},{128,64},{192,128},{256,192},{320,256},{384,320},{448,384},... | collective-permute-start | bytes 417800 | tf_op jit(solution)/shard_map/ppermute | solution.py:56
  40.9 7.8 %collective-permute-start.1 = (bf16[17,32,128]{2,1,0:T(8,128)(2,1)S(1)}, bf16[17,32,128]{2,1,0:T(8,128)(2,1)S(1)}, u32[]{:S(2)}, u32[]{:S(2)}) collective-permute-start(bf16[17,32,128]{2,1,0:T(8,128)(2,1)S(1)} %get-tuple-element.18), channel_id=1, source_target_pairs={{0,64},{64,128},{128,192},{192,256},{256,320},{320,384},{384,448},... | collective-permute-start | bytes 417800 | tf_op jit(solution)/shard_map/ppermute | solution.py:55
  43.1 7.6 %collective-permute-start = (bf16[17,32,256]{2,1,0:T(8,128)(2,1)S(1)}, bf16[17,32,256]{2,1,0:T(8,128)(2,1)S(1)}, u32[]{:S(2)}, u32[]{:S(2)}) collective-permute-start(bf16[17,32,256]{2,1,0:T(8,128)(2,1)S(1)} %constant_dynamic-slice_fusion.4), channel_id=1, source_target_pairs={{0,1},{1,0},{2,3},{3,2},{4,5},{5,4},{6,7},{7,6},{8,9},{9,8},{10,11... | collective-permute-start | bytes 835592 | tf_op jit(solution)/shard_map/ppermute | solution.py:47
  45.1 5.8 %copy-start = (bf16[16,512,256]{2,1,0:T(8,128)(2,1)S(1)}, bf16[16,512,256]{2,1,0:T(8,128)(2,1)}, u32[]{:S(2)}) copy-start(bf16[16,512,256]{2,1,0:T(8,128)(2,1)} %w_ref.3) | copy-start | bytes 12582916
  48.8 4.5 %collective-permute-start.3 = (bf16[17,32,256]{2,1,0:T(8,128)(2,1)S(1)}, bf16[17,32,256]{2,1,0:T(8,128)(2,1)S(1)}, u32[]{:S(2)}, u32[]{:S(2)}) collective-permute-start(bf16[17,32,256]{2,1,0:T(8,128)(2,1)S(1)} %constant_dynamic-update-slice_fusion), channel_id=1, source_target_pairs={{0,1},{1,0},{2,3},{3,2},{4,5},{5,4},{6,7},{7,6},{8,9},{9,8},{10,11... | collective-permute-start | bytes 835592 | tf_op jit(solution)/shard_map/ppermute | solution.py:47
  56.1 3.9 %collective-permute-start.4 = (f32[32,16,256]{2,1,0:T(8,128)S(1)}, f32[32,16,256]{2,1,0:T(8,128)S(1)}, u32[]{:S(2)}, u32[]{:S(2)}) collective-permute-start(f32[32,16,256]{2,1,0:T(8,128)S(1)} %select_bitcast_fusion), channel_id=1, source_target_pairs={{0,1},{1,0},{2,3},{3,2},{4,5},{5,4},{6,7},{7,6},{8,9},{9,8},{10,11... | collective-permute-start | bytes 1572872 | tf_op jit(solution)/shard_map/ppermute | solution.py:47

commit v18 on v16

--- a/solution.py
+++ b/solution.py
@@ -74,8 +74,9 @@
     span = (length + 2 * pair_rows - align - 1) // pair_rows
     first_pair = jnp.minimum(base // pair_rows, chips - span)
     needed = lax.dynamic_slice_in_dim(mine, first_pair, span, 0)
+    needed, other = lax.optimization_barrier((needed, swap_core(needed)))
     edges = band_halo(needed, width)
-    own = assemble(needed, base, first_pair, pair_rows, length)
+    own = assemble(needed, base, first_pair, pair_rows, length, other)
     return own, lambda edges, other: assemble(edges, base, first_pair, pair_rows, length, other), edges
 
 

time: 85.9 us -> 89.8 us (1.045)
  waiting for transfers between devices: 22.9 us -> 26.7 us
    ppermute x1, waiting for transfers between devices: 3.58 us -> 5.95 us  [band_halo(): lax.ppermute(tail, 'band', [(i, (i + 1) % count) for i in range(ends)])]
  transfers between devices with their start and end apart: 6 -> 6, of which waited for: 3 -> 4; matrix products, arithmetic and copies ran while one was open for 2% -> 2% of each run, Pallas kernels for 3% -> 3%
where the time goes in v18:
time: 89.8 us; the launch traced here: 89.3 us
  starting transfers between devices  28.4 us (32%)
  waiting for transfers between devices  26.7 us (30%)
  blocking collectives  24.5 us (27%)
  Pallas kernels  4.81 us (5%)
  other arithmetic  2.77 us (3%)
  local copies, waits for them, and re-layouts  1.84 us (2%)
    all_to_all x1, blocking collectives, reduce_scatter(): return lax.all_to_all(combined, ('y', 'zh'), 0, 0, tiled=True).sum(0)  24.5 us
    all_to_all x1, waiting for transfers between devices, split_windows(): mine = lax.all_to_all(spread, ('y', 'zh'), 0, 0, tiled=True)  18.6 us
    all_to_all x1, starting transfers between devices, split_windows(): mine = lax.all_to_all(spread, ('y', 'zh'), 0, 0, tiled=True)  16.2 us
    ppermute x3, starting transfers between devices, swap_core(): return lax.ppermute(x, 'core', [(0, 1), (1, 0)])  6.26 us
    ppermute x1, waiting for transfers between devices, band_halo(): lax.ppermute(tail, 'band', [(i, (i + 1) % count) for i in range(ends)])  5.95 us
    pallas_call x2, Pallas kernels, conv_part(): pl.pallas_call(functools.partial(conv_kernel, segments), out_shape=jax.Sh...  4.81 us
    ppermute x1, starting transfers between devices, band_halo(): lax.ppermute(head, 'band', [((i + 1) % count, i) for i in range(ends)])  3.74 us
    ppermute x1, starting transfers between devices, band_halo(): lax.ppermute(tail, 'band', [(i, (i + 1) % count) for i in range(ends)])  2.24 us
  transfers between devices with their start and end apart: 6, of which 4 were waited for; matrix products, arithmetic and copies ran while one was open for 2% of the time, Pallas kernels for 3%

profile of v18, /device:TPU:14, one launch (start us, length us, event | category | flops | bytes accessed | tf_op | source)
XLA Modules:
  0.0 89.3 jit_solution(2282465651655393410)
XLA Ops:
  0.0 1.6 %broadcast_in_dim.2 = bf16[32,32,256]{2,1,0:T(8,128)(2,1)} broadcast(bf16[32,256]{1,0:T(8,128)(2,1)} %param.4), dimensions={1,2} | broadcast | bytes 540672 | tf_op jit(solution)/shard_map/broadcast_in_dim | solution.py:71
  1.6 16.2 %all-to-all-start = ((bf16[32,32,256]{2,1,0:T(8,128)(2,1)}), bf16[32,32,256]{2,1,0:T(8,128)(2,1)S(1)}, u32[]{:S(2)}, u32[]{:S(2)}) async-start(bf16[32,32,256]{2,1,0:T(8,128)(2,1)} %broadcast_in_dim.2), calls=%async_computation | async-start | bytes 1048576 | tf_op jit(solution)/shard_map/all_to_all | solution.py:72
  17.8 0.8 compare_reduce_fusion.1
  18.6 18.6 %all-to-all-done = bf16[32,32,256]{2,1,0:T(8,128)(2,1)S(1)} async-done(((bf16[32,32,256]{2,1,0:T(8,128)(2,1)}), bf16[32,32,256]{2,1,0:T(8,128)(2,1)S(1)}, u32[]{:S(2)}, u32[]{:S(2)}) %all-to-all-start) | async-done | bytes 524320 | tf_op jit(solution)/shard_map/all_to_all | solution.py:72
  37.2 1.9 %collective-permute-start = (bf16[17,32,256]{2,1,0:T(8,128)(2,1)S(1)}, bf16[17,32,256]{2,1,0:T(8,128)(2,1)S(1)}, u32[]{:S(2)}, u32[]{:S(2)}) collective-permute-start(bf16[17,32,256]{2,1,0:T(8,128)(2,1)S(1)} %constant_dynamic-slice_fusion.2), channel_id=1, source_target_pairs={{0,1},{1,0},{2,3},{3,2},{4,5},{5,4},{6,7},{7,6},{8,9},{9,8},{10,11... | collective-permute-start | bytes 835592 | tf_op jit(solution)/shard_map/ppermute | solution.py:47
  39.1 0.8 broadcast_and_fusion.1
  40.0 0.0 copy-start
  40.0 0.1 pad_add_fusion
  40.1 0.6 collective-permute-done
  40.7 3.7 %collective-permute-start.2 = (bf16[17,32,128]{2,1,0:T(8,128)(2,1)S(1)}, bf16[17,32,128]{2,1,0:T(8,128)(2,1)S(1)}, u32[]{:S(2)}, u32[]{:S(2)}) collective-permute-start(bf16[17,32,128]{2,1,0:T(8,128)(2,1)S(1)} %get-tuple-element.21), channel_id=1, source_target_pairs={{64,0},{128,64},{192,128},{256,192},{320,256},{384,320},{448,384},... | collective-permute-start | bytes 417800 | tf_op jit(solution)/shard_map/ppermute | solution.py:56
  44.5 2.2 %collective-permute-start.1 = (bf16[17,32,128]{2,1,0:T(8,128)(2,1)S(1)}, bf16[17,32,128]{2,1,0:T(8,128)(2,1)S(1)}, u32[]{:S(2)}, u32[]{:S(2)}) collective-permute-start(bf16[17,32,128]{2,1,0:T(8,128)(2,1)S(1)} %get-tuple-element.22), channel_id=1, source_target_pairs={{0,64},{64,128},{128,192},{192,256},{256,320},{320,384},{384,448},... | collective-permute-start | bytes 417800 | tf_op jit(solution)/shard_map/ppermute | solution.py:55
  46.8 0.1 pad_maximum_fusion
  46.9 6.0 %collective-permute-done.1 = bf16[17,32,128]{2,1,0:T(8,128)(2,1)S(1)} collective-permute-done((bf16[17,32,128]{2,1,0:T(8,128)(2,1)S(1)}, bf16[17,32,128]{2,1,0:T(8,128)(2,1)S(1)}, u32[]{:S(2)}, u32[]{:S(2)}) %collective-permute-start.1) | collective-permute-done | bytes 139296 | tf_op jit(solution)/shard_map/ppermute | solution.py:55
  52.9 0.0 collective-permute-done.2
  52.9 1.9 %collective-permute-start.3 = (bf16[17,32,256]{2,1,0:T(8,128)(2,1)S(1)}, bf16[17,32,256]{2,1,0:T(8,128)(2,1)S(1)}, u32[]{:S(2)}, u32[]{:S(2)}) collective-permute-start(bf16[17,32,256]{2,1,0:T(8,128)(2,1)S(1)} %constant_dynamic-update-slice_fusion), channel_id=1, source_target_pairs={{0,1},{1,0},{2,3},{3,2},{4,5},{5,4},{6,7},{7,6},{8,9},{9,8},{10,11... | collective-permute-start | bytes 835592 | tf_op jit(solution)/shard_map/ppermute | solution.py:47
  54.9 0.0 copy-done
  54.9 2.4 %shard_map.46.refs_0_ = f32[1024,256]{1,0:T(8,128)S(1)} custom-call(bf16[1040,256]{1,0:T(8,128)(2,1)S(1)} %constant_dynamic-slice_fusion.1.x_ref, bf16[16,512,256]{2,1,0:T(8,128)(2,1)S(1)} %copy-done, s32[16,8,256]{2,1,0:T(8,128)S(1)} %pad_convert_fusion.m_ref), custom_call_target="tpu_custom_call" | custom-call | flops 2147483648 | bytes 3678208 | tf_op jit(solution)/shard_map/pallas_call | solution.py:138
  57.3 0.0 collective-permute-done.3
  57.3 0.1 pad_maximum_fusion.1
  57.5 2.4 %shard_map.47 = f32[1024,256]{1,0:T(8,128)S(1)} custom-call(bf16[1040,256]{1,0:T(8,128)(2,1)S(1)} %constant_dynamic-slice_fusion.x_ref, bf16[16,512,256]{2,1,0:T(8,128)(2,1)S(1)} %copy-done, s32[16,8,256]{2,1,0:T(8,128)S(1)} %pad_convert_fusion.m_ref, f32[1024,256]{1,0:T(8,128)S(1)} %shard_map.46.refs_0_), custom_call_target="tpu_custom_call", output_to_operand_aliasing={{}: (3, {})} | custom-call | flops 2147483648 | bytes 3678208 | tf_op jit(solution)/shard_map/pallas_call | solution.py:138
  59.9 0.1 select_bitcast_fusion
  60.0 2.4 %collective-permute-start.4 = (f32[32,16,256]{2,1,0:T(8,128)S(1)}, f32[32,16,256]{2,1,0:T(8,128)S(1)}, u32[]{:S(2)}, u32[]{:S(2)}) collective-permute-start(f32[32,16,256]{2,1,0:T(8,128)S(1)} %select_bitcast_fusion), channel_id=1, source_target_pairs={{0,1},{1,0},{2,3},{3,2},{4,5},{5,4},{6,7},{7,6},{8,9},{9,8},{10,11... | collective-permute-start | bytes 1572872 | tf_op jit(solution)/shard_map/ppermute | solution.py:47
  62.4 1.5 %collective-permute-done.4 = f32[32,16,256]{2,1,0:T(8,128)S(1)} collective-permute-done((f32[32,16,256]{2,1,0:T(8,128)S(1)}, f32[32,16,256]{2,1,0:T(8,128)S(1)}, u32[]{:S(2)}, u32[]{:S(2)}) %collective-permute-start.4) | collective-permute-done | bytes 524320 | tf_op jit(solution)/shard_map/ppermute | solution.py:47
  64.0 0.2 fusion.1
  64.1 24.5 %all_to_all.10 = f32[32,16,256]{2,1,0:T(8,128)S(1)} all-to-all(f32[32,16,256]{2,1,0:T(8,128)S(1)} %fusion.1), channel_id=1, replica_groups=mesh['band'=8,'y'=8,'zh'=4,'core'=2] {'y','zh'}, dimensions={0} | all-to-all | bytes 1048576 | tf_op jit(solution)/shard_map/all_to_all | solution.py:90
  88.7 0.6 reduce_sum.9
  (11 shorter events, 0.4 us)
Async XLA Ops:
  1.6 35.6 %all-to-all-start = ((bf16[32,32,256]{2,1,0:T(8,128)(2,1)}), bf16[32,32,256]{2,1,0:T(8,128)(2,1)S(1)}, u32[]{:S(2)}, u32[]{:S(2)}) async-start(bf16[32,32,256]{2,1,0:T(8,128)(2,1)} %broadcast_in_dim.2), calls=%async_computation | async-start | bytes 1048576 | tf_op jit(solution)/shard_map/all_to_all | solution.py:72
  37.2 3.5 %collective-permute-start = (bf16[17,32,256]{2,1,0:T(8,128)(2,1)S(1)}, bf16[17,32,256]{2,1,0:T(8,128)(2,1)S(1)}, u32[]{:S(2)}, u32[]{:S(2)}) collective-permute-start(bf16[17,32,256]{2,1,0:T(8,128)(2,1)S(1)} %constant_dynamic-slice_fusion.2), channel_id=1, source_target_pairs={{0,1},{1,0},{2,3},{3,2},{4,5},{5,4},{6,7},{7,6},{8,9},{9,8},{10,11... | collective-permute-start | bytes 835592 | tf_op jit(solution)/shard_map/ppermute | solution.py:47
  40.0 14.9 %copy-start = (bf16[16,512,256]{2,1,0:T(8,128)(2,1)S(1)}, bf16[16,512,256]{2,1,0:T(8,128)(2,1)}, u32[]{:S(2)}) copy-start(bf16[16,512,256]{2,1,0:T(8,128)(2,1)} %w_ref.3) | copy-start | bytes 12582916
  40.7 12.1 %collective-permute-start.2 = (bf16[17,32,128]{2,1,0:T(8,128)(2,1)S(1)}, bf16[17,32,128]{2,1,0:T(8,128)(2,1)S(1)}, u32[]{:S(2)}, u32[]{:S(2)}) collective-permute-start(bf16[17,32,128]{2,1,0:T(8,128)(2,1)S(1)} %get-tuple-element.21), channel_id=1, source_target_pairs={{64,0},{128,64},{192,128},{256,192},{320,256},{384,320},{448,384},... | collective-permute-start | bytes 417800 | tf_op jit(solution)/shard_map/ppermute | solution.py:56
  44.5 8.4 %collective-permute-start.1 = (bf16[17,32,128]{2,1,0:T(8,128)(2,1)S(1)}, bf16[17,32,128]{2,1,0:T(8,128)(2,1)S(1)}, u32[]{:S(2)}, u32[]{:S(2)}) collective-permute-start(bf16[17,32,128]{2,1,0:T(8,128)(2,1)S(1)} %get-tuple-element.22), channel_id=1, source_target_pairs={{0,64},{64,128},{128,192},{192,256},{256,320},{320,384},{384,448},... | collective-permute-start | bytes 417800 | tf_op jit(solution)/shard_map/ppermute | solution.py:55
  52.9 4.4 %collective-permute-start.3 = (bf16[17,32,256]{2,1,0:T(8,128)(2,1)S(1)}, bf16[17,32,256]{2,1,0:T(8,128)(2,1)S(1)}, u32[]{:S(2)}, u32[]{:S(2)}) collective-permute-start(bf16[17,32,256]{2,1,0:T(8,128)(2,1)S(1)} %constant_dynamic-update-slice_fusion), channel_id=1, source_target_pairs={{0,1},{1,0},{2,3},{3,2},{4,5},{5,4},{6,7},{7,6},{8,9},{9,8},{10,11... | collective-permute-start | bytes 835592 | tf_op jit(solution)/shard_map/ppermute | solution.py:47
  60.0 3.9 %collective-permute-start.4 = (f32[32,16,256]{2,1,0:T(8,128)S(1)}, f32[32,16,256]{2,1,0:T(8,128)S(1)}, u32[]{:S(2)}, u32[]{:S(2)}) collective-permute-start(f32[32,16,256]{2,1,0:T(8,128)S(1)} %select_bitcast_fusion), channel_id=1, source_target_pairs={{0,1},{1,0},{2,3},{3,2},{4,5},{5,4},{6,7},{7,6},{8,9},{9,8},{10,11... | collective-permute-start | bytes 1572872 | tf_op jit(solution)/shard_map/ppermute | solution.py:47
